TPU v7x, 32 devices: a whole 2x2x4 slice. The times are simulated.
32 devices in a mesh: day: 2 (over y), stu: 16 (over z, x, core).
Axes of the slice: x: 2, y: 2, z: 4, core: 2. Of those that a mesh axis runs over, the one named last changes fastest.
Arguments:
- performance: bfloat16 [64, 128, 1024], P('day', 'stu'), may hold values from -8 to 8
- student_factor: bfloat16 [128, 256], P('stu'), may hold values from -0.5 to 0.5
- skill_factor: bfloat16 [1024, 256], replicated, may hold values from -0.1875 to 0.1875
- day_prev: float32 [64, 256], P('day'), may hold values from -6 to 6
- ar_coef: float32 [7], replicated, may hold values from -0.3 to 0.3
Outputs:
- day_factor: float32 [64, 256], P('day', 'stu')
- residual: float32 [64, 256], P('day', 'stu')
All inputs are finite; a program needn't handle non-finite values.
Results may differ from a plain program's by a relative error of at most 0.0003.
Values sent between devices are 32-bit elements; how exact they have to be, the bound alone decides.
No kernel may reach another device: no remote copies, remote signals or barrier semaphores. Data moves between devices by JAX's collectives and lax.ppermute only.
A program may use at most 64 MiB of HBM per device.

v0:
```python
import jax
import jax.numpy as jnp
from jax import lax
from jax.sharding import PartitionSpec as P

LAGS = 7
ITERS = 3


smoothing = 1.0


def shifted(block, axis, distance):
    devices = range(lax.axis_size(axis))
    route = [(i - distance, i) for i in devices if i - distance in devices]
    return lax.ppermute(block, axis, route)


def filter_rows(extended, coef, count):
    out = extended[LAGS : LAGS + count]
    for lag in range(1, LAGS + 1):
        out = out - coef[lag - 1] * extended[LAGS - lag : LAGS - lag + count]
    return out


def smooth(values, coef):
    count = values.shape[0]
    below = shifted(values[count - LAGS :], "day", 1)
    ahead_core = filter_rows(jnp.concatenate([below, values], 0), coef, count)
    above = shifted(ahead_core[:LAGS], "day", -1)
    ahead = jnp.concatenate([ahead_core, above], 0)
    out = ahead[:count]
    for lag in range(1, LAGS + 1):
        out = out - coef[lag - 1] * ahead[lag : lag + count]
    return out


def with_gram(values, gram_part):
    return jnp.dot(
        lax.all_gather(values, "stu", axis=1, tiled=True),
        gram_part,
        precision=lax.Precision.HIGHEST,
        preferred_element_type=jnp.float32,
    )


def operate(values, gram_part, coef):
    return with_gram(values, gram_part) + smoothing * smooth(values, coef)


def global_total(value):
    return lax.psum(value, ("day", "stu"))


def summed_gram(local_gram):
    return lax.psum(local_gram, "stu")


def local(performance, student_factor, skill_factor, day_prev, ar_coef):
    days, students, skills = performance.shape
    rank = skill_factor.shape[1]
    proj = jnp.dot(
        performance.reshape(days * students, skills),
        skill_factor,
        preferred_element_type=jnp.float32,
    )
    proj = proj.reshape(days, students, rank)
    local_terms = jnp.sum(proj * student_factor.astype(jnp.float32)[None], axis=1)
    local_gram = jnp.dot(student_factor.T, student_factor, preferred_element_type=jnp.float32)
    skill_gram = jnp.dot(skill_factor.T, skill_factor, preferred_element_type=jnp.float32)
    columns = rank // lax.axis_size("stu")
    first_col = lax.axis_index("stu") * columns
    gram = summed_gram(local_gram) * skill_gram
    mttkrp = lax.psum_scatter(local_terms, "stu", scatter_dimension=1, tiled=True)
    gram_part = lax.dynamic_slice_in_dim(gram, first_col, columns, 1)
    day_factor = lax.dynamic_slice_in_dim(day_prev, first_col, columns, 1)
    residual = mttkrp - operate(day_factor, gram_part, ar_coef)
    direction = residual
    norm_now = global_total(jnp.sum(residual * residual))
    for step in range(ITERS):
        image = operate(direction, gram_part, ar_coef)
        alpha = norm_now / global_total(jnp.sum(direction * image))
        day_factor = day_factor + alpha * direction
        residual = residual - alpha * image
        norm_next = global_total(jnp.sum(residual * residual))
        direction = residual + norm_next / norm_now * direction
        norm_now = norm_next
    return (day_factor, residual)


def solution(mesh):
    return jax.shard_map(
        local,
        mesh=mesh,
        in_specs=(P("day", "stu", None), P("stu", None), P(), P("day", None), P()),
        out_specs=(P("day", "stu"), P("day", "stu")),
        check_vma=False,
    )
```

profile of v0, /device:TPU:0, one launch (start us, length us, event | category | flops | bytes accessed | tf_op | source)
XLA Modules:
  0.0 490.8 jit_solution(908321572501885240)
XLA Ops:
  7.2 0.9 constant_dynamic-slice_fusion
  8.3 4.9 collective-permute-start
  13.1 1.7 fusion.139
  17.9 22.0 %all_gather.12 = f32[32,256]{0,1:T(8,128)S(1)} all-gather(f32[32,16]{0,1:T(8,128)S(1)} %copy.10), channel_id=1, replica_groups=mesh['day'=2,'stu'=16] {'stu'}, dimensions={1}, use_global_device_ids=true | all-gather | bytes 34816 | tf_op jit(solution)/shard_map/all_gather | solution.py:40
  39.9 4.5 fusion.120
  44.4 1.3 collective-permute-start.1
  45.7 58.5 %all-reduce.3.cloned.1.call-done = f32[256,256]{0,1:T(8,128)} async-done(((f32[256,256]{0,1:T(8,128)}), f32[256,256]{0,1:T(8,128)}) %all-reduce.3.cloned.1.call-update) | async-done | bytes 262160 | tf_op jit(solution)/shard_map/psum | solution.py:56
  104.9 58.3 %reduce-scatter.2.cloned.1.call-done = f32[32,16]{0,1:T(8,128)} async-done(((f32[32,256]{0,1:T(8,128)}), f32[32,16]{0,1:T(8,128)}) %reduce-scatter.2.cloned.1.call-update) | async-done | bytes 2064 | tf_op jit(solution)/shard_map/reduce_scatter | solution.py:74
  163.2 5.2 %fusion.104 = f32[32,16]{0,1:T(8,128)S(1)} fusion(f32[32,16]{0,1:T(8,128)} %reduce-scatter.2.cloned.1.call-done, f32[7,16]{0,1:T(8,128)S(1)} %collective-permute-done.1, f32[32,16]{0,1:T(8,128)S(1)} %fusion.120, f32[]{:T(128)} %bitcast.7, f32[]{:T(128)} %bitcast.6, f32[]{:T(128)} %bitcast.5, f32[]{:T(128)} %bitcast.4, f32[]{:T(128)} %bitcast.3, ...), kind=kOutput, calls=%fused_computation.173 | convolution fusion | flops 1584640 | bytes 55772 | tf_op jit(solution)/shard_map/dot_general | solution.py:39
  168.5 3.4 collective-permute-start.2
  171.9 1.3 collective-permute-done.2
  173.2 4.5 fusion.86
  177.7 1.3 collective-permute-start.3
  179.0 19.8 %all_gather.13 = f32[32,256]{0,1:T(8,128)S(1)} all-gather(f32[32,16]{0,1:T(8,128)S(1)} %fusion.104), channel_id=1, replica_groups=mesh['day'=2,'stu'=16] {'stu'}, dimensions={1}, use_global_device_ids=true | all-gather | bytes 34816 | tf_op jit(solution)/shard_map/all_gather | solution.py:40
  198.8 5.2 %multiply_reduce_fusion.4 = (f32[]{:T(128)}, f32[]{:T(128)}, f32[32,16]{0,1:T(8,128)S(1)}) fusion(f32[32,16]{0,1:T(8,128)S(1)} %fusion.104, f32[7,16]{0,1:T(8,128)S(1)} %collective-permute-done.3, f32[32,16]{0,1:T(8,128)S(1)} %fusion.86, f32[]{:T(128)} %bitcast.7, f32[]{:T(128)} %bitcast.6, f32[]{:T(128)} %bitcast.5, f32[]{:T(128)} %bitcast.4, ...), kind=kOutput, calls=%fused_computation.235 | convolution fusion | flops 1586174 | bytes 55780 | tf_op jit(solution)/shard_map/dot_general | solution.py:39
  204.0 38.1 %all-reduce = (f32[]{:T(128)}, f32[]{:T(128)}) all-reduce(f32[]{:T(128)} %get-tuple-element.3, f32[]{:T(128)} %get-tuple-element.2), channel_id=1, replica_groups=mesh['day'=2,'stu'=16] {'day','stu'}, use_global_device_ids=true, to_apply=%region_4.0 | all-reduce | flops 2 | bytes 16 | tf_op jit(solution)/shard_map/psum | solution.py:52
  244.1 42.9 %psum.52 = f32[]{:T(128)} all-reduce(f32[]{:T(128)} %multiply_reduce_fusion.3), channel_id=1, replica_groups=mesh['day'=2,'stu'=16] {'day','stu'}, use_global_device_ids=true, to_apply=%region_8.0 | all-reduce | flops 1 | bytes 8 | tf_op jit(solution)/shard_map/psum | solution.py:52
  288.4 4.4 collective-permute-start.4
  292.8 1.3 collective-permute-done.4
  294.2 4.5 fusion.53
  298.6 1.3 collective-permute-start.5
  299.9 18.8 %all_gather.14 = f32[32,256]{0,1:T(8,128)S(1)} all-gather(f32[32,16]{0,1:T(8,128)S(1)} %multiply_add_fusion.2), channel_id=1, replica_groups=mesh['day'=2,'stu'=16] {'stu'}, dimensions={1}, use_global_device_ids=true | all-gather | bytes 34816 | tf_op jit(solution)/shard_map/all_gather | solution.py:40
  318.7 5.2 %multiply_reduce_fusion.2 = (f32[]{:T(128)}, f32[32,16]{0,1:T(8,128)S(1)}) fusion(f32[32,16]{0,1:T(8,128)S(1)} %multiply_add_fusion.2, f32[7,16]{0,1:T(8,128)S(1)} %collective-permute-done.5, f32[32,16]{0,1:T(8,128)S(1)} %fusion.53, f32[]{:T(128)} %bitcast.7, f32[]{:T(128)} %bitcast.6, f32[]{:T(128)} %bitcast.5, f32[]{:T(128)} %bitcast.4, f32[]{:T(128)} %bitcast.3, ...), kind=kOutput, calls=%fused_computation.231 | convolution fusion | flops 1585151 | bytes 55776 | tf_op jit(solution)/shard_map/dot_general | solution.py:39
  323.9 38.4 %psum.53 = f32[]{:T(128)} all-reduce(f32[]{:T(128)} %get-tuple-element.10), channel_id=1, replica_groups=mesh['day'=2,'stu'=16] {'day','stu'}, use_global_device_ids=true, to_apply=%region_10.0 | all-reduce | flops 1 | bytes 8 | tf_op jit(solution)/shard_map/psum | solution.py:52
  364.2 42.5 %psum.54 = f32[]{:T(128)} all-reduce(f32[]{:T(128)} %get-tuple-element.8), channel_id=1, replica_groups=mesh['day'=2,'stu'=16] {'day','stu'}, use_global_device_ids=true, to_apply=%region_12.0 | all-reduce | flops 1 | bytes 8 | tf_op jit(solution)/shard_map/psum | solution.py:52
  408.1 4.4 collective-permute-start.6
  412.6 1.3 collective-permute-done.6
  413.9 4.5 fusion.20
  418.4 1.3 collective-permute-start.7
  419.7 19.1 %all_gather.15 = f32[32,256]{0,1:T(8,128)S(1)} all-gather(f32[32,16]{0,1:T(8,128)S(1)} %multiply_add_fusion.1), channel_id=1, replica_groups=mesh['day'=2,'stu'=16] {'stu'}, dimensions={1}, use_global_device_ids=true | all-gather | bytes 34816 | tf_op jit(solution)/shard_map/all_gather | solution.py:40
  438.8 5.1 %multiply_reduce_fusion = (f32[]{:T(128)}, f32[32,16]{0,1:T(8,128)S(1)}) fusion(f32[32,16]{0,1:T(8,128)S(1)} %multiply_add_fusion.1, f32[7,16]{0,1:T(8,128)S(1)} %collective-permute-done.7, f32[32,16]{0,1:T(8,128)S(1)} %fusion.20, f32[]{:T(128)} %bitcast.7, f32[]{:T(128)} %bitcast.6, f32[]{:T(128)} %bitcast.5, f32[]{:T(128)} %bitcast.4, f32[]{:T(128)} %bitcast.3, ...), kind=kOutput, calls=%fused_computation.227 | convolution fusion | flops 1585151 | bytes 55776 | tf_op jit(solution)/shard_map/dot_general | solution.py:39
  444.0 38.1 %psum.55 = f32[]{:T(128)} all-reduce(f32[]{:T(128)} %get-tuple-element.6), channel_id=1, replica_groups=mesh['day'=2,'stu'=16] {'day','stu'}, use_global_device_ids=true, to_apply=%region_14.0 | all-reduce | flops 1 | bytes 8 | tf_op jit(solution)/shard_map/psum | solution.py:52
  (33 shorter events, 6.0 us)
Async XLA Ops:
  7.2 8.3 %copy-start = (bf16[1024,256]{1,0:T(8,128)(2,1)S(1)}, bf16[1024,256]{1,0:T(8,128)(2,1)}, u32[]{:S(2)}) copy-start(bf16[1024,256]{1,0:T(8,128)(2,1)} %param.7) | copy-start | bytes 1572868
  7.2 8.3 %copy-start.1 = (bf16[32,8,1024]{2,1,0:T(8,128)(2,1)S(1)}, bf16[32,8,1024]{2,1,0:T(8,128)(2,1)}, u32[]{:S(2)}) copy-start(bf16[32,8,1024]{2,1,0:T(8,128)(2,1)} %param.5) | copy-start | bytes 1572868
  7.2 97.0 %all-reduce.3.cloned.1.call-start = ((), (), s32[]{:S(2)}) async-start(), calls=%async_computation.2 | async-start | bytes 524288 | tf_op jit(solution)/shard_map/psum | solution.py:56
  8.3 31.6 %collective-permute-start = (f32[7,16]{0,1:T(8,128)S(1)}, f32[7,16]{0,1:T(8,128)S(1)}, u32[]{:S(2)}, u32[]{:S(2)}) collective-permute-start(f32[7,16]{0,1:T(8,128)S(1)} %slice.333), channel_id=1, source_target_pairs={{0,16},{1,17},{2,18},{3,19},{4,20},{5,21},{6,22},{7,23},{8,24},{9,... | collective-permute-start | bytes 1352 | tf_op jit(solution)/shard_map/ppermute | solution.py:16
  14.8 0.7 copy-start.2
  14.8 148.3 %reduce-scatter.2.cloned.1.call-start = ((), (), s32[]{:S(2)}) async-start(), calls=%async_computation.1 | async-start | bytes 139264 | tf_op jit(solution)/shard_map/reduce_scatter | solution.py:74
  16.6 0.7 copy-start.3
  44.4 60.5 %collective-permute-start.1 = (f32[7,16]{0,1:T(8,128)S(1)}, f32[7,16]{0,1:T(8,128)S(1)}, u32[]{:S(2)}, u32[]{:S(2)}) collective-permute-start(f32[7,16]{0,1:T(8,128)S(1)} %bitcast.27), channel_id=1, source_target_pairs={{16,0},{17,1},{18,2},{19,3},{20,4},{21,5},{22,6},{23,7},{24,8},{25... | collective-permute-start | bytes 1352 | tf_op jit(solution)/shard_map/ppermute | solution.py:16
  168.5 4.7 collective-permute-start.2
  177.7 21.1 %collective-permute-start.3 = (f32[7,16]{0,1:T(8,128)S(1)}, f32[7,16]{0,1:T(8,128)S(1)}, u32[]{:S(2)}, u32[]{:S(2)}) collective-permute-start(f32[7,16]{0,1:T(8,128)S(1)} %bitcast.29), channel_id=1, source_target_pairs={{16,0},{17,1},{18,2},{19,3},{20,4},{21,5},{22,6},{23,7},{24,8},{25... | collective-permute-start | bytes 1352 | tf_op jit(solution)/shard_map/ppermute | solution.py:16
  288.4 5.7 %collective-permute-start.4 = (f32[7,16]{0,1:T(8,128)S(1)}, f32[7,16]{0,1:T(8,128)S(1)}, u32[]{:S(2)}, u32[]{:S(2)}) collective-permute-start(f32[7,16]{0,1:T(8,128)S(1)} %slice.385), channel_id=1, source_target_pairs={{0,16},{1,17},{2,18},{3,19},{4,20},{5,21},{6,22},{7,23},{8,24},{9,... | collective-permute-start | bytes 1352 | tf_op jit(solution)/shard_map/ppermute | solution.py:16
  298.6 20.1 %collective-permute-start.5 = (f32[7,16]{0,1:T(8,128)S(1)}, f32[7,16]{0,1:T(8,128)S(1)}, u32[]{:S(2)}, u32[]{:S(2)}) collective-permute-start(f32[7,16]{0,1:T(8,128)S(1)} %bitcast.30), channel_id=1, source_target_pairs={{16,0},{17,1},{18,2},{19,3},{20,4},{21,5},{22,6},{23,7},{24,8},{25... | collective-permute-start | bytes 1352 | tf_op jit(solution)/shard_map/ppermute | solution.py:16
  408.1 5.8 %collective-permute-start.6 = (f32[7,16]{0,1:T(8,128)S(1)}, f32[7,16]{0,1:T(8,128)S(1)}, u32[]{:S(2)}, u32[]{:S(2)}) collective-permute-start(f32[7,16]{0,1:T(8,128)S(1)} %slice.411), channel_id=1, source_target_pairs={{0,16},{1,17},{2,18},{3,19},{4,20},{5,21},{6,22},{7,23},{8,24},{9,... | collective-permute-start | bytes 1352 | tf_op jit(solution)/shard_map/ppermute | solution.py:16
  418.4 20.4 %collective-permute-start.7 = (f32[7,16]{0,1:T(8,128)S(1)}, f32[7,16]{0,1:T(8,128)S(1)}, u32[]{:S(2)}, u32[]{:S(2)}) collective-permute-start(f32[7,16]{0,1:T(8,128)S(1)} %bitcast.28), channel_id=1, source_target_pairs={{16,0},{17,1},{18,2},{19,3},{20,4},{21,5},{22,6},{23,7},{24,8},{25... | collective-permute-start | bytes 1352 | tf_op jit(solution)/shard_map/ppermute | solution.py:16
Sparse Core Ops, SparseCore 0:
  15.0 89.1 all-reduce.2
  107.6 55.5 reduce-scatter.1
where the time goes:
time: 494 us; the launch traced here: 491 us
  blocking collectives  280 us (57%)
  waiting for transfers between devices  121 us (24%)
  matrix products  23.1 us (5%)
  starting transfers between devices  22.3 us (5%)
  between operations  20.9 us (4%)
  other arithmetic  20.4 us (4%)
    psum x5, blocking collectives, global_total(): return lax.psum(value, ('day', 'stu'))  200 us
    all_gather x4, blocking collectives, with_gram(): lax.all_gather(values, 'stu', axis=1, tiled=True)  79.7 us
    psum x1, waiting for transfers between devices, summed_gram(): return lax.psum(local_gram, 'stu')  58.5 us
    reduce_scatter x1, waiting for transfers between devices, local(): lax.psum_scatter(local_terms, 'stu', scatter_dimension=1, tiled=True)  58.3 us
    ppermute x8, starting transfers between devices, shifted(): return lax.ppermute(block, axis, route)  22.2 us
    dot_general x4, matrix products, with_gram(): jnp.dot(lax.all_gather(values, 'stu', axis=1, tiled=True), gram_part, pre...  20.8 us
    sub x4, other arithmetic, filter_rows(): out = out - coef[lag - 1] * extended[LAGS - lag:LAGS - lag + count]  17.8 us
  transfers between devices with their start and end apart: 10, of which 5 were waited for; matrix products, arithmetic and copies ran while one was open for 2% of the time, Pallas kernels for 0%

commit v1 on v0

v1 whole, which is shorter than its diff:
```python
import functools

import jax
import jax.numpy as jnp
from jax import lax
from jax.experimental import pallas as pl
from jax.experimental.pallas import tpu as pltpu
from jax.sharding import PartitionSpec as P

LAGS = 7
ITERS = 3
PAD = 8
LANES = 128
CHUNKS = 4


smoothing = 1.0


def exchange(block, axis, bit):
    route = [(i, i ^ bit) for i in range(lax.axis_size(axis))]
    return lax.ppermute(block, axis, route)


def split(values):
    high = values.astype(jnp.bfloat16)
    return high, (values - high.astype(jnp.float32)).astype(jnp.bfloat16)


def product(a, b):
    return jnp.dot(a, b, preferred_element_type=jnp.float32)


def front_kernel(days, students, perf_hbm, skill_hbm, student_ref, out_ref, perf, skill, proj, sems):
    depth = perf.shape[1] // CHUNKS
    copies = []
    for c in range(CHUNKS):
        part = pl.ds(c * depth, depth)
        one = pltpu.make_async_copy(perf_hbm.at[:, part], perf.at[:, part], sems.at[0, c])
        two = pltpu.make_async_copy(skill_hbm.at[part], skill.at[part], sems.at[1, c])
        one.start()
        two.start()
        copies.append((one, two))
    wide = student_ref[...].astype(jnp.float32)
    total = None
    for c in range(CHUNKS):
        part = pl.ds(c * depth, depth)
        for copy in copies[c]:
            copy.wait()
        term = product(perf[:, part], skill[part])
        total = term if total is None else total + term
    tiles = proj.shape[0]
    for t in range(tiles):
        lanes = pl.ds(t * LANES, LANES)
        proj[t] = total[:, t * LANES : (t + 1) * LANES]
        terms = None
        for s in range(students):
            row = proj[t, pl.ds(s, days, stride=students), :] * wide[s : s + 1, t * LANES : (t + 1) * LANES]
            terms = row if terms is None else terms + row
        out_ref[:days, lanes] = terms
    out_ref[days:, :] = wide


def front(performance, student_factor, skill_factor):
    days, students, skills = performance.shape
    rank = skill_factor.shape[1]
    return pl.pallas_call(
        functools.partial(front_kernel, days, students),
        out_shape=jax.ShapeDtypeStruct((days + students, rank), jnp.float32),
        in_specs=[
            pl.BlockSpec(memory_space=pl.ANY),
            pl.BlockSpec(memory_space=pl.ANY),
            pl.BlockSpec(memory_space=pltpu.VMEM),
        ],
        out_specs=pl.BlockSpec(memory_space=pltpu.VMEM),
        scratch_shapes=[
            pltpu.VMEM((days * students, skills), jnp.bfloat16),
            pltpu.VMEM((skills, rank), jnp.bfloat16),
            pltpu.VMEM((rank // LANES, days * students, LANES), jnp.float32),
            pltpu.SemaphoreType.DMA((2, CHUNKS)),
        ],
        cost_estimate=pl.CostEstimate(
            flops=2 * days * students * skills * rank,
            bytes_accessed=2 * (days * students + rank) * skills,
            transcendentals=0,
        ),
    )(performance.reshape(days * students, skills), skill_factor, student_factor)


def cg_kernel(
    where_ref, coef_ref, mine_ref, other_ref, gram_ref, factor_ref, residual_ref, mttkrp, values, low, high, block
):
    half = mine_ref.shape[0] // 2
    total = 2 * half
    mine = pl.multiple_of(where_ref[0] * half, half)
    other = pl.multiple_of((1 - where_ref[0]) * half, half)
    for place, source in ((mine, mine_ref), (other, other_ref)):
        mttkrp[pl.ds(place, half), :] = source[:half, :]
        values[pl.ds(place, half), :] = source[half:, :]
    gram_high, gram_low = split(gram_ref[...])
    width = gram_ref.shape[1]
    low[:PAD, :] = jnp.zeros((PAD, width), jnp.float32)
    high[pl.ds(total, PAD), :] = jnp.zeros((PAD, width), jnp.float32)
    coef = [coef_ref[l] for l in range(LAGS)]

    def operate(v):
        v_high, v_low = split(v)
        mixed = product(v_high, gram_high) + (product(v_low, gram_high) + product(v_high, gram_low))
        low[pl.ds(PAD, total), :] = v
        ahead = v
        for lag in range(1, LAGS + 1):
            ahead = ahead - coef[lag - 1] * low[pl.ds(PAD - lag, total), :]
        high[:total, :] = ahead
        back = ahead
        for lag in range(1, LAGS + 1):
            back = back - coef[lag - 1] * high[pl.ds(lag, total), :]
        return mixed + smoothing * back

    def inner(a, b):
        return jnp.sum(jnp.sum(a * b, axis=0, keepdims=True), axis=1, keepdims=True)

    factor = values[...]
    residual = mttkrp[...] - operate(factor)
    direction = residual
    now = inner(residual, residual)
    for step in range(ITERS):
        image = operate(direction)
        alpha = now / inner(direction, image)
        factor = factor + alpha * direction
        residual = residual - alpha * image
        if step < ITERS - 1:
            following = inner(residual, residual)
            direction = residual + (following / now) * direction
            now = following
    days, columns = factor_ref.shape
    start = pl.multiple_of(where_ref[1] * days, days)
    for result, target in ((factor, factor_ref), (residual, residual_ref)):
        block[...] = result
        rows = block[pl.ds(start, days), :]
        target[...] = pltpu.roll(rows, where_ref[2], axis=1)[:, :columns]


def conjugate(where, coef, mine, other, gram, days, columns):
    half = mine.shape[0] // 2
    width = gram.shape[1]
    total = 2 * half
    vmem = pl.BlockSpec(memory_space=pltpu.VMEM)
    smem = pl.BlockSpec(memory_space=pltpu.SMEM)
    shape = jax.ShapeDtypeStruct((days, columns), jnp.float32)
    return pl.pallas_call(
        cg_kernel,
        out_shape=(shape, shape),
        in_specs=[smem, smem, vmem, vmem, vmem],
        out_specs=(vmem, vmem),
        scratch_shapes=[
            pltpu.VMEM((total, width), jnp.float32),
            pltpu.VMEM((total, width), jnp.float32),
            pltpu.VMEM((total + PAD, width), jnp.float32),
            pltpu.VMEM((total + PAD, width), jnp.float32),
            pltpu.VMEM((total, width), jnp.float32),
        ],
        cost_estimate=pl.CostEstimate(
            flops=24 * total * width * width, bytes_accessed=4 * width * (width + 2 * total), transcendentals=0
        ),
    )(where, coef, mine, other, gram)


def bits_of(count):
    assert count & (count - 1) == 0 and count > 1
    return [1 << b for b in range(count.bit_length() - 1)]


def local(performance, student_factor, skill_factor, day_prev, ar_coef):
    days, students, _ = performance.shape
    rank = skill_factor.shape[1]
    columns = rank // lax.axis_size("stu")
    payload = front(performance, student_factor, skill_factor)
    skill_gram = lax.dot_general(
        skill_factor, skill_factor, (((0,), (0,)), ((), ())), preferred_element_type=jnp.float32
    )
    for bit in reversed(bits_of(lax.axis_size("stu"))):
        got = exchange(payload, "stu", bit)
        payload = jnp.concatenate([payload[:days] + got[:days], payload[days:], got[days:]], 0)
    student = payload[days:].astype(jnp.bfloat16)
    student_gram = lax.dot_general(
        student, student, (((0,), (0,)), ((), ())), preferred_element_type=jnp.float32
    )
    gram = student_gram * skill_gram
    day = lax.axis_index("day")
    mttkrp, factor = payload[:days], day_prev
    bits = bits_of(lax.axis_size("day"))
    for bit in bits:
        mine = jnp.concatenate([mttkrp, factor], 0)
        other = exchange(mine, "day", bit)
        upper = (day // bit) % 2
        if bit != bits[-1]:
            half = mttkrp.shape[0]
            first = jnp.where(upper == 0, mine, other)
            second = jnp.where(upper == 0, other, mine)
            mttkrp = jnp.concatenate([first[:half], second[:half]], 0)
            factor = jnp.concatenate([first[half:], second[half:]], 0)
    stu = lax.axis_index("stu")
    where = jnp.stack([upper, day, (rank - stu * columns) % rank]).astype(jnp.int32)
    return conjugate(where, ar_coef, mine, other, gram, days, columns)


def solution(mesh):
    return jax.shard_map(
        local,
        mesh=mesh,
        in_specs=(P("day", "stu", None), P("stu", None), P(), P("day", None), P()),
        out_specs=(P("day", "stu"), P("day", "stu")),
        check_vma=False,
    )
```

time: 494 us -> 31 us (0.06)
  blocking collectives: 280 us -> 0 us
  waiting for transfers between devices: 121 us -> 9.66 us
  matrix products: 23.1 us -> 1.26 us
  between operations: 20.9 us -> 0.79 us
  other arithmetic: 20.4 us -> 0.7 us
  starting transfers between devices: 22.3 us -> 9.26 us
  Pallas kernels: 0 us -> 6.3 us
    psum x5 -> x0, blocking collectives: 200 us -> none  [global_total(): return lax.psum(value, ('day', 'stu'))]
    all_gather x4 -> x0, blocking collectives: 79.7 us -> none  [with_gram(): lax.all_gather(values, 'stu', axis=1, tiled=True)]
    psum x1 -> x0, waiting for transfers between devices: 58.5 us -> none  [summed_gram(): return lax.psum(local_gram, 'stu')]
    reduce_scatter x1 -> x0, waiting for transfers between devices: 58.3 us -> none  [local(): lax.psum_scatter(local_terms, 'stu', scatter_dimension=1, tiled=True)]
    dot_general x7 -> x2, matrix products: 23.1 us -> 1.26 us  [the longest x1 0.92 us: local(): lax.dot_general(student, student, (((0,), (0,)), ((), ())), preferred_ele...]
    sub x5 -> x0, other arithmetic: 18.4 us -> none  [the longest x4 17.8 us: filter_rows(): out = out - coef[lag - 1] * extended[LAGS - lag:LAGS - lag + count]]
    ppermute x8 -> x5, starting transfers between devices: 22.2 us -> 9.26 us  [exchange(): return lax.ppermute(block, axis, route)]
    pallas_call x0 -> x2, Pallas kernels: none -> 6.3 us  [the longest x1 3.15 us: conjugate(): pl.pallas_call(cg_kernel, out_shape=(shape, shape), in_specs=[smem, smem,...]
  transfers between devices with their start and end apart: 10 -> 5, of which waited for: 5 -> 5; matrix products, arithmetic and copies ran while one was open for 2% -> 6% of each run, Pallas kernels for 0% -> 0%
where the time goes in v1:
time: 31 us; the launch traced here: 30.7 us
  waiting for transfers between devices  9.66 us (31%)
  starting transfers between devices  9.26 us (30%)
  Pallas kernels  6.3 us (20%)
  local copies, waits for them, and re-layouts  2.75 us (9%)
  matrix products  1.26 us (4%)
  between operations  0.79 us (3%)
  other arithmetic  0.7 us (2%)
    ppermute x5, waiting for transfers between devices, exchange(): return lax.ppermute(block, axis, route)  9.66 us
    ppermute x5, starting transfers between devices, exchange(): return lax.ppermute(block, axis, route)  9.26 us
    pallas_call x1, Pallas kernels, conjugate(): pl.pallas_call(cg_kernel, out_shape=(shape, shape), in_specs=[smem, smem,...  3.15 us
    pallas_call x1, Pallas kernels, front(): pl.pallas_call(functools.partial(front_kernel, days, students), out_shape...  3.15 us
    pallas_call x2, local copies, waits for them, and re-layouts, conjugate(): pl.pallas_call(cg_kernel, out_shape=(shape, shape), in_specs=[smem, smem,...  2.07 us
    dot_general x1, matrix products, local(): lax.dot_general(student, student, (((0,), (0,)), ((), ())), preferred_ele...  0.92 us
    unnamed x19, local copies, waits for them, and re-layouts  0.66 us
    another operation x1, other arithmetic, local(): jnp.stack([upper, day, (rank - stu * columns) % rank]).astype(jnp.int32)  0.65 us
  transfers between devices with their start and end apart: 5, of which 5 were waited for; matrix products, arithmetic and copies ran while one was open for 6% of the time, Pallas kernels for 0%

profile of v1, /device:TPU:0, one launch (start us, length us, event | category | flops | bytes accessed | tf_op | source)
XLA Modules:
  0.0 30.7 jit_solution(13340596838332564070)
XLA Ops:
  0.6 0.0 copy-start
  0.6 3.1 %shard_map.68 = f32[40,256]{1,0:T(8,128)} custom-call(bf16[256,1024]{1,0:T(8,128)(2,1)} %bitcast.8, bf16[1024,256]{1,0:T(8,128)(2,1)} %skill_hbm.1, bf16[8,256]{1,0:T(8,128)(2,1)} %student_ref.1), custom_call_target="tpu_custom_call" | custom-call | flops 134217728 | bytes 1048576 | tf_op jit(solution)/shard_map/pallas_call | solution.py:67
  3.8 0.0 copy-start.2
  3.8 4.1 %collective-permute-start = (f32[40,256]{1,0:T(8,128)}, f32[40,256]{1,0:T(8,128)S(1)}, u32[]{:S(2)}, u32[]{:S(2)}) collective-permute-start(f32[40,256]{1,0:T(8,128)} %shard_map.68), channel_id=1, source_target_pairs={{0,8},{1,9},{2,10},{3,11},{4,12},{5,13},{6,14},{7,15},{8,0},{9,1},... | collective-permute-start | bytes 122888 | tf_op jit(solution)/shard_map/ppermute | solution.py:22
  7.9 0.0 copy-done.2
  7.9 0.0 copy-done
  7.9 0.3 %fusion.1 = f32[256,256]{1,0:T(8,128)S(1)} fusion(bf16[1024,256]{1,0:T(8,128)(2,1)S(1)} %copy-done), kind=kOutput, calls=%fused_computation.21 | convolution fusion | flops 134217728 | bytes 786432 | tf_op jit(solution)/shard_map/dot_general | solution.py:178
  8.3 0.7 %pad_add_fusion.where_ref = s32[3]{0:T(128)} fusion(s32[1]{0:T(128)} %bitcast.2, s32[1]{0:T(128)} %bitcast.1, s32[1]{0:T(128)} %bitcast), kind=kLoop, calls=%fused_computation.20 | loop fusion | flops 6 | bytes 24 | tf_op jit(solution)/shard_map/stack | solution.py:203
  8.9 1.6 %collective-permute-done = f32[40,256]{1,0:T(8,128)S(1)} collective-permute-done((f32[40,256]{1,0:T(8,128)}, f32[40,256]{1,0:T(8,128)S(1)}, u32[]{:S(2)}, u32[]{:S(2)}) %collective-permute-start) | collective-permute-done | bytes 40992 | tf_op jit(solution)/shard_map/ppermute | solution.py:22
  10.6 1.5 %collective-permute-start.1 = (f32[48,256]{1,0:T(8,128)S(1)}, f32[48,256]{1,0:T(8,128)S(1)}, u32[]{:S(2)}, u32[]{:S(2)}) collective-permute-start(f32[48,256]{1,0:T(8,128)S(1)} %pad_maximum_fusion.2), channel_id=1, source_target_pairs={{0,4},{1,5},{2,6},{3,7},{4,0},{5,1},{6,2},{7,3},{8,12},{9,13},{10,... | collective-permute-start | bytes 147464 | tf_op jit(solution)/shard_map/ppermute | solution.py:22
  12.1 2.6 %collective-permute-done.1 = f32[48,256]{1,0:T(8,128)S(1)} collective-permute-done((f32[48,256]{1,0:T(8,128)S(1)}, f32[48,256]{1,0:T(8,128)S(1)}, u32[]{:S(2)}, u32[]{:S(2)}) %collective-permute-start.1) | collective-permute-done | bytes 49184 | tf_op jit(solution)/shard_map/ppermute | solution.py:22
  14.7 1.8 %collective-permute-start.2 = (f32[64,256]{1,0:T(8,128)S(1)}, f32[64,256]{1,0:T(8,128)S(1)}, u32[]{:S(2)}, u32[]{:S(2)}) collective-permute-start(f32[64,256]{1,0:T(8,128)S(1)} %pad_maximum_fusion), channel_id=1, source_target_pairs={{0,2},{1,3},{2,0},{3,1},{4,6},{5,7},{6,4},{7,5},{8,10},{9,11},{10,... | collective-permute-start | bytes 196616 | tf_op jit(solution)/shard_map/ppermute | solution.py:22
  16.5 2.6 %collective-permute-done.2 = f32[64,256]{1,0:T(8,128)S(1)} collective-permute-done((f32[64,256]{1,0:T(8,128)S(1)}, f32[64,256]{1,0:T(8,128)S(1)}, u32[]{:S(2)}, u32[]{:S(2)}) %collective-permute-start.2) | collective-permute-done | bytes 65568 | tf_op jit(solution)/shard_map/ppermute | solution.py:22
  19.1 0.1 collective-permute-start.3
  19.2 0.0 copy-start.4
  19.2 1.3 %collective-permute-done.3 = f32[96,256]{1,0:T(8,128)S(1)} collective-permute-done((f32[96,256]{1,0:T(8,128)S(1)}, f32[96,256]{1,0:T(8,128)S(1)}, u32[]{:S(2)}, u32[]{:S(2)}) %collective-permute-start.3) | collective-permute-done | bytes 98336 | tf_op jit(solution)/shard_map/ppermute | solution.py:22
  20.5 0.0 copy-done.4
  20.5 0.0 copy-start.1
  20.5 1.8 %collective-permute-start.4 = (f32[64,256]{1,0:T(8,128)S(1)}, f32[64,256]{1,0:T(8,128)S(1)}, u32[]{:S(2)}, u32[]{:S(2)}) collective-permute-start(f32[64,256]{1,0:T(8,128)S(1)} %pad_maximum_fusion.1.mine_ref), channel_id=1, source_target_pairs={{0,16},{16,0},{1,17},{17,1},{2,18},{18,2},{3,19},{19,3},{4,20},{20... | collective-permute-start | bytes 196616 | tf_op jit(solution)/shard_map/ppermute | solution.py:22
  22.3 0.9 %convolution_multiply_fusion.gram_ref = f32[256,256]{1,0:T(8,128)} fusion(f32[256,256]{1,0:T(8,128)S(1)} %fusion.1, bf16[128,256]{1,0:T(8,128)(2,1)S(1)} %fusion), kind=kOutput, calls=%fused_computation | convolution fusion | flops 16842752 | bytes 589824 | tf_op jit(solution)/shard_map/dot_general | solution.py:185
  23.2 0.0 copy-done.1
  23.3 1.6 %collective-permute-done.4.other_ref = f32[64,256]{1,0:T(8,128)S(1)} collective-permute-done((f32[64,256]{1,0:T(8,128)S(1)}, f32[64,256]{1,0:T(8,128)S(1)}, u32[]{:S(2)}, u32[]{:S(2)}) %collective-permute-start.4) | collective-permute-done | bytes 65568 | tf_op jit(solution)/shard_map/ppermute | solution.py:22
  24.9 0.0 copy-start.3
  24.9 0.6 %copy-done.3 = f32[64,256]{1,0:T(8,128)} copy-done((f32[64,256]{1,0:T(8,128)}, f32[64,256]{1,0:T(8,128)S(1)}, u32[]{:S(2)}) %copy-start.3) | copy-done | bytes 65560
  25.5 3.2 %shard_map.69 = (f32[32,16]{1,0:T(8,128)}, f32[32,16]{1,0:T(8,128)}) custom-call(s32[3]{0:T(128)} %pad_add_fusion.where_ref, f32[7]{0:T(128)} %coef_ref.1, f32[64,256]{1,0:T(8,128)} %copy-done.1, f32[64,256]{1,0:T(8,128)} %copy-done.3, f32[256,256]{1,0:T(8,128)} %convolution_multiply_fusion.gram_ref), custom_call_target="tpu_custom_call" | custom-call | flops 100663296 | bytes 393216 | tf_op jit(solution)/shard_map/pallas_call | solution.py:150
  28.6 0.0 copy-start.5
  28.6 1.4 %copy.7 = f32[32,16]{0,1:T(8,128)} copy(f32[32,16]{1,0:T(8,128)} %get-tuple-element.2) | data formatting | bytes 4096 | tf_op jit(solution)/shard_map/pallas_call | solution.py:150
  30.0 0.0 copy-done.5
  30.0 0.7 %copy.8 = f32[32,16]{0,1:T(8,128)} copy(f32[32,16]{1,0:T(8,128)S(1)} %copy-done.5) | data formatting | bytes 4096 | tf_op jit(solution)/shard_map/pallas_call | solution.py:150
  (19 shorter events, 0.1 us)
Async XLA Ops:
  0.6 7.3 %copy-start = (bf16[1024,256]{1,0:T(8,128)(2,1)S(1)}, bf16[1024,256]{1,0:T(8,128)(2,1)}, u32[]{:S(2)}) copy-start(bf16[1024,256]{1,0:T(8,128)(2,1)} %skill_hbm.1) | copy-start | bytes 1572868
  3.8 4.1 %copy-start.2 = (f32[40,256]{1,0:T(8,128)S(1)}, f32[40,256]{1,0:T(8,128)}, u32[]{:S(2)}) copy-start(f32[40,256]{1,0:T(8,128)} %shard_map.68) | copy-start | bytes 122884
  3.8 6.7 %collective-permute-start = (f32[40,256]{1,0:T(8,128)}, f32[40,256]{1,0:T(8,128)S(1)}, u32[]{:S(2)}, u32[]{:S(2)}) collective-permute-start(f32[40,256]{1,0:T(8,128)} %shard_map.68), channel_id=1, source_target_pairs={{0,8},{1,9},{2,10},{3,11},{4,12},{5,13},{6,14},{7,15},{8,0},{9,1},... | collective-permute-start | bytes 122888 | tf_op jit(solution)/shard_map/ppermute | solution.py:22
  10.6 4.2 %collective-permute-start.1 = (f32[48,256]{1,0:T(8,128)S(1)}, f32[48,256]{1,0:T(8,128)S(1)}, u32[]{:S(2)}, u32[]{:S(2)}) collective-permute-start(f32[48,256]{1,0:T(8,128)S(1)} %pad_maximum_fusion.2), channel_id=1, source_target_pairs={{0,4},{1,5},{2,6},{3,7},{4,0},{5,1},{6,2},{7,3},{8,12},{9,13},{10,... | collective-permute-start | bytes 147464 | tf_op jit(solution)/shard_map/ppermute | solution.py:22
  14.7 4.3 %collective-permute-start.2 = (f32[64,256]{1,0:T(8,128)S(1)}, f32[64,256]{1,0:T(8,128)S(1)}, u32[]{:S(2)}, u32[]{:S(2)}) collective-permute-start(f32[64,256]{1,0:T(8,128)S(1)} %pad_maximum_fusion), channel_id=1, source_target_pairs={{0,2},{1,3},{2,0},{3,1},{4,6},{5,7},{6,4},{7,5},{8,10},{9,11},{10,... | collective-permute-start | bytes 196616 | tf_op jit(solution)/shard_map/ppermute | solution.py:22
  19.1 1.4 %collective-permute-start.3 = (f32[96,256]{1,0:T(8,128)S(1)}, f32[96,256]{1,0:T(8,128)S(1)}, u32[]{:S(2)}, u32[]{:S(2)}) collective-permute-start(f32[96,256]{1,0:T(8,128)S(1)} %slice_dynamic-update-slice_fusion), channel_id=1, source_target_pairs={{0,1},{1,0},{2,3},{3,2},{4,5},{5,4},{6,7},{7,6},{8,9},{9,8},{10,11... | collective-permute-start | bytes 294920 | tf_op jit(solution)/shard_map/ppermute | solution.py:22
  19.2 1.3 %copy-start.4 = (f32[32,256]{1,0:T(8,128)S(1)}, f32[32,256]{1,0:T(8,128)}, u32[]{:S(2)}) copy-start(f32[32,256]{1,0:T(8,128)} %param.8) | copy-start | bytes 98308
  20.5 2.7 %copy-start.1 = (f32[64,256]{1,0:T(8,128)}, f32[64,256]{1,0:T(8,128)S(1)}, u32[]{:S(2)}) copy-start(f32[64,256]{1,0:T(8,128)S(1)} %pad_maximum_fusion.1.mine_ref) | copy-start | bytes 196612
  20.5 4.3 %collective-permute-start.4 = (f32[64,256]{1,0:T(8,128)S(1)}, f32[64,256]{1,0:T(8,128)S(1)}, u32[]{:S(2)}, u32[]{:S(2)}) collective-permute-start(f32[64,256]{1,0:T(8,128)S(1)} %pad_maximum_fusion.1.mine_ref), channel_id=1, source_target_pairs={{0,16},{16,0},{1,17},{17,1},{2,18},{18,2},{3,19},{19,3},{4,20},{20... | collective-permute-start | bytes 196616 | tf_op jit(solution)/shard_map/ppermute | solution.py:22
  24.9 0.6 %copy-start.3 = (f32[64,256]{1,0:T(8,128)}, f32[64,256]{1,0:T(8,128)S(1)}, u32[]{:S(2)}) copy-start(f32[64,256]{1,0:T(8,128)S(1)} %collective-permute-done.4.other_ref) | copy-start | bytes 196612
  28.6 1.4 %copy-start.5 = (f32[32,16]{1,0:T(8,128)S(1)}, f32[32,16]{1,0:T(8,128)}, u32[]{:S(2)}) copy-start(f32[32,16]{1,0:T(8,128)} %get-tuple-element.3) | copy-start | bytes 6148

commit v2 on v1

--- a/solution.py
+++ b/solution.py
@@ -12,14 +12,15 @@
 PAD = 8
 LANES = 128
 CHUNKS = 4
+VMEM_BYTES = 8 << 20
+FRONT_BYTES = 429 << 17
 
 
 smoothing = 1.0
 
 
-def exchange(block, axis, bit):
-    route = [(i, i ^ bit) for i in range(lax.axis_size(axis))]
-    return lax.ppermute(block, axis, route)
+def exchange(block, mask):
+    return lax.ppermute(block, ("day", "stu"), [(i, i ^ mask) for i in range(lax.axis_size(("day", "stu")))])
 
 
 def split(values):
@@ -66,10 +67,11 @@
     rank = skill_factor.shape[1]
     return pl.pallas_call(
         functools.partial(front_kernel, days, students),
+        compiler_params=pltpu.CompilerParams(vmem_limit_bytes=FRONT_BYTES),
         out_shape=jax.ShapeDtypeStruct((days + students, rank), jnp.float32),
         in_specs=[
-            pl.BlockSpec(memory_space=pl.ANY),
-            pl.BlockSpec(memory_space=pl.ANY),
+            pl.BlockSpec(memory_space=pltpu.HBM),
+            pl.BlockSpec(memory_space=pltpu.HBM),
             pl.BlockSpec(memory_space=pltpu.VMEM),
         ],
         out_specs=pl.BlockSpec(memory_space=pltpu.VMEM),
@@ -132,12 +134,12 @@
             following = inner(residual, residual)
             direction = residual + (following / now) * direction
             now = following
-    days, columns = factor_ref.shape
+    columns, days = factor_ref.shape
     start = pl.multiple_of(where_ref[1] * days, days)
     for result, target in ((factor, factor_ref), (residual, residual_ref)):
         block[...] = result
         rows = block[pl.ds(start, days), :]
-        target[...] = pltpu.roll(rows, where_ref[2], axis=1)[:, :columns]
+        target[...] = pltpu.roll(rows, where_ref[2], axis=1)[:, :columns].T
 
 
 def conjugate(where, coef, mine, other, gram, days, columns):
@@ -146,9 +148,10 @@
     total = 2 * half
     vmem = pl.BlockSpec(memory_space=pltpu.VMEM)
     smem = pl.BlockSpec(memory_space=pltpu.SMEM)
-    shape = jax.ShapeDtypeStruct((days, columns), jnp.float32)
+    shape = jax.ShapeDtypeStruct((columns, days), jnp.float32)
     return pl.pallas_call(
         cg_kernel,
+        compiler_params=pltpu.CompilerParams(vmem_limit_bytes=VMEM_BYTES),
         out_shape=(shape, shape),
         in_specs=[smem, smem, vmem, vmem, vmem],
         out_specs=(vmem, vmem),
@@ -178,8 +181,9 @@
     skill_gram = lax.dot_general(
         skill_factor, skill_factor, (((0,), (0,)), ((), ())), preferred_element_type=jnp.float32
     )
-    for bit in reversed(bits_of(lax.axis_size("stu"))):
-        got = exchange(payload, "stu", bit)
+    stu_size, day_size = lax.axis_size("stu"), lax.axis_size("day")
+    for bit in reversed(bits_of(stu_size)):
+        got = exchange(payload, bit | 1)
         payload = jnp.concatenate([payload[:days] + got[:days], payload[days:], got[days:]], 0)
     student = payload[days:].astype(jnp.bfloat16)
     student_gram = lax.dot_general(
@@ -188,10 +192,10 @@
     gram = student_gram * skill_gram
     day = lax.axis_index("day")
     mttkrp, factor = payload[:days], day_prev
-    bits = bits_of(lax.axis_size("day"))
+    bits = bits_of(day_size)
     for bit in bits:
         mine = jnp.concatenate([mttkrp, factor], 0)
-        other = exchange(mine, "day", bit)
+        other = exchange(mine, bit * stu_size + 1)
         upper = (day // bit) % 2
         if bit != bits[-1]:
             half = mttkrp.shape[0]
@@ -201,7 +205,8 @@
             factor = jnp.concatenate([first[half:], second[half:]], 0)
     stu = lax.axis_index("stu")
     where = jnp.stack([upper, day, (rank - stu * columns) % rank]).astype(jnp.int32)
-    return conjugate(where, ar_coef, mine, other, gram, days, columns)
+    factor, residual = conjugate(where, ar_coef, mine, other, gram, days, columns)
+    return factor.T, residual.T
 
 
 def solution(mesh):

time: 31 us -> 25.6 us (0.83)
  local copies, waits for them, and re-layouts: 2.75 us -> 0.73 us
  Pallas kernels: 6.3 us -> 4.57 us
  matrix products: 1.26 us -> 0.55 us
  other arithmetic: 0.7 us -> 0.12 us
    pallas_call x2 -> x0, local copies, waits for them, and re-layouts: 2.07 us -> none  [conjugate(): pl.pallas_call(cg_kernel, out_shape=(shape, shape), in_specs=[smem, smem,...]
    pallas_call x2, Pallas kernels: 6.3 us -> 4.57 us  [the longest x1 2.72 us: conjugate(): pl.pallas_call(cg_kernel, compiler_params=pltpu.CompilerParams(vmem_limit...]
    dot_general x1, matrix products: 0.92 us -> 0.21 us  [local(): lax.dot_general(student, student, (((0,), (0,)), ((), ())), preferred_ele...]
    another operation x1, other arithmetic: 0.65 us -> 0.08 us  [local(): jnp.stack([upper, day, (rank - stu * columns) % rank]).astype(jnp.int32)]
    unnamed x19 -> x15, local copies, waits for them, and re-layouts: 0.66 us -> 0.71 us
  transfers between devices with their start and end apart: 5 -> 5, of which waited for: 5 -> 5; matrix products, arithmetic and copies ran while one was open for 6% -> 3% of each run, Pallas kernels for 0% -> 0%
where the time goes in v2:
time: 25.6 us; the launch traced here: 25.3 us
  waiting for transfers between devices  9.6 us (38%)
  starting transfers between devices  8.98 us (35%)
  Pallas kernels  4.57 us (18%)
  between operations  0.74 us (3%)
  local copies, waits for them, and re-layouts  0.73 us (3%)
  matrix products  0.55 us (2%)
    ppermute x5, waiting for transfers between devices, exchange(): lax.ppermute(block, ('day', 'stu'), [(i, i ^ mask) for i in range(lax.axi...  9.6 us
    ppermute x5, starting transfers between devices, exchange(): lax.ppermute(block, ('day', 'stu'), [(i, i ^ mask) for i in range(lax.axi...  8.98 us
    pallas_call x1, Pallas kernels, conjugate(): pl.pallas_call(cg_kernel, compiler_params=pltpu.CompilerParams(vmem_limit...  2.72 us
    pallas_call x1, Pallas kernels, front(): pl.pallas_call(functools.partial(front_kernel, days, students), compiler_...  1.85 us
    unnamed x15, local copies, waits for them, and re-layouts  0.71 us
  transfers between devices with their start and end apart: 5, of which 5 were waited for; matrix products, arithmetic and copies ran while one was open for 3% of the time, Pallas kernels for 0%

profile of v2, /device:TPU:0, one launch (start us, length us, event | category | flops | bytes accessed | tf_op | source)
XLA Modules:
  0.0 25.3 jit_solution(294165401304578977)
XLA Ops:
  0.6 0.0 copy-start
  0.6 0.7 %copy-done = bf16[8,256]{1,0:T(8,128)(2,1)S(1)} copy-done((bf16[8,256]{1,0:T(8,128)(2,1)S(1)}, bf16[8,256]{1,0:T(8,128)(2,1)}, u32[]{:S(2)}) %copy-start) | copy-done | bytes 4120
  1.3 0.0 copy-start.2
  1.3 1.9 %shard_map.68 = f32[40,256]{1,0:T(8,128)S(1)} custom-call(bf16[256,1024]{1,0:T(8,128)(2,1)} %bitcast.10, bf16[1024,256]{1,0:T(8,128)(2,1)} %skill_hbm.1, bf16[8,256]{1,0:T(8,128)(2,1)S(1)} %copy-done), custom_call_target="tpu_custom_call" | custom-call | flops 134217728 | bytes 1048576 | tf_op jit(solution)/shard_map/pallas_call | solution.py:68
  3.2 3.5 %collective-permute-start = (f32[40,256]{1,0:T(8,128)S(1)}, f32[40,256]{1,0:T(8,128)S(1)}, u32[]{:S(2)}, u32[]{:S(2)}) collective-permute-start(f32[40,256]{1,0:T(8,128)S(1)} %shard_map.68), channel_id=1, source_target_pairs={{0,9},{1,8},{2,11},{3,10},{4,13},{5,12},{6,15},{7,14},{8,1},{9,0},... | collective-permute-start | bytes 122888 | tf_op jit(solution)/shard_map/ppermute | solution.py:23
  6.7 0.0 copy-done.2
  6.7 0.3 %fusion.1 = f32[256,256]{1,0:T(8,128)S(1)} fusion(bf16[1024,256]{1,0:T(8,128)(2,1)S(1)} %copy-done.2), kind=kOutput, calls=%fused_computation.21 | convolution fusion | flops 134217728 | bytes 786432 | tf_op jit(solution)/shard_map/dot_general | solution.py:181
  7.1 0.1 pad_add_fusion.where_ref
  7.2 1.5 %collective-permute-done = f32[40,256]{1,0:T(8,128)S(1)} collective-permute-done((f32[40,256]{1,0:T(8,128)S(1)}, f32[40,256]{1,0:T(8,128)S(1)}, u32[]{:S(2)}, u32[]{:S(2)}) %collective-permute-start) | collective-permute-done | bytes 40992 | tf_op jit(solution)/shard_map/ppermute | solution.py:23
  8.7 2.1 %collective-permute-start.1 = (f32[48,256]{1,0:T(8,128)S(1)}, f32[48,256]{1,0:T(8,128)S(1)}, u32[]{:S(2)}, u32[]{:S(2)}) collective-permute-start(f32[48,256]{1,0:T(8,128)S(1)} %pad_maximum_fusion.2), channel_id=1, source_target_pairs={{0,5},{1,4},{2,7},{3,6},{4,1},{5,0},{6,3},{7,2},{8,13},{9,12},{10,... | collective-permute-start | bytes 147464 | tf_op jit(solution)/shard_map/ppermute | solution.py:23
  10.8 2.0 %collective-permute-done.1 = f32[48,256]{1,0:T(8,128)S(1)} collective-permute-done((f32[48,256]{1,0:T(8,128)S(1)}, f32[48,256]{1,0:T(8,128)S(1)}, u32[]{:S(2)}, u32[]{:S(2)}) %collective-permute-start.1) | collective-permute-done | bytes 49184 | tf_op jit(solution)/shard_map/ppermute | solution.py:23
  12.8 1.6 %collective-permute-start.2 = (f32[64,256]{1,0:T(8,128)S(1)}, f32[64,256]{1,0:T(8,128)S(1)}, u32[]{:S(2)}, u32[]{:S(2)}) collective-permute-start(f32[64,256]{1,0:T(8,128)S(1)} %pad_maximum_fusion), channel_id=1, source_target_pairs={{0,3},{1,2},{2,1},{3,0},{4,7},{5,6},{6,5},{7,4},{8,11},{9,10},{10,... | collective-permute-start | bytes 196616 | tf_op jit(solution)/shard_map/ppermute | solution.py:23
  14.4 2.6 %collective-permute-done.2 = f32[64,256]{1,0:T(8,128)S(1)} collective-permute-done((f32[64,256]{1,0:T(8,128)S(1)}, f32[64,256]{1,0:T(8,128)S(1)}, u32[]{:S(2)}, u32[]{:S(2)}) %collective-permute-start.2) | collective-permute-done | bytes 65568 | tf_op jit(solution)/shard_map/ppermute | solution.py:23
  17.0 0.2 collective-permute-start.3
  17.2 0.0 copy-start.3
  17.2 1.2 %collective-permute-done.3 = f32[96,256]{1,0:T(8,128)S(1)} collective-permute-done((f32[96,256]{1,0:T(8,128)S(1)}, f32[96,256]{1,0:T(8,128)S(1)}, u32[]{:S(2)}, u32[]{:S(2)}) %collective-permute-start.3) | collective-permute-done | bytes 98336 | tf_op jit(solution)/shard_map/ppermute | solution.py:23
  18.4 0.0 copy-done.3
  18.4 1.6 %collective-permute-start.4 = (f32[64,256]{1,0:T(8,128)S(1)}, f32[64,256]{1,0:T(8,128)S(1)}, u32[]{:S(2)}, u32[]{:S(2)}) collective-permute-start(f32[64,256]{1,0:T(8,128)S(1)} %pad_maximum_fusion.1.mine_ref), channel_id=1, source_target_pairs={{0,17},{1,16},{2,19},{3,18},{4,21},{5,20},{6,23},{7,22},{8,25},{9,... | collective-permute-start | bytes 196616 | tf_op jit(solution)/shard_map/ppermute | solution.py:23
  20.0 0.0 copy-start.1
  20.0 0.2 convolution_multiply_fusion.gram_ref
  20.2 2.3 %collective-permute-done.4.other_ref = f32[64,256]{1,0:T(8,128)S(1)} collective-permute-done((f32[64,256]{1,0:T(8,128)S(1)}, f32[64,256]{1,0:T(8,128)S(1)}, u32[]{:S(2)}, u32[]{:S(2)}) %collective-permute-start.4) | collective-permute-done | bytes 65568 | tf_op jit(solution)/shard_map/ppermute | solution.py:23
  22.6 0.0 copy-done.1
  22.6 2.7 %shard_map.69 = (f32[16,32]{1,0:T(8,128)}, f32[16,32]{1,0:T(8,128)}) custom-call(s32[3]{0:T(128)S(1)} %pad_add_fusion.where_ref, f32[7]{0:T(128)S(1)} %copy-done.1, f32[64,256]{1,0:T(8,128)S(1)} %pad_maximum_fusion.1.mine_ref, f32[64,256]{1,0:T(8,128)S(1)} %collective-permute-done.4.other_ref, f32[256,256]{1,0:T(8,128)S(1)} %convolution_multiply_fusion.gram_ref), custom_call_target="tpu_custom_call" | custom-call | flops 100663296 | bytes 393216 | tf_op jit(solution)/shard_map/pallas_call | solution.py:152
  (19 shorter events, 0.1 us)
Async XLA Ops:
  0.6 0.7 %copy-start = (bf16[8,256]{1,0:T(8,128)(2,1)S(1)}, bf16[8,256]{1,0:T(8,128)(2,1)}, u32[]{:S(2)}) copy-start(bf16[8,256]{1,0:T(8,128)(2,1)} %student_ref.1) | copy-start | bytes 12292
  1.3 5.4 %copy-start.2 = (bf16[1024,256]{1,0:T(8,128)(2,1)S(1)}, bf16[1024,256]{1,0:T(8,128)(2,1)}, u32[]{:S(2)}) copy-start(bf16[1024,256]{1,0:T(8,128)(2,1)} %skill_hbm.1) | copy-start | bytes 1572868
  3.2 5.5 %collective-permute-start = (f32[40,256]{1,0:T(8,128)S(1)}, f32[40,256]{1,0:T(8,128)S(1)}, u32[]{:S(2)}, u32[]{:S(2)}) collective-permute-start(f32[40,256]{1,0:T(8,128)S(1)} %shard_map.68), channel_id=1, source_target_pairs={{0,9},{1,8},{2,11},{3,10},{4,13},{5,12},{6,15},{7,14},{8,1},{9,0},... | collective-permute-start | bytes 122888 | tf_op jit(solution)/shard_map/ppermute | solution.py:23
  8.7 4.1 %collective-permute-start.1 = (f32[48,256]{1,0:T(8,128)S(1)}, f32[48,256]{1,0:T(8,128)S(1)}, u32[]{:S(2)}, u32[]{:S(2)}) collective-permute-start(f32[48,256]{1,0:T(8,128)S(1)} %pad_maximum_fusion.2), channel_id=1, source_target_pairs={{0,5},{1,4},{2,7},{3,6},{4,1},{5,0},{6,3},{7,2},{8,13},{9,12},{10,... | collective-permute-start | bytes 147464 | tf_op jit(solution)/shard_map/ppermute | solution.py:23
  12.8 4.2 %collective-permute-start.2 = (f32[64,256]{1,0:T(8,128)S(1)}, f32[64,256]{1,0:T(8,128)S(1)}, u32[]{:S(2)}, u32[]{:S(2)}) collective-permute-start(f32[64,256]{1,0:T(8,128)S(1)} %pad_maximum_fusion), channel_id=1, source_target_pairs={{0,3},{1,2},{2,1},{3,0},{4,7},{5,6},{6,5},{7,4},{8,11},{9,10},{10,... | collective-permute-start | bytes 196616 | tf_op jit(solution)/shard_map/ppermute | solution.py:23
  17.0 1.4 %collective-permute-start.3 = (f32[96,256]{1,0:T(8,128)S(1)}, f32[96,256]{1,0:T(8,128)S(1)}, u32[]{:S(2)}, u32[]{:S(2)}) collective-permute-start(f32[96,256]{1,0:T(8,128)S(1)} %slice_dynamic-update-slice_fusion), channel_id=1, source_target_pairs={{0,1},{1,0},{2,3},{3,2},{4,5},{5,4},{6,7},{7,6},{8,9},{9,8},{10,11... | collective-permute-start | bytes 294920 | tf_op jit(solution)/shard_map/ppermute | solution.py:23
  17.2 1.2 %copy-start.3 = (f32[32,256]{1,0:T(8,128)S(1)}, f32[32,256]{1,0:T(8,128)}, u32[]{:S(2)}) copy-start(f32[32,256]{1,0:T(8,128)} %param.8) | copy-start | bytes 98308
  18.4 4.1 %collective-permute-start.4 = (f32[64,256]{1,0:T(8,128)S(1)}, f32[64,256]{1,0:T(8,128)S(1)}, u32[]{:S(2)}, u32[]{:S(2)}) collective-permute-start(f32[64,256]{1,0:T(8,128)S(1)} %pad_maximum_fusion.1.mine_ref), channel_id=1, source_target_pairs={{0,17},{1,16},{2,19},{3,18},{4,21},{5,20},{6,23},{7,22},{8,25},{9,... | collective-permute-start | bytes 196616 | tf_op jit(solution)/shard_map/ppermute | solution.py:23
  20.0 2.5 %copy-start.1 = (f32[7]{0:T(128)S(1)}, f32[7]{0:T(128)}, u32[]{:S(2)}) copy-start(f32[7]{0:T(128)} %coef_ref.1) | copy-start | bytes 88

commit v3 on v2

v3 whole, which is shorter than its diff:
```python
import functools

import jax
import jax.numpy as jnp
from jax import lax
from jax.experimental import pallas as pl
from jax.experimental.pallas import tpu as pltpu
from jax.sharding import PartitionSpec as P

LAGS = 7
ITERS = 3
PAD = 8
LANES = 128
VMEM_BYTES = 8 << 20


smoothing = 1.0

VMEM = pl.BlockSpec(memory_space=pltpu.VMEM)
HBM = pl.BlockSpec(memory_space=pltpu.HBM)


def exchange(block, mask):
    return lax.ppermute(block, ("day", "stu"), [(i, i ^ mask) for i in range(lax.axis_size(("day", "stu")))])


def own_part():
    place = lax.axis_index("day") ^ lax.axis_index("stu")
    for shift in (8, 4, 2, 1):
        place = place ^ (place >> shift)
    return place & 1


def split(values):
    high = values.astype(jnp.bfloat16)
    return high, (values - high.astype(jnp.float32)).astype(jnp.bfloat16)


def product(a, b):
    return jnp.dot(a, b, preferred_element_type=jnp.float32)


def student_sums(perf, skill, wide, proj, out_ref):
    students = wide.shape[0]
    total = product(perf[...], skill[...])
    days = total.shape[0] // students
    for t in range(proj.shape[0]):
        lanes = slice(t * LANES, (t + 1) * LANES)
        proj[t] = total[:, lanes]
        terms = None
        for s in range(students):
            row = proj[t, pl.ds(s, days, stride=students), :] * wide[s : s + 1, lanes]
            terms = row if terms is None else terms + row
        out_ref[:days, lanes] = terms


def send_kernel(perf_hbm, skill_hbm, student_hbm, send_ref, skill, keep, student, perf, proj, sems):
    rows = perf.shape[0]
    part = own_part()
    away = perf_hbm.at[pl.ds(pl.multiple_of((1 - part) * rows, rows), rows)]
    home = perf_hbm.at[pl.ds(pl.multiple_of(part * rows, rows), rows)]
    copies = []
    for i, (source, target) in enumerate(
        ((student_hbm, student), (skill_hbm, skill), (away, perf), (home, keep))
    ):
        copies.append(pltpu.make_async_copy(source, target, sems.at[i]))
        copies[i].start()
    for copy in copies[:3]:
        copy.wait()
    student_sums(perf, skill, student[...].astype(jnp.float32), proj, send_ref)
    copies[3].wait()


def send_part(performance, student_factor, skill_factor):
    days, students, skills = performance.shape
    rank = skill_factor.shape[1]
    rows = days * students // 2
    operands = performance.reshape(2 * rows, skills), skill_factor, student_factor
    return pl.pallas_call(
        send_kernel,
        compiler_params=pltpu.CompilerParams(vmem_limit_bytes=VMEM_BYTES),
        out_shape=(
            jax.ShapeDtypeStruct((days // 2, rank), jnp.float32),
            jax.ShapeDtypeStruct((skills, rank), jnp.bfloat16),
            jax.ShapeDtypeStruct((rows, skills), jnp.bfloat16),
            jax.ShapeDtypeStruct((students, rank), jnp.bfloat16),
        ),
        in_specs=[HBM] * 3,
        out_specs=(VMEM,) * 4,
        scratch_shapes=[
            pltpu.VMEM((rows, skills), jnp.bfloat16),
            pltpu.VMEM((rank // LANES, rows, LANES), jnp.float32),
            pltpu.SemaphoreType.DMA((4,)),
        ],
        cost_estimate=pl.CostEstimate(
            flops=2 * rows * skills * rank, bytes_accessed=2 * (2 * rows + rank) * skills, transcendentals=0
        ),
    )(*(pltpu.with_memory_space_constraint(x, pltpu.HBM) for x in operands))


def keep_kernel(perf, skill, student, keep_ref, proj):
    wide = student[...].astype(jnp.float32)
    student_sums(perf, skill, wide, proj, keep_ref)
    keep_ref[-wide.shape[0] :, :] = wide


def keep_part(perf, skill, student):
    rows, skills = perf.shape
    students, rank = student.shape
    return pl.pallas_call(
        keep_kernel,
        compiler_params=pltpu.CompilerParams(vmem_limit_bytes=VMEM_BYTES),
        out_shape=jax.ShapeDtypeStruct((rows // students + students, rank), jnp.float32),
        in_specs=[VMEM] * 3,
        out_specs=VMEM,
        scratch_shapes=[pltpu.VMEM((rank // LANES, rows, LANES), jnp.float32)],
        cost_estimate=pl.CostEstimate(
            flops=2 * rows * skills * rank, bytes_accessed=2 * (rows + rank) * skills, transcendentals=0
        ),
    )(perf, skill, student)


def cg_kernel(
    columns, coef_ref, prev_ref, mine_ref, other_ref, skill_gram_ref, factor_hbm, residual_hbm,
    mttkrp, values, low, high, block, results, sems,
):
    days, width = prev_ref.shape
    total = mttkrp.shape[0]
    blocks, half = total // days, days // 2
    day, stu, part = lax.axis_index("day"), lax.axis_index("stu"), own_part()
    values[pl.ds(pl.multiple_of(day * days, days), days), :] = prev_ref[...]
    for source, at in ((mine_ref, part), (other_ref, 1 - part)):
        for b in range(blocks):
            place = pl.ds(pl.multiple_of((day ^ b) * days + at * half, half), half)
            mttkrp[place, :] = source[b * half : (b + 1) * half, :]
            if b > 0:
                row = (blocks + b - 1) * half
                values[place, :] = source[row : row + half, :]
    start = (2 * blocks - 1) * half
    students = jnp.concatenate([mine_ref[start:, :], other_ref[start:, :]], 0).astype(jnp.bfloat16)
    student_gram = lax.dot_general(
        students, students, (((0,), (0,)), ((), ())), preferred_element_type=jnp.float32
    )
    gram_high, gram_low = split(student_gram * skill_gram_ref[...])
    gram = jnp.concatenate([gram_high, gram_high, gram_low], 0)
    low[:PAD, :] = jnp.zeros((PAD, width), jnp.float32)
    high[pl.ds(total, PAD), :] = jnp.zeros((PAD, width), jnp.float32)
    coef = [coef_ref[:, l : l + 1] for l in range(LAGS)]

    def operate(v):
        v_high, v_low = split(v)
        mixed = product(jnp.concatenate([v_high, v_low, v_high], 1), gram)
        low[pl.ds(PAD, total), :] = v
        ahead = v
        for lag in range(1, LAGS + 1):
            ahead = ahead - coef[lag - 1] * low[pl.ds(PAD - lag, total), :]
        high[:total, :] = ahead
        back = ahead
        for lag in range(1, LAGS + 1):
            back = back - coef[lag - 1] * high[pl.ds(lag, total), :]
        return mixed + smoothing * back

    def inner(a, b):
        return jnp.sum(jnp.sum(a * b, axis=0, keepdims=True), axis=1, keepdims=True)

    factor = values[...]
    residual = mttkrp[...] - operate(factor)
    direction = residual
    now = inner(residual, residual)
    for step in range(ITERS):
        image = operate(direction)
        alpha = now / inner(direction, image)
        factor = factor + alpha * direction
        residual = residual - alpha * image
        if step < ITERS - 1:
            following = inner(residual, residual)
            direction = residual + (following / now) * direction
            now = following
    start = pl.multiple_of(day * days, days)
    turn = jnp.where(stu == 0, 0, width - stu * columns)
    copies = []
    for i, (result, target) in enumerate(((factor, factor_hbm), (residual, residual_hbm))):
        block[i] = result
        rows = block[i, pl.ds(start, days), :]
        results[i] = pltpu.roll(rows, turn, axis=1)[:, :columns].T
        copies.append(pltpu.make_async_copy(results.at[i], target, sems.at[i]))
        copies[i].start()
    for copy in copies:
        copy.wait()


def conjugate(coef, prev, mine, other, skill_gram, blocks, columns):
    days, width = prev.shape
    total = days * blocks
    shape = jax.ShapeDtypeStruct((columns, days), jnp.float32)
    return pl.pallas_call(
        functools.partial(cg_kernel, columns),
        compiler_params=pltpu.CompilerParams(vmem_limit_bytes=VMEM_BYTES),
        out_shape=(shape, shape),
        in_specs=[VMEM] * 5,
        out_specs=(HBM, HBM),
        scratch_shapes=[
            pltpu.VMEM((total, width), jnp.float32),
            pltpu.VMEM((total, width), jnp.float32),
            pltpu.VMEM((total + PAD, width), jnp.float32),
            pltpu.VMEM((total + PAD, width), jnp.float32),
            pltpu.VMEM((2, total, width), jnp.float32),
            pltpu.VMEM((2, columns, days), jnp.float32),
            pltpu.SemaphoreType.DMA((2,)),
        ],
        cost_estimate=pl.CostEstimate(
            flops=24 * total * width * width, bytes_accessed=4 * width * (width + 2 * total), transcendentals=0
        ),
    )(coef.reshape(1, LAGS), prev, mine, other, skill_gram)


def bits_of(count):
    assert count & (count - 1) == 0 and count > 1
    return [1 << b for b in range(count.bit_length() - 1)]


def local(performance, student_factor, skill_factor, day_prev, ar_coef):
    days = performance.shape[0]
    half = days // 2
    rank = skill_factor.shape[1]
    stu_size, day_size = lax.axis_size("stu"), lax.axis_size("day")
    send, skill, perf, student = send_part(performance, student_factor, skill_factor)
    got = exchange(send, 1)
    keep = keep_part(perf, skill, student)
    skill_gram = lax.dot_general(skill, skill, (((0,), (0,)), ((), ())), preferred_element_type=jnp.float32)
    payload = jnp.concatenate([keep[:half] + got, keep[half:]], 0)
    for bit in bits_of(stu_size)[:0:-1]:
        got = exchange(payload, bit | 1)
        payload = jnp.concatenate([payload[:half] + got[:half], payload[half:], got[half:]], 0)
    mttkrp, students = payload[:half], payload[half:]
    factor = lax.dynamic_slice_in_dim(day_prev, own_part() * half, half, 0)
    for bit in bits_of(day_size):
        got = exchange(jnp.concatenate([mttkrp, factor], 0), bit * stu_size + 1)
        rows = bit * half
        mttkrp = jnp.concatenate([mttkrp, got[:rows]], 0)
        factor = jnp.concatenate([factor, got[rows:]], 0)
    mine = jnp.concatenate([mttkrp, factor[half:], students], 0)
    other = exchange(mine, 1)
    factor, residual = conjugate(ar_coef, day_prev, mine, other, skill_gram, day_size, rank // stu_size)
    return factor.T, residual.T


def solution(mesh):
    return jax.shard_map(
        local,
        mesh=mesh,
        in_specs=(P("day", "stu", None), P("stu", None), P(), P("day", None), P()),
        out_specs=(P("day", "stu"), P("day", "stu")),
        check_vma=False,
    )
```

time: 25.6 us -> 23.3 us (0.910)
  waiting for transfers between devices: 9.6 us -> 8.01 us
  starting transfers between devices: 8.98 us -> 9.86 us
  local copies, waits for them, and re-layouts: 0.73 us -> 0.06 us
  Pallas kernels: 4.57 us -> 4.08 us
    ppermute x5 -> x6, waiting for transfers between devices: 9.6 us -> 8.01 us  [exchange(): lax.ppermute(block, ('day', 'stu'), [(i, i ^ mask) for i in range(lax.axi...]
    ppermute x5 -> x6, starting transfers between devices: 8.98 us -> 9.86 us  [exchange(): lax.ppermute(block, ('day', 'stu'), [(i, i ^ mask) for i in range(lax.axi...]
    unnamed x15 -> x8, local copies, waits for them, and re-layouts: 0.71 us -> 0.05 us
    pallas_call x2 -> x3, Pallas kernels: 4.57 us -> 4.08 us  [the longest x1 2.41 us: conjugate(): pl.pallas_call(functools.partial(cg_kernel, columns), compiler_params=plt...]
    dot_general x2 -> x1, matrix products: 0.55 us -> 0.33 us  [local(): lax.dot_general(skill, skill, (((0,), (0,)), ((), ())), preferred_element...]
  transfers between devices with their start and end apart: 5 -> 6, of which waited for: 5 -> 6; matrix products, arithmetic and copies ran while one was open for 3% -> 1% of each run, Pallas kernels for 0% -> 1%
where the time goes in v3:
time: 23.3 us; the launch traced here: 23.1 us
  starting transfers between devices  9.86 us (42%)
  waiting for transfers between devices  8.01 us (34%)
  Pallas kernels  4.08 us (18%)
  between operations  0.7 us (3%)
  matrix products  0.33 us (1%)
    ppermute x6, starting transfers between devices, exchange(): lax.ppermute(block, ('day', 'stu'), [(i, i ^ mask) for i in range(lax.axi...  9.86 us
    ppermute x6, waiting for transfers between devices, exchange(): lax.ppermute(block, ('day', 'stu'), [(i, i ^ mask) for i in range(lax.axi...  8.01 us
    pallas_call x1, Pallas kernels, conjugate(): pl.pallas_call(functools.partial(cg_kernel, columns), compiler_params=plt...  2.41 us
    pallas_call x1, Pallas kernels, send_part(): pl.pallas_call(send_kernel, compiler_params=pltpu.CompilerParams(vmem_lim...  1.42 us
  transfers between devices with their start and end apart: 6, of which 6 were waited for; matrix products, arithmetic and copies ran while one was open for 1% of the time, Pallas kernels for 1%

profile of v3, /device:TPU:0, one launch (start us, length us, event | category | flops | bytes accessed | tf_op | source)
XLA Modules:
  0.0 23.1 jit_solution(14058486872630472888)
XLA Ops:
  0.6 1.4 %shard_map.68 = (f32[16,256]{1,0:T(8,128)S(1)}, bf16[1024,256]{1,0:T(8,128)(2,1)S(1)}, bf16[128,1024]{1,0:T(8,128)(2,1)S(1)}, bf16[8,256]{1,0:T(8,128)(2,1)S(1)}) custom-call(bf16[256,1024]{1,0:T(8,128)(2,1)} %bitcast.7, bf16[1024,256]{1,0:T(8,128)(2,1)} %skill_hbm.1, bf16[8,256]{1,0:T(8,128)(2,1)} %student_hbm.1), custom_call_target="tpu_custom_call" | custom-call | flops 67108864 | bytes 1048576 | tf_op jit(solution)/shard_map/pallas_call | solution.py:79
  2.1 0.5 %collective-permute-start = (f32[16,256]{1,0:T(8,128)S(1)}, f32[16,256]{1,0:T(8,128)S(1)}, u32[]{:S(2)}, u32[]{:S(2)}) collective-permute-start(f32[16,256]{1,0:T(8,128)S(1)} %get-tuple-element.11), channel_id=1, source_target_pairs={{0,1},{1,0},{2,3},{3,2},{4,5},{5,4},{6,7},{7,6},{8,9},{9,8},{10,11... | collective-permute-start | bytes 49160 | tf_op jit(solution)/shard_map/ppermute | solution.py:24
  2.6 0.3 %shard_map.69 = f32[24,256]{1,0:T(8,128)S(1)} custom-call(bf16[128,1024]{1,0:T(8,128)(2,1)S(1)} %get-tuple-element.8.perf, bf16[1024,256]{1,0:T(8,128)(2,1)S(1)} %get-tuple-element.9.skill, bf16[8,256]{1,0:T(8,128)(2,1)S(1)} %get-tuple-element.10.student), custom_call_target="tpu_custom_call" | custom-call | flops 67108864 | bytes 786432 | tf_op jit(solution)/shard_map/pallas_call | solution.py:110
  2.8 0.6 %collective-permute-done = f32[16,256]{1,0:T(8,128)S(1)} collective-permute-done((f32[16,256]{1,0:T(8,128)S(1)}, f32[16,256]{1,0:T(8,128)S(1)}, u32[]{:S(2)}, u32[]{:S(2)}) %collective-permute-start) | collective-permute-done | bytes 16416 | tf_op jit(solution)/shard_map/ppermute | solution.py:24
  3.4 3.7 %collective-permute-start.1 = (f32[24,256]{1,0:T(8,128)S(1)}, f32[24,256]{1,0:T(8,128)S(1)}, u32[]{:S(2)}, u32[]{:S(2)}) collective-permute-start(f32[24,256]{1,0:T(8,128)S(1)} %pad_maximum_fusion.3), channel_id=1, source_target_pairs={{0,9},{1,8},{2,11},{3,10},{4,13},{5,12},{6,15},{7,14},{8,1},{9,0},... | collective-permute-start | bytes 73736 | tf_op jit(solution)/shard_map/ppermute | solution.py:24
  7.1 1.5 %collective-permute-done.1 = f32[24,256]{1,0:T(8,128)S(1)} collective-permute-done((f32[24,256]{1,0:T(8,128)S(1)}, f32[24,256]{1,0:T(8,128)S(1)}, u32[]{:S(2)}, u32[]{:S(2)}) %collective-permute-start.1) | collective-permute-done | bytes 24608 | tf_op jit(solution)/shard_map/ppermute | solution.py:24
  8.7 1.7 %collective-permute-start.2 = (f32[32,256]{1,0:T(8,128)S(1)}, f32[32,256]{1,0:T(8,128)S(1)}, u32[]{:S(2)}, u32[]{:S(2)}) collective-permute-start(f32[32,256]{1,0:T(8,128)S(1)} %pad_maximum_fusion.1), channel_id=1, source_target_pairs={{0,5},{1,4},{2,7},{3,6},{4,1},{5,0},{6,3},{7,2},{8,13},{9,12},{10,... | collective-permute-start | bytes 98312 | tf_op jit(solution)/shard_map/ppermute | solution.py:24
  10.4 1.7 %collective-permute-done.2 = f32[32,256]{1,0:T(8,128)S(1)} collective-permute-done((f32[32,256]{1,0:T(8,128)S(1)}, f32[32,256]{1,0:T(8,128)S(1)}, u32[]{:S(2)}, u32[]{:S(2)}) %collective-permute-start.2) | collective-permute-done | bytes 32800 | tf_op jit(solution)/shard_map/ppermute | solution.py:24
  12.1 0.0 copy-start
  12.1 1.6 %collective-permute-start.3 = (f32[48,256]{1,0:T(8,128)S(1)}, f32[48,256]{1,0:T(8,128)S(1)}, u32[]{:S(2)}, u32[]{:S(2)}) collective-permute-start(f32[48,256]{1,0:T(8,128)S(1)} %pad_maximum_fusion), channel_id=1, source_target_pairs={{0,3},{1,2},{2,1},{3,0},{4,7},{5,6},{6,5},{7,4},{8,11},{9,10},{10,... | collective-permute-start | bytes 147464 | tf_op jit(solution)/shard_map/ppermute | solution.py:24
  13.7 0.0 copy-done
  13.8 2.0 %collective-permute-done.3 = f32[48,256]{1,0:T(8,128)S(1)} collective-permute-done((f32[48,256]{1,0:T(8,128)S(1)}, f32[48,256]{1,0:T(8,128)S(1)}, u32[]{:S(2)}, u32[]{:S(2)}) %collective-permute-start.3) | collective-permute-done | bytes 49184 | tf_op jit(solution)/shard_map/ppermute | solution.py:24
  15.7 1.9 %collective-permute-start.4 = (f32[32,256]{1,0:T(8,128)S(1)}, f32[32,256]{1,0:T(8,128)S(1)}, u32[]{:S(2)}, u32[]{:S(2)}) collective-permute-start(f32[32,256]{1,0:T(8,128)S(1)} %pad_maximum_fusion.2), channel_id=1, source_target_pairs={{0,17},{1,16},{2,19},{3,18},{4,21},{5,20},{6,23},{7,22},{8,25},{9,... | collective-permute-start | bytes 98312 | tf_op jit(solution)/shard_map/ppermute | solution.py:24
  17.6 1.6 %collective-permute-done.4 = f32[32,256]{1,0:T(8,128)S(1)} collective-permute-done((f32[32,256]{1,0:T(8,128)S(1)}, f32[32,256]{1,0:T(8,128)S(1)}, u32[]{:S(2)}, u32[]{:S(2)}) %collective-permute-start.4) | collective-permute-done | bytes 32800 | tf_op jit(solution)/shard_map/ppermute | solution.py:24
  19.2 0.4 %collective-permute-start.5 = (f32[112,256]{1,0:T(8,128)S(1)}, f32[112,256]{1,0:T(8,128)S(1)}, u32[]{:S(2)}, u32[]{:S(2)}) collective-permute-start(f32[112,256]{1,0:T(8,128)S(1)} %slice_dynamic-update-slice_fusion.mine_ref), channel_id=1, source_target_pairs={{0,1},{1,0},{2,3},{3,2},{4,5},{5,4},{6,7},{7,6},{8,9},{9,8},{10,11... | collective-permute-start | bytes 344072 | tf_op jit(solution)/shard_map/ppermute | solution.py:24
  19.7 0.3 %fusion.1.skill_gram_ref = f32[256,256]{1,0:T(8,128)S(1)} fusion(bf16[1024,256]{1,0:T(8,128)(2,1)S(1)} %get-tuple-element.9.skill), kind=kOutput, calls=%fused_computation.16 | convolution fusion | flops 134217728 | bytes 786432 | tf_op jit(solution)/shard_map/dot_general | solution.py:230
  20.0 0.0 copy-start.1
  20.0 0.6 %collective-permute-done.5.other_ref = f32[112,256]{1,0:T(8,128)S(1)} collective-permute-done((f32[112,256]{1,0:T(8,128)S(1)}, f32[112,256]{1,0:T(8,128)S(1)}, u32[]{:S(2)}, u32[]{:S(2)}) %collective-permute-start.5) | collective-permute-done | bytes 114720 | tf_op jit(solution)/shard_map/ppermute | solution.py:24
  20.6 0.0 copy-done.1
  20.7 2.4 %shard_map.70 = (f32[16,32]{1,0:T(8,128)}, f32[16,32]{1,0:T(8,128)}) custom-call(f32[1,7]{1,0:T(1,128)S(1)} %bitcast.6, f32[32,256]{1,0:T(8,128)S(1)} %copy-done, f32[112,256]{1,0:T(8,128)S(1)} %slice_dynamic-update-slice_fusion.mine_ref, f32[112,256]{1,0:T(8,128)S(1)} %collective-permute-done.5.other_ref, f32[256,256]{1,0:T(8,128)S(1)} %fusion.1.skill_gram_ref), custom_call_target="tpu_custom_call" | custom-call | flops 100663296 | bytes 393216 | tf_op jit(solution)/shard_map/pallas_call | solution.py:196
  (16 shorter events, 0.1 us)
Async XLA Ops:
  2.1 1.4 %collective-permute-start = (f32[16,256]{1,0:T(8,128)S(1)}, f32[16,256]{1,0:T(8,128)S(1)}, u32[]{:S(2)}, u32[]{:S(2)}) collective-permute-start(f32[16,256]{1,0:T(8,128)S(1)} %get-tuple-element.11), channel_id=1, source_target_pairs={{0,1},{1,0},{2,3},{3,2},{4,5},{5,4},{6,7},{7,6},{8,9},{9,8},{10,11... | collective-permute-start | bytes 49160 | tf_op jit(solution)/shard_map/ppermute | solution.py:24
  3.4 5.2 %collective-permute-start.1 = (f32[24,256]{1,0:T(8,128)S(1)}, f32[24,256]{1,0:T(8,128)S(1)}, u32[]{:S(2)}, u32[]{:S(2)}) collective-permute-start(f32[24,256]{1,0:T(8,128)S(1)} %pad_maximum_fusion.3), channel_id=1, source_target_pairs={{0,9},{1,8},{2,11},{3,10},{4,13},{5,12},{6,15},{7,14},{8,1},{9,0},... | collective-permute-start | bytes 73736 | tf_op jit(solution)/shard_map/ppermute | solution.py:24
  8.7 3.4 %collective-permute-start.2 = (f32[32,256]{1,0:T(8,128)S(1)}, f32[32,256]{1,0:T(8,128)S(1)}, u32[]{:S(2)}, u32[]{:S(2)}) collective-permute-start(f32[32,256]{1,0:T(8,128)S(1)} %pad_maximum_fusion.1), channel_id=1, source_target_pairs={{0,5},{1,4},{2,7},{3,6},{4,1},{5,0},{6,3},{7,2},{8,13},{9,12},{10,... | collective-permute-start | bytes 98312 | tf_op jit(solution)/shard_map/ppermute | solution.py:24
  12.1 1.6 %copy-start = (f32[32,256]{1,0:T(8,128)S(1)}, f32[32,256]{1,0:T(8,128)}, u32[]{:S(2)}) copy-start(f32[32,256]{1,0:T(8,128)} %prev_ref.1) | copy-start | bytes 98308
  12.1 3.6 %collective-permute-start.3 = (f32[48,256]{1,0:T(8,128)S(1)}, f32[48,256]{1,0:T(8,128)S(1)}, u32[]{:S(2)}, u32[]{:S(2)}) collective-permute-start(f32[48,256]{1,0:T(8,128)S(1)} %pad_maximum_fusion), channel_id=1, source_target_pairs={{0,3},{1,2},{2,1},{3,0},{4,7},{5,6},{6,5},{7,4},{8,11},{9,10},{10,... | collective-permute-start | bytes 147464 | tf_op jit(solution)/shard_map/ppermute | solution.py:24
  15.7 3.5 %collective-permute-start.4 = (f32[32,256]{1,0:T(8,128)S(1)}, f32[32,256]{1,0:T(8,128)S(1)}, u32[]{:S(2)}, u32[]{:S(2)}) collective-permute-start(f32[32,256]{1,0:T(8,128)S(1)} %pad_maximum_fusion.2), channel_id=1, source_target_pairs={{0,17},{1,16},{2,19},{3,18},{4,21},{5,20},{6,23},{7,22},{8,25},{9,... | collective-permute-start | bytes 98312 | tf_op jit(solution)/shard_map/ppermute | solution.py:24
  19.2 1.4 %collective-permute-start.5 = (f32[112,256]{1,0:T(8,128)S(1)}, f32[112,256]{1,0:T(8,128)S(1)}, u32[]{:S(2)}, u32[]{:S(2)}) collective-permute-start(f32[112,256]{1,0:T(8,128)S(1)} %slice_dynamic-update-slice_fusion.mine_ref), channel_id=1, source_target_pairs={{0,1},{1,0},{2,3},{3,2},{4,5},{5,4},{6,7},{7,6},{8,9},{9,8},{10,11... | collective-permute-start | bytes 344072 | tf_op jit(solution)/shard_map/ppermute | solution.py:24
  20.0 0.7 %copy-start.1 = (f32[7]{0:T(128)S(1)}, f32[7]{0:T(128)}, u32[]{:S(2)}) copy-start(f32[7]{0:T(128)} %param.9) | copy-start | bytes 88

commit v4 on v3

--- a/solution.py
+++ b/solution.py
@@ -20,8 +20,11 @@
 HBM = pl.BlockSpec(memory_space=pltpu.HBM)
 
 
-def exchange(block, mask):
-    return lax.ppermute(block, ("day", "stu"), [(i, i ^ mask) for i in range(lax.axis_size(("day", "stu")))])
+def exchange(block, mask, other=None):
+    both = mask, mask if other is None else other
+    union = both[0] | both[1]
+    route = [(i, i ^ both[(i & union).bit_count() % 2]) for i in range(lax.axis_size(("day", "stu")))]
+    return lax.ppermute(block, ("day", "stu"), route)
 
 
 def own_part():
@@ -161,20 +164,27 @@
         return mixed + smoothing * back
 
     def inner(a, b):
-        return jnp.sum(jnp.sum(a * b, axis=0, keepdims=True), axis=1, keepdims=True)
+        terms = a * b
+        tiles = [
+            terms[i : i + PAD, j : j + LANES] for i in range(0, total, PAD) for j in range(0, width, LANES)
+        ]
+        while len(tiles) > 1:
+            tiles = [x + y for x, y in zip(tiles[::2], tiles[1::2], strict=True)]
+        return jnp.sum(jnp.sum(tiles[0], axis=1, keepdims=True), axis=0, keepdims=True)
 
     factor = values[...]
     residual = mttkrp[...] - operate(factor)
-    direction = residual
+    direction, image = residual, operate(residual)
     now = inner(residual, residual)
     for step in range(ITERS):
-        image = operate(direction)
         alpha = now / inner(direction, image)
         factor = factor + alpha * direction
         residual = residual - alpha * image
         if step < ITERS - 1:
-            following = inner(residual, residual)
-            direction = residual + (following / now) * direction
+            ahead, following = operate(residual), inner(residual, residual)
+            beta = following / now
+            direction = residual + beta * direction
+            image = ahead + beta * image
             now = following
     start = pl.multiple_of(day * days, days)
     turn = jnp.where(stu == 0, 0, width - stu * columns)
@@ -229,8 +239,9 @@
     keep = keep_part(perf, skill, student)
     skill_gram = lax.dot_general(skill, skill, (((0,), (0,)), ((), ())), preferred_element_type=jnp.float32)
     payload = jnp.concatenate([keep[:half] + got, keep[half:]], 0)
-    for bit in bits_of(stu_size)[:0:-1]:
-        got = exchange(payload, bit | 1)
+    masks = [bit | 1 for bit in bits_of(stu_size)[:0:-1]]
+    for mask, other in zip(masks, masks[:-2] + masks[:-3:-1], strict=True):
+        got = exchange(payload, mask, other)
         payload = jnp.concatenate([payload[:half] + got[:half], payload[half:], got[half:]], 0)
     mttkrp, students = payload[:half], payload[half:]
     factor = lax.dynamic_slice_in_dim(day_prev, own_part() * half, half, 0)

time: 23.3 us -> 23.1 us (level)
  starting transfers between devices: 9.86 us -> 9.57 us
    ppermute x6, starting transfers between devices: 9.86 us -> 9.57 us  [exchange(): return lax.ppermute(block, ('day', 'stu'), route)]
where the time goes in v4:
time: 23.1 us; the launch traced here: 22.9 us
  starting transfers between devices  9.57 us (41%)
  waiting for transfers between devices  8.2 us (35%)
  Pallas kernels  3.97 us (17%)
  between operations  0.7 us (3%)
  matrix products  0.34 us (1%)
    ppermute x6, starting transfers between devices, exchange(): return lax.ppermute(block, ('day', 'stu'), route)  9.57 us
    ppermute x6, waiting for transfers between devices, exchange(): return lax.ppermute(block, ('day', 'stu'), route)  8.2 us
    pallas_call x1, Pallas kernels, conjugate(): pl.pallas_call(functools.partial(cg_kernel, columns), compiler_params=plt...  2.31 us
    pallas_call x1, Pallas kernels, send_part(): pl.pallas_call(send_kernel, compiler_params=pltpu.CompilerParams(vmem_lim...  1.42 us
  transfers between devices with their start and end apart: 6, of which 6 were waited for; matrix products, arithmetic and copies ran while one was open for 1% of the time, Pallas kernels for 1%

profile of v4, /device:TPU:0, one launch (start us, length us, event | category | flops | bytes accessed | tf_op | source)
XLA Modules:
  0.0 22.9 jit_solution(13741419753535728463)
XLA Ops:
  0.6 1.4 %shard_map.68 = (f32[16,256]{1,0:T(8,128)S(1)}, bf16[1024,256]{1,0:T(8,128)(2,1)S(1)}, bf16[128,1024]{1,0:T(8,128)(2,1)S(1)}, bf16[8,256]{1,0:T(8,128)(2,1)S(1)}) custom-call(bf16[256,1024]{1,0:T(8,128)(2,1)} %bitcast.7, bf16[1024,256]{1,0:T(8,128)(2,1)} %skill_hbm.1, bf16[8,256]{1,0:T(8,128)(2,1)} %student_hbm.1), custom_call_target="tpu_custom_call" | custom-call | flops 67108864 | bytes 1048576 | tf_op jit(solution)/shard_map/pallas_call | solution.py:82
  2.1 0.5 %collective-permute-start = (f32[16,256]{1,0:T(8,128)S(1)}, f32[16,256]{1,0:T(8,128)S(1)}, u32[]{:S(2)}, u32[]{:S(2)}) collective-permute-start(f32[16,256]{1,0:T(8,128)S(1)} %get-tuple-element.11), channel_id=1, source_target_pairs={{0,1},{1,0},{2,3},{3,2},{4,5},{5,4},{6,7},{7,6},{8,9},{9,8},{10,11... | collective-permute-start | bytes 49160 | tf_op jit(solution)/shard_map/ppermute | solution.py:27
  2.6 0.3 %shard_map.69 = f32[24,256]{1,0:T(8,128)S(1)} custom-call(bf16[128,1024]{1,0:T(8,128)(2,1)S(1)} %get-tuple-element.8.perf, bf16[1024,256]{1,0:T(8,128)(2,1)S(1)} %get-tuple-element.9.skill, bf16[8,256]{1,0:T(8,128)(2,1)S(1)} %get-tuple-element.10.student), custom_call_target="tpu_custom_call" | custom-call | flops 67108864 | bytes 786432 | tf_op jit(solution)/shard_map/pallas_call | solution.py:113
  2.8 0.6 %collective-permute-done = f32[16,256]{1,0:T(8,128)S(1)} collective-permute-done((f32[16,256]{1,0:T(8,128)S(1)}, f32[16,256]{1,0:T(8,128)S(1)}, u32[]{:S(2)}, u32[]{:S(2)}) %collective-permute-start) | collective-permute-done | bytes 16416 | tf_op jit(solution)/shard_map/ppermute | solution.py:27
  3.4 3.7 %collective-permute-start.1 = (f32[24,256]{1,0:T(8,128)S(1)}, f32[24,256]{1,0:T(8,128)S(1)}, u32[]{:S(2)}, u32[]{:S(2)}) collective-permute-start(f32[24,256]{1,0:T(8,128)S(1)} %pad_maximum_fusion.3), channel_id=1, source_target_pairs={{0,9},{1,8},{2,11},{3,10},{4,13},{5,12},{6,15},{7,14},{8,1},{9,0},... | collective-permute-start | bytes 73736 | tf_op jit(solution)/shard_map/ppermute | solution.py:27
  7.1 1.5 %collective-permute-done.1 = f32[24,256]{1,0:T(8,128)S(1)} collective-permute-done((f32[24,256]{1,0:T(8,128)S(1)}, f32[24,256]{1,0:T(8,128)S(1)}, u32[]{:S(2)}, u32[]{:S(2)}) %collective-permute-start.1) | collective-permute-done | bytes 24608 | tf_op jit(solution)/shard_map/ppermute | solution.py:27
  8.7 1.7 %collective-permute-start.2 = (f32[32,256]{1,0:T(8,128)S(1)}, f32[32,256]{1,0:T(8,128)S(1)}, u32[]{:S(2)}, u32[]{:S(2)}) collective-permute-start(f32[32,256]{1,0:T(8,128)S(1)} %pad_maximum_fusion.1), channel_id=1, source_target_pairs={{0,5},{1,2},{2,1},{3,6},{4,7},{5,0},{6,3},{7,4},{8,13},{9,10},{10,... | collective-permute-start | bytes 98312 | tf_op jit(solution)/shard_map/ppermute | solution.py:27
  10.4 1.7 %collective-permute-done.2 = f32[32,256]{1,0:T(8,128)S(1)} collective-permute-done((f32[32,256]{1,0:T(8,128)S(1)}, f32[32,256]{1,0:T(8,128)S(1)}, u32[]{:S(2)}, u32[]{:S(2)}) %collective-permute-start.2) | collective-permute-done | bytes 32800 | tf_op jit(solution)/shard_map/ppermute | solution.py:27
  12.1 0.0 copy-start
  12.1 1.6 %collective-permute-start.3 = (f32[48,256]{1,0:T(8,128)S(1)}, f32[48,256]{1,0:T(8,128)S(1)}, u32[]{:S(2)}, u32[]{:S(2)}) collective-permute-start(f32[48,256]{1,0:T(8,128)S(1)} %pad_maximum_fusion), channel_id=1, source_target_pairs={{0,3},{1,4},{2,7},{3,0},{4,1},{5,6},{6,5},{7,2},{8,11},{9,12},{10,... | collective-permute-start | bytes 147464 | tf_op jit(solution)/shard_map/ppermute | solution.py:27
  13.7 0.0 copy-done
  13.7 2.0 %collective-permute-done.3 = f32[48,256]{1,0:T(8,128)S(1)} collective-permute-done((f32[48,256]{1,0:T(8,128)S(1)}, f32[48,256]{1,0:T(8,128)S(1)}, u32[]{:S(2)}, u32[]{:S(2)}) %collective-permute-start.3) | collective-permute-done | bytes 49184 | tf_op jit(solution)/shard_map/ppermute | solution.py:27
  15.7 1.6 %collective-permute-start.4 = (f32[32,256]{1,0:T(8,128)S(1)}, f32[32,256]{1,0:T(8,128)S(1)}, u32[]{:S(2)}, u32[]{:S(2)}) collective-permute-start(f32[32,256]{1,0:T(8,128)S(1)} %pad_maximum_fusion.2), channel_id=1, source_target_pairs={{0,17},{1,16},{2,19},{3,18},{4,21},{5,20},{6,23},{7,22},{8,25},{9,... | collective-permute-start | bytes 98312 | tf_op jit(solution)/shard_map/ppermute | solution.py:27
  17.3 1.8 %collective-permute-done.4 = f32[32,256]{1,0:T(8,128)S(1)} collective-permute-done((f32[32,256]{1,0:T(8,128)S(1)}, f32[32,256]{1,0:T(8,128)S(1)}, u32[]{:S(2)}, u32[]{:S(2)}) %collective-permute-start.4) | collective-permute-done | bytes 32800 | tf_op jit(solution)/shard_map/ppermute | solution.py:27
  19.2 0.4 %collective-permute-start.5 = (f32[112,256]{1,0:T(8,128)S(1)}, f32[112,256]{1,0:T(8,128)S(1)}, u32[]{:S(2)}, u32[]{:S(2)}) collective-permute-start(f32[112,256]{1,0:T(8,128)S(1)} %slice_dynamic-update-slice_fusion.mine_ref), channel_id=1, source_target_pairs={{0,1},{1,0},{2,3},{3,2},{4,5},{5,4},{6,7},{7,6},{8,9},{9,8},{10,11... | collective-permute-start | bytes 344072 | tf_op jit(solution)/shard_map/ppermute | solution.py:27
  19.6 0.3 %fusion.1.skill_gram_ref = f32[256,256]{1,0:T(8,128)S(1)} fusion(bf16[1024,256]{1,0:T(8,128)(2,1)S(1)} %get-tuple-element.9.skill), kind=kOutput, calls=%fused_computation.16 | convolution fusion | flops 134217728 | bytes 786432 | tf_op jit(solution)/shard_map/dot_general | solution.py:240
  19.9 0.0 copy-start.1
  19.9 0.6 %collective-permute-done.5.other_ref = f32[112,256]{1,0:T(8,128)S(1)} collective-permute-done((f32[112,256]{1,0:T(8,128)S(1)}, f32[112,256]{1,0:T(8,128)S(1)}, u32[]{:S(2)}, u32[]{:S(2)}) %collective-permute-start.5) | collective-permute-done | bytes 114720 | tf_op jit(solution)/shard_map/ppermute | solution.py:27
  20.5 0.0 copy-done.1
  20.6 2.3 %shard_map.70 = (f32[16,32]{1,0:T(8,128)}, f32[16,32]{1,0:T(8,128)}) custom-call(f32[1,7]{1,0:T(1,128)S(1)} %bitcast.6, f32[32,256]{1,0:T(8,128)S(1)} %copy-done, f32[112,256]{1,0:T(8,128)S(1)} %slice_dynamic-update-slice_fusion.mine_ref, f32[112,256]{1,0:T(8,128)S(1)} %collective-permute-done.5.other_ref, f32[256,256]{1,0:T(8,128)S(1)} %fusion.1.skill_gram_ref), custom_call_target="tpu_custom_call" | custom-call | flops 100663296 | bytes 393216 | tf_op jit(solution)/shard_map/pallas_call | solution.py:206
  (16 shorter events, 0.1 us)
Async XLA Ops:
  2.1 1.4 %collective-permute-start = (f32[16,256]{1,0:T(8,128)S(1)}, f32[16,256]{1,0:T(8,128)S(1)}, u32[]{:S(2)}, u32[]{:S(2)}) collective-permute-start(f32[16,256]{1,0:T(8,128)S(1)} %get-tuple-element.11), channel_id=1, source_target_pairs={{0,1},{1,0},{2,3},{3,2},{4,5},{5,4},{6,7},{7,6},{8,9},{9,8},{10,11... | collective-permute-start | bytes 49160 | tf_op jit(solution)/shard_map/ppermute | solution.py:27
  3.4 5.2 %collective-permute-start.1 = (f32[24,256]{1,0:T(8,128)S(1)}, f32[24,256]{1,0:T(8,128)S(1)}, u32[]{:S(2)}, u32[]{:S(2)}) collective-permute-start(f32[24,256]{1,0:T(8,128)S(1)} %pad_maximum_fusion.3), channel_id=1, source_target_pairs={{0,9},{1,8},{2,11},{3,10},{4,13},{5,12},{6,15},{7,14},{8,1},{9,0},... | collective-permute-start | bytes 73736 | tf_op jit(solution)/shard_map/ppermute | solution.py:27
  8.7 3.4 %collective-permute-start.2 = (f32[32,256]{1,0:T(8,128)S(1)}, f32[32,256]{1,0:T(8,128)S(1)}, u32[]{:S(2)}, u32[]{:S(2)}) collective-permute-start(f32[32,256]{1,0:T(8,128)S(1)} %pad_maximum_fusion.1), channel_id=1, source_target_pairs={{0,5},{1,2},{2,1},{3,6},{4,7},{5,0},{6,3},{7,4},{8,13},{9,10},{10,... | collective-permute-start | bytes 98312 | tf_op jit(solution)/shard_map/ppermute | solution.py:27
  12.1 1.6 %copy-start = (f32[32,256]{1,0:T(8,128)S(1)}, f32[32,256]{1,0:T(8,128)}, u32[]{:S(2)}) copy-start(f32[32,256]{1,0:T(8,128)} %prev_ref.1) | copy-start | bytes 98308
  12.1 3.6 %collective-permute-start.3 = (f32[48,256]{1,0:T(8,128)S(1)}, f32[48,256]{1,0:T(8,128)S(1)}, u32[]{:S(2)}, u32[]{:S(2)}) collective-permute-start(f32[48,256]{1,0:T(8,128)S(1)} %pad_maximum_fusion), channel_id=1, source_target_pairs={{0,3},{1,4},{2,7},{3,0},{4,1},{5,6},{6,5},{7,2},{8,11},{9,12},{10,... | collective-permute-start | bytes 147464 | tf_op jit(solution)/shard_map/ppermute | solution.py:27
  15.7 3.4 %collective-permute-start.4 = (f32[32,256]{1,0:T(8,128)S(1)}, f32[32,256]{1,0:T(8,128)S(1)}, u32[]{:S(2)}, u32[]{:S(2)}) collective-permute-start(f32[32,256]{1,0:T(8,128)S(1)} %pad_maximum_fusion.2), channel_id=1, source_target_pairs={{0,17},{1,16},{2,19},{3,18},{4,21},{5,20},{6,23},{7,22},{8,25},{9,... | collective-permute-start | bytes 98312 | tf_op jit(solution)/shard_map/ppermute | solution.py:27
  19.2 1.4 %collective-permute-start.5 = (f32[112,256]{1,0:T(8,128)S(1)}, f32[112,256]{1,0:T(8,128)S(1)}, u32[]{:S(2)}, u32[]{:S(2)}) collective-permute-start(f32[112,256]{1,0:T(8,128)S(1)} %slice_dynamic-update-slice_fusion.mine_ref), channel_id=1, source_target_pairs={{0,1},{1,0},{2,3},{3,2},{4,5},{5,4},{6,7},{7,6},{8,9},{9,8},{10,11... | collective-permute-start | bytes 344072 | tf_op jit(solution)/shard_map/ppermute | solution.py:27
  19.9 0.7 %copy-start.1 = (f32[7]{0:T(128)S(1)}, f32[7]{0:T(128)}, u32[]{:S(2)}) copy-start(f32[7]{0:T(128)} %param.9) | copy-start | bytes 88

commit v5 on v4

--- a/solution.py
+++ b/solution.py
@@ -101,30 +101,70 @@
     )(*(pltpu.with_memory_space_constraint(x, pltpu.HBM) for x in operands))
 
 
-def keep_kernel(perf, skill, student, keep_ref, proj):
+def keep_kernel(perf, skill, student, prev_hbm, coef_hbm, keep_ref, prev, coef, proj, sems):
+    copies = [
+        pltpu.make_async_copy(prev_hbm, prev, sems.at[0]),
+        pltpu.make_async_copy(coef_hbm, coef, sems.at[1]),
+    ]
+    for copy in copies:
+        copy.start()
     wide = student[...].astype(jnp.float32)
     student_sums(perf, skill, wide, proj, keep_ref)
     keep_ref[-wide.shape[0] :, :] = wide
-
-
-def keep_part(perf, skill, student):
+    for copy in copies:
+        copy.wait()
+
+
+def keep_part(perf, skill, student, prev, coef):
     rows, skills = perf.shape
     students, rank = student.shape
+    small = prev, coef.reshape(1, LAGS)
     return pl.pallas_call(
         keep_kernel,
         compiler_params=pltpu.CompilerParams(vmem_limit_bytes=VMEM_BYTES),
-        out_shape=jax.ShapeDtypeStruct((rows // students + students, rank), jnp.float32),
+        out_shape=(
+            jax.ShapeDtypeStruct((rows // students + students, rank), jnp.float32),
+            *(jax.ShapeDtypeStruct(x.shape, x.dtype) for x in small),
+        ),
+        in_specs=[VMEM] * 3 + [HBM] * 2,
+        out_specs=(VMEM,) * 3,
+        scratch_shapes=[
+            pltpu.VMEM((rank // LANES, rows, LANES), jnp.float32),
+            pltpu.SemaphoreType.DMA((2,)),
+        ],
+        cost_estimate=pl.CostEstimate(
+            flops=2 * rows * skills * rank, bytes_accessed=2 * (rows + rank) * skills, transcendentals=0
+        ),
+    )(perf, skill, student, *(pltpu.with_memory_space_constraint(x, pltpu.HBM) for x in small))
+
+
+def gram_kernel(mine_ref, other_ref, skill_gram_ref, out_ref):
+    students = jnp.concatenate([mine_ref[...], other_ref[...]], 0).astype(jnp.bfloat16)
+    student_gram = lax.dot_general(
+        students, students, (((0,), (0,)), ((), ())), preferred_element_type=jnp.float32
+    )
+    rank = out_ref.shape[0]
+    high, low = split(student_gram * skill_gram_ref[...])
+    out_ref[:, :rank] = high
+    out_ref[:, rank:] = low
+
+
+def gram_stack(mine, other, skill_gram):
+    count, rank = mine.shape
+    return pl.pallas_call(
+        gram_kernel,
+        compiler_params=pltpu.CompilerParams(vmem_limit_bytes=VMEM_BYTES),
+        out_shape=jax.ShapeDtypeStruct((rank, 2 * rank), jnp.bfloat16),
         in_specs=[VMEM] * 3,
         out_specs=VMEM,
-        scratch_shapes=[pltpu.VMEM((rank // LANES, rows, LANES), jnp.float32)],
         cost_estimate=pl.CostEstimate(
-            flops=2 * rows * skills * rank, bytes_accessed=2 * (rows + rank) * skills, transcendentals=0
-        ),
-    )(perf, skill, student)
+            flops=4 * count * rank * rank, bytes_accessed=8 * rank * rank, transcendentals=0
+        ),
+    )(mine, other, skill_gram)
 
 
 def cg_kernel(
-    columns, coef_ref, prev_ref, mine_ref, other_ref, skill_gram_ref, factor_hbm, residual_hbm,
+    columns, coef_ref, prev_ref, mine_ref, other_ref, gram_ref, factor_hbm, residual_hbm,
     mttkrp, values, low, high, block, results, sems,
 ):
     days, width = prev_ref.shape
@@ -139,20 +179,15 @@
             if b > 0:
                 row = (blocks + b - 1) * half
                 values[place, :] = source[row : row + half, :]
-    start = (2 * blocks - 1) * half
-    students = jnp.concatenate([mine_ref[start:, :], other_ref[start:, :]], 0).astype(jnp.bfloat16)
-    student_gram = lax.dot_general(
-        students, students, (((0,), (0,)), ((), ())), preferred_element_type=jnp.float32
-    )
-    gram_high, gram_low = split(student_gram * skill_gram_ref[...])
-    gram = jnp.concatenate([gram_high, gram_high, gram_low], 0)
+    gram_high, gram_wide = gram_ref[:, :width], gram_ref[...]
     low[:PAD, :] = jnp.zeros((PAD, width), jnp.float32)
     high[pl.ds(total, PAD), :] = jnp.zeros((PAD, width), jnp.float32)
     coef = [coef_ref[:, l : l + 1] for l in range(LAGS)]
 
     def operate(v):
         v_high, v_low = split(v)
-        mixed = product(jnp.concatenate([v_high, v_low, v_high], 1), gram)
+        both = product(jnp.concatenate([v_high, v_low], 0), gram_wide)
+        mixed = both[:total, :width] + (both[total:, :width] + both[:total, width:])
         low[pl.ds(PAD, total), :] = v
         ahead = v
         for lag in range(1, LAGS + 1):
@@ -199,7 +234,7 @@
         copy.wait()
 
 
-def conjugate(coef, prev, mine, other, skill_gram, blocks, columns):
+def conjugate(coef, prev, mine, other, gram, blocks, columns):
     days, width = prev.shape
     total = days * blocks
     shape = jax.ShapeDtypeStruct((columns, days), jnp.float32)
@@ -221,7 +256,7 @@
         cost_estimate=pl.CostEstimate(
             flops=24 * total * width * width, bytes_accessed=4 * width * (width + 2 * total), transcendentals=0
         ),
-    )(coef.reshape(1, LAGS), prev, mine, other, skill_gram)
+    )(coef, prev, mine, other, gram)
 
 
 def bits_of(count):
@@ -236,12 +271,14 @@
     stu_size, day_size = lax.axis_size("stu"), lax.axis_size("day")
     send, skill, perf, student = send_part(performance, student_factor, skill_factor)
     got = exchange(send, 1)
-    keep = keep_part(perf, skill, student)
+    keep, day_prev, coef = keep_part(perf, skill, student, day_prev, ar_coef)
     skill_gram = lax.dot_general(skill, skill, (((0,), (0,)), ((), ())), preferred_element_type=jnp.float32)
     payload = jnp.concatenate([keep[:half] + got, keep[half:]], 0)
     masks = [bit | 1 for bit in bits_of(stu_size)[:0:-1]]
     for mask, other in zip(masks, masks[:-2] + masks[:-3:-1], strict=True):
         got = exchange(payload, mask, other)
+        if mask == masks[0]:
+            got, skill_gram = lax.optimization_barrier((got, skill_gram))
         payload = jnp.concatenate([payload[:half] + got[:half], payload[half:], got[half:]], 0)
     mttkrp, students = payload[:half], payload[half:]
     factor = lax.dynamic_slice_in_dim(day_prev, own_part() * half, half, 0)
@@ -250,9 +287,10 @@
         rows = bit * half
         mttkrp = jnp.concatenate([mttkrp, got[:rows]], 0)
         factor = jnp.concatenate([factor, got[rows:]], 0)
-    mine = jnp.concatenate([mttkrp, factor[half:], students], 0)
+    stack = gram_stack(students, exchange(students, 1), skill_gram)
+    mine = jnp.concatenate([mttkrp, factor[half:]], 0)
     other = exchange(mine, 1)
-    factor, residual = conjugate(ar_coef, day_prev, mine, other, skill_gram, day_size, rank // stu_size)
+    factor, residual = conjugate(coef, day_prev, mine, other, stack, day_size, rank // stu_size)
     return factor.T, residual.T
 
 

time: 23.1 us -> 22.6 us (0.978)
  waiting for transfers between devices: 8.2 us -> 6.92 us
  Pallas kernels: 3.97 us -> 4.48 us
  starting transfers between devices: 9.57 us -> 9.94 us
    ppermute x6 -> x7, waiting for transfers between devices: 8.2 us -> 6.92 us  [exchange(): return lax.ppermute(block, ('day', 'stu'), route)]
    pallas_call x1, Pallas kernels: 0.25 us -> 0.78 us  [keep_part(): pl.pallas_call(keep_kernel, compiler_params=pltpu.CompilerParams(vmem_lim...]
    ppermute x6 -> x7, starting transfers between devices: 9.57 us -> 9.94 us  [exchange(): return lax.ppermute(block, ('day', 'stu'), route)]
    pallas_call x1, Pallas kernels: 2.31 us -> 2.06 us  [conjugate(): pl.pallas_call(functools.partial(cg_kernel, columns), compiler_params=plt...]
  transfers between devices with their start and end apart: 6 -> 7, of which waited for: 6 -> 5; matrix products, arithmetic and copies ran while one was open for 1% -> 2% of each run, Pallas kernels for 1% -> 4%
where the time goes in v5:
time: 22.6 us; the launch traced here: 22.4 us
  starting transfers between devices  9.94 us (44%)
  waiting for transfers between devices  6.92 us (31%)
  Pallas kernels  4.48 us (20%)
  between operations  0.68 us (3%)
  matrix products  0.34 us (2%)
    ppermute x7, starting transfers between devices, exchange(): return lax.ppermute(block, ('day', 'stu'), route)  9.94 us
    ppermute x7, waiting for transfers between devices, exchange(): return lax.ppermute(block, ('day', 'stu'), route)  6.92 us
    pallas_call x1, Pallas kernels, conjugate(): pl.pallas_call(functools.partial(cg_kernel, columns), compiler_params=plt...  2.06 us
    pallas_call x1, Pallas kernels, send_part(): pl.pallas_call(send_kernel, compiler_params=pltpu.CompilerParams(vmem_lim...  1.42 us
    pallas_call x1, Pallas kernels, keep_part(): pl.pallas_call(keep_kernel, compiler_params=pltpu.CompilerParams(vmem_lim...  0.78 us
  transfers between devices with their start and end apart: 7, of which 5 were waited for; matrix products, arithmetic and copies ran while one was open for 2% of the time, Pallas kernels for 4%

profile of v5, /device:TPU:0, one launch (start us, length us, event | category | flops | bytes accessed | tf_op | source)
XLA Modules:
  0.0 22.4 jit_solution(2039775035540510798)
XLA Ops:
  0.6 1.4 %shard_map.68 = (f32[16,256]{1,0:T(8,128)S(1)}, bf16[1024,256]{1,0:T(8,128)(2,1)S(1)}, bf16[128,1024]{1,0:T(8,128)(2,1)S(1)}, bf16[8,256]{1,0:T(8,128)(2,1)S(1)}) custom-call(bf16[256,1024]{1,0:T(8,128)(2,1)} %bitcast.6, bf16[1024,256]{1,0:T(8,128)(2,1)} %skill_hbm.1, bf16[8,256]{1,0:T(8,128)(2,1)} %student_hbm.1), custom_call_target="tpu_custom_call" | custom-call | flops 67108864 | bytes 1048576 | tf_op jit(solution)/shard_map/pallas_call | solution.py:82
  2.1 0.5 %collective-permute-start = (f32[16,256]{1,0:T(8,128)S(1)}, f32[16,256]{1,0:T(8,128)S(1)}, u32[]{:S(2)}, u32[]{:S(2)}) collective-permute-start(f32[16,256]{1,0:T(8,128)S(1)} %get-tuple-element.19), channel_id=1, source_target_pairs={{0,1},{1,0},{2,3},{3,2},{4,5},{5,4},{6,7},{7,6},{8,9},{9,8},{10,11... | collective-permute-start | bytes 49160 | tf_op jit(solution)/shard_map/ppermute | solution.py:27
  2.6 0.8 %shard_map.69 = (f32[24,256]{1,0:T(8,128)S(1)}, f32[32,256]{1,0:T(8,128)S(1)}, f32[1,7]{1,0:T(1,128)S(1)}) custom-call(bf16[128,1024]{1,0:T(8,128)(2,1)S(1)} %get-tuple-element.13.perf, bf16[1024,256]{1,0:T(8,128)(2,1)S(1)} %get-tuple-element.14.skill, bf16[8,256]{1,0:T(8,128)(2,1)S(1)} %get-tuple-element.15.student, f32[32,256]{1,0:T(8,128)} %prev_hbm.1, ...), custom_call_target="tpu_custom_call" | custom-call | flops 67108864 | bytes 786432 | tf_op jit(solution)/shard_map/pallas_call | solution.py:122
  3.4 0.0 collective-permute-done
  3.4 3.8 %collective-permute-start.1 = (f32[24,256]{1,0:T(8,128)S(1)}, f32[24,256]{1,0:T(8,128)S(1)}, u32[]{:S(2)}, u32[]{:S(2)}) collective-permute-start(f32[24,256]{1,0:T(8,128)S(1)} %pad_maximum_fusion.5), channel_id=1, source_target_pairs={{0,9},{1,8},{2,11},{3,10},{4,13},{5,12},{6,15},{7,14},{8,1},{9,0},... | collective-permute-start | bytes 73736 | tf_op jit(solution)/shard_map/ppermute | solution.py:27
  7.2 0.3 %fusion.1.skill_gram_ref = f32[256,256]{1,0:T(8,128)S(1)} fusion(bf16[1024,256]{1,0:T(8,128)(2,1)S(1)} %get-tuple-element.14.skill), kind=kOutput, calls=%fused_computation.12 | convolution fusion | flops 134217728 | bytes 786432 | tf_op jit(solution)/shard_map/dot_general | solution.py:275
  7.5 1.2 %collective-permute-done.1 = f32[24,256]{1,0:T(8,128)S(1)} collective-permute-done((f32[24,256]{1,0:T(8,128)S(1)}, f32[24,256]{1,0:T(8,128)S(1)}, u32[]{:S(2)}, u32[]{:S(2)}) %collective-permute-start.1) | collective-permute-done | bytes 24608 | tf_op jit(solution)/shard_map/ppermute | solution.py:27
  8.7 1.7 %collective-permute-start.2 = (f32[32,256]{1,0:T(8,128)S(1)}, f32[32,256]{1,0:T(8,128)S(1)}, u32[]{:S(2)}, u32[]{:S(2)}) collective-permute-start(f32[32,256]{1,0:T(8,128)S(1)} %pad_maximum_fusion.3), channel_id=1, source_target_pairs={{0,5},{1,2},{2,1},{3,6},{4,7},{5,0},{6,3},{7,4},{8,13},{9,10},{10,... | collective-permute-start | bytes 98312 | tf_op jit(solution)/shard_map/ppermute | solution.py:27
  10.4 1.7 %collective-permute-done.2 = f32[32,256]{1,0:T(8,128)S(1)} collective-permute-done((f32[32,256]{1,0:T(8,128)S(1)}, f32[32,256]{1,0:T(8,128)S(1)}, u32[]{:S(2)}, u32[]{:S(2)}) %collective-permute-start.2) | collective-permute-done | bytes 32800 | tf_op jit(solution)/shard_map/ppermute | solution.py:27
  12.1 1.6 %collective-permute-start.3 = (f32[48,256]{1,0:T(8,128)S(1)}, f32[48,256]{1,0:T(8,128)S(1)}, u32[]{:S(2)}, u32[]{:S(2)}) collective-permute-start(f32[48,256]{1,0:T(8,128)S(1)} %pad_maximum_fusion.1), channel_id=1, source_target_pairs={{0,3},{1,4},{2,7},{3,0},{4,1},{5,6},{6,5},{7,2},{8,11},{9,12},{10,... | collective-permute-start | bytes 147464 | tf_op jit(solution)/shard_map/ppermute | solution.py:27
  13.7 2.0 %collective-permute-done.3 = f32[48,256]{1,0:T(8,128)S(1)} collective-permute-done((f32[48,256]{1,0:T(8,128)S(1)}, f32[48,256]{1,0:T(8,128)S(1)}, u32[]{:S(2)}, u32[]{:S(2)}) %collective-permute-start.3) | collective-permute-done | bytes 49184 | tf_op jit(solution)/shard_map/ppermute | solution.py:27
  15.7 1.6 %collective-permute-start.4 = (f32[32,256]{1,0:T(8,128)S(1)}, f32[32,256]{1,0:T(8,128)S(1)}, u32[]{:S(2)}, u32[]{:S(2)}) collective-permute-start(f32[32,256]{1,0:T(8,128)S(1)} %pad_maximum_fusion.4), channel_id=1, source_target_pairs={{0,17},{1,16},{2,19},{3,18},{4,21},{5,20},{6,23},{7,22},{8,25},{9,... | collective-permute-start | bytes 98312 | tf_op jit(solution)/shard_map/ppermute | solution.py:27
  17.4 0.4 %collective-permute-start.6 = (f32[64,256]{1,0:T(8,128)S(1)}, f32[64,256]{1,0:T(8,128)S(1)}, u32[]{:S(2)}, u32[]{:S(2)}) collective-permute-start(f32[64,256]{1,0:T(8,128)S(1)} %pad_maximum_fusion.mine_ref), channel_id=1, source_target_pairs={{0,1},{1,0},{2,3},{3,2},{4,5},{5,4},{6,7},{7,6},{8,9},{9,8},{10,11... | collective-permute-start | bytes 196616 | tf_op jit(solution)/shard_map/ppermute | solution.py:27
  17.8 1.3 %collective-permute-done.4 = f32[32,256]{1,0:T(8,128)S(1)} collective-permute-done((f32[32,256]{1,0:T(8,128)S(1)}, f32[32,256]{1,0:T(8,128)S(1)}, u32[]{:S(2)}, u32[]{:S(2)}) %collective-permute-start.4) | collective-permute-done | bytes 32800 | tf_op jit(solution)/shard_map/ppermute | solution.py:27
  19.1 0.3 %collective-permute-start.5 = (f32[48,256]{1,0:T(8,128)S(1)}, f32[48,256]{1,0:T(8,128)S(1)}, u32[]{:S(2)}, u32[]{:S(2)}) collective-permute-start(f32[48,256]{1,0:T(8,128)S(1)} %pad_maximum_fusion.2.mine_ref), channel_id=1, source_target_pairs={{0,1},{1,0},{2,3},{3,2},{4,5},{5,4},{6,7},{7,6},{8,9},{9,8},{10,11... | collective-permute-start | bytes 147464 | tf_op jit(solution)/shard_map/ppermute | solution.py:27
  19.5 0.0 collective-permute-done.6.other_ref
  19.5 0.2 shard_map.70.gram_ref
  19.7 0.7 %collective-permute-done.5.other_ref = f32[48,256]{1,0:T(8,128)S(1)} collective-permute-done((f32[48,256]{1,0:T(8,128)S(1)}, f32[48,256]{1,0:T(8,128)S(1)}, u32[]{:S(2)}, u32[]{:S(2)}) %collective-permute-start.5) | collective-permute-done | bytes 49184 | tf_op jit(solution)/shard_map/ppermute | solution.py:27
  20.4 2.1 %shard_map.71 = (f32[16,32]{1,0:T(8,128)}, f32[16,32]{1,0:T(8,128)}) custom-call(f32[1,7]{1,0:T(1,128)S(1)} %get-tuple-element.16.coef_ref, f32[32,256]{1,0:T(8,128)S(1)} %get-tuple-element.17.prev_ref, f32[48,256]{1,0:T(8,128)S(1)} %pad_maximum_fusion.2.mine_ref, f32[48,256]{1,0:T(8,128)S(1)} %collective-permute-done.5.other_ref, ...), custom_call_target="tpu_custom_call" | custom-call | flops 100663296 | bytes 393216 | tf_op jit(solution)/shard_map/pallas_call | solution.py:241
  (14 shorter events, 0.1 us)
Async XLA Ops:
  2.1 1.4 %collective-permute-start = (f32[16,256]{1,0:T(8,128)S(1)}, f32[16,256]{1,0:T(8,128)S(1)}, u32[]{:S(2)}, u32[]{:S(2)}) collective-permute-start(f32[16,256]{1,0:T(8,128)S(1)} %get-tuple-element.19), channel_id=1, source_target_pairs={{0,1},{1,0},{2,3},{3,2},{4,5},{5,4},{6,7},{7,6},{8,9},{9,8},{10,11... | collective-permute-start | bytes 49160 | tf_op jit(solution)/shard_map/ppermute | solution.py:27
  3.4 5.3 %collective-permute-start.1 = (f32[24,256]{1,0:T(8,128)S(1)}, f32[24,256]{1,0:T(8,128)S(1)}, u32[]{:S(2)}, u32[]{:S(2)}) collective-permute-start(f32[24,256]{1,0:T(8,128)S(1)} %pad_maximum_fusion.5), channel_id=1, source_target_pairs={{0,9},{1,8},{2,11},{3,10},{4,13},{5,12},{6,15},{7,14},{8,1},{9,0},... | collective-permute-start | bytes 73736 | tf_op jit(solution)/shard_map/ppermute | solution.py:27
  8.7 3.4 %collective-permute-start.2 = (f32[32,256]{1,0:T(8,128)S(1)}, f32[32,256]{1,0:T(8,128)S(1)}, u32[]{:S(2)}, u32[]{:S(2)}) collective-permute-start(f32[32,256]{1,0:T(8,128)S(1)} %pad_maximum_fusion.3), channel_id=1, source_target_pairs={{0,5},{1,2},{2,1},{3,6},{4,7},{5,0},{6,3},{7,4},{8,13},{9,10},{10,... | collective-permute-start | bytes 98312 | tf_op jit(solution)/shard_map/ppermute | solution.py:27
  12.1 3.6 %collective-permute-start.3 = (f32[48,256]{1,0:T(8,128)S(1)}, f32[48,256]{1,0:T(8,128)S(1)}, u32[]{:S(2)}, u32[]{:S(2)}) collective-permute-start(f32[48,256]{1,0:T(8,128)S(1)} %pad_maximum_fusion.1), channel_id=1, source_target_pairs={{0,3},{1,4},{2,7},{3,0},{4,1},{5,6},{6,5},{7,2},{8,11},{9,12},{10,... | collective-permute-start | bytes 147464 | tf_op jit(solution)/shard_map/ppermute | solution.py:27
  15.7 3.4 %collective-permute-start.4 = (f32[32,256]{1,0:T(8,128)S(1)}, f32[32,256]{1,0:T(8,128)S(1)}, u32[]{:S(2)}, u32[]{:S(2)}) collective-permute-start(f32[32,256]{1,0:T(8,128)S(1)} %pad_maximum_fusion.4), channel_id=1, source_target_pairs={{0,17},{1,16},{2,19},{3,18},{4,21},{5,20},{6,23},{7,22},{8,25},{9,... | collective-permute-start | bytes 98312 | tf_op jit(solution)/shard_map/ppermute | solution.py:27
  17.4 2.1 %collective-permute-start.6 = (f32[64,256]{1,0:T(8,128)S(1)}, f32[64,256]{1,0:T(8,128)S(1)}, u32[]{:S(2)}, u32[]{:S(2)}) collective-permute-start(f32[64,256]{1,0:T(8,128)S(1)} %pad_maximum_fusion.mine_ref), channel_id=1, source_target_pairs={{0,1},{1,0},{2,3},{3,2},{4,5},{5,4},{6,7},{7,6},{8,9},{9,8},{10,11... | collective-permute-start | bytes 196616 | tf_op jit(solution)/shard_map/ppermute | solution.py:27
  19.1 1.2 %collective-permute-start.5 = (f32[48,256]{1,0:T(8,128)S(1)}, f32[48,256]{1,0:T(8,128)S(1)}, u32[]{:S(2)}, u32[]{:S(2)}) collective-permute-start(f32[48,256]{1,0:T(8,128)S(1)} %pad_maximum_fusion.2.mine_ref), channel_id=1, source_target_pairs={{0,1},{1,0},{2,3},{3,2},{4,5},{5,4},{6,7},{7,6},{8,9},{9,8},{10,11... | collective-permute-start | bytes 147464 | tf_op jit(solution)/shard_map/ppermute | solution.py:27

commit v6 on v5

--- a/solution.py
+++ b/solution.py
@@ -209,25 +209,29 @@
 
     factor = values[...]
     residual = mttkrp[...] - operate(factor)
+    start = pl.multiple_of(day * days, days)
+    turn = jnp.where(stu == 0, 0, width - stu * columns)
+
+    def own(v, slot):
+        block[slot] = v
+        return pltpu.roll(block[slot, pl.ds(start, days), :], turn, axis=1)[:, :columns].T
+
     direction, image = residual, operate(residual)
     now = inner(residual, residual)
-    for step in range(ITERS):
+    for step in range(ITERS - 1):
         alpha = now / inner(direction, image)
         factor = factor + alpha * direction
         residual = residual - alpha * image
-        if step < ITERS - 1:
-            ahead, following = operate(residual), inner(residual, residual)
-            beta = following / now
-            direction = residual + beta * direction
-            image = ahead + beta * image
-            now = following
-    start = pl.multiple_of(day * days, days)
-    turn = jnp.where(stu == 0, 0, width - stu * columns)
+        ahead, following = operate(residual), inner(residual, residual)
+        beta = following / now
+        direction = residual + beta * direction
+        image = ahead + beta * image
+        now = following
+    alpha = now / inner(direction, image)
+    results[0] = own(factor, 0) + alpha * own(direction, 1)
+    results[1] = own(residual, 2) - alpha * own(image, 3)
     copies = []
-    for i, (result, target) in enumerate(((factor, factor_hbm), (residual, residual_hbm))):
-        block[i] = result
-        rows = block[i, pl.ds(start, days), :]
-        results[i] = pltpu.roll(rows, turn, axis=1)[:, :columns].T
+    for i, target in enumerate((factor_hbm, residual_hbm)):
         copies.append(pltpu.make_async_copy(results.at[i], target, sems.at[i]))
         copies[i].start()
     for copy in copies:
@@ -249,7 +253,7 @@
             pltpu.VMEM((total, width), jnp.float32),
             pltpu.VMEM((total + PAD, width), jnp.float32),
             pltpu.VMEM((total + PAD, width), jnp.float32),
-            pltpu.VMEM((2, total, width), jnp.float32),
+            pltpu.VMEM((4, total, width), jnp.float32),
             pltpu.VMEM((2, columns, days), jnp.float32),
             pltpu.SemaphoreType.DMA((2,)),
         ],

time: 22.6 us -> 22.6 us (level)
  transfers between devices with their start and end apart: 7 -> 7, of which waited for: 5 -> 5; matrix products, arithmetic and copies ran while one was open for 2% -> 2% of each run, Pallas kernels for 4% -> 5%
where the time goes in v6:
time: 22.6 us; the launch traced here: 22.3 us
  starting transfers between devices  9.94 us (44%)
  waiting for transfers between devices  6.92 us (31%)
  Pallas kernels  4.4 us (19%)
  between operations  0.68 us (3%)
  matrix products  0.34 us (2%)
    ppermute x7, starting transfers between devices, exchange(): return lax.ppermute(block, ('day', 'stu'), route)  9.94 us
    ppermute x7, waiting for transfers between devices, exchange(): return lax.ppermute(block, ('day', 'stu'), route)  6.92 us
    pallas_call x1, Pallas kernels, conjugate(): pl.pallas_call(functools.partial(cg_kernel, columns), compiler_params=plt...  1.98 us
    pallas_call x1, Pallas kernels, send_part(): pl.pallas_call(send_kernel, compiler_params=pltpu.CompilerParams(vmem_lim...  1.42 us
    pallas_call x1, Pallas kernels, keep_part(): pl.pallas_call(keep_kernel, compiler_params=pltpu.CompilerParams(vmem_lim...  0.78 us
  transfers between devices with their start and end apart: 7, of which 5 were waited for; matrix products, arithmetic and copies ran while one was open for 2% of the time, Pallas kernels for 5%

profile of v6, /device:TPU:0, one launch (start us, length us, event | category | flops | bytes accessed | tf_op | source)
XLA Modules:
  0.0 22.3 jit_solution(18233241131475527195)
XLA Ops:
  0.6 1.4 %shard_map.68 = (f32[16,256]{1,0:T(8,128)S(1)}, bf16[1024,256]{1,0:T(8,128)(2,1)S(1)}, bf16[128,1024]{1,0:T(8,128)(2,1)S(1)}, bf16[8,256]{1,0:T(8,128)(2,1)S(1)}) custom-call(bf16[256,1024]{1,0:T(8,128)(2,1)} %bitcast.6, bf16[1024,256]{1,0:T(8,128)(2,1)} %skill_hbm.1, bf16[8,256]{1,0:T(8,128)(2,1)} %student_hbm.1), custom_call_target="tpu_custom_call" | custom-call | flops 67108864 | bytes 1048576 | tf_op jit(solution)/shard_map/pallas_call | solution.py:82
  2.1 0.5 %collective-permute-start = (f32[16,256]{1,0:T(8,128)S(1)}, f32[16,256]{1,0:T(8,128)S(1)}, u32[]{:S(2)}, u32[]{:S(2)}) collective-permute-start(f32[16,256]{1,0:T(8,128)S(1)} %get-tuple-element.19), channel_id=1, source_target_pairs={{0,1},{1,0},{2,3},{3,2},{4,5},{5,4},{6,7},{7,6},{8,9},{9,8},{10,11... | collective-permute-start | bytes 49160 | tf_op jit(solution)/shard_map/ppermute | solution.py:27
  2.6 0.8 %shard_map.69 = (f32[24,256]{1,0:T(8,128)S(1)}, f32[32,256]{1,0:T(8,128)S(1)}, f32[1,7]{1,0:T(1,128)S(1)}) custom-call(bf16[128,1024]{1,0:T(8,128)(2,1)S(1)} %get-tuple-element.13.perf, bf16[1024,256]{1,0:T(8,128)(2,1)S(1)} %get-tuple-element.14.skill, bf16[8,256]{1,0:T(8,128)(2,1)S(1)} %get-tuple-element.15.student, f32[32,256]{1,0:T(8,128)} %prev_hbm.1, ...), custom_call_target="tpu_custom_call" | custom-call | flops 67108864 | bytes 786432 | tf_op jit(solution)/shard_map/pallas_call | solution.py:122
  3.4 0.0 collective-permute-done
  3.4 3.8 %collective-permute-start.1 = (f32[24,256]{1,0:T(8,128)S(1)}, f32[24,256]{1,0:T(8,128)S(1)}, u32[]{:S(2)}, u32[]{:S(2)}) collective-permute-start(f32[24,256]{1,0:T(8,128)S(1)} %pad_maximum_fusion.5), channel_id=1, source_target_pairs={{0,9},{1,8},{2,11},{3,10},{4,13},{5,12},{6,15},{7,14},{8,1},{9,0},... | collective-permute-start | bytes 73736 | tf_op jit(solution)/shard_map/ppermute | solution.py:27
  7.2 0.3 %fusion.1.skill_gram_ref = f32[256,256]{1,0:T(8,128)S(1)} fusion(bf16[1024,256]{1,0:T(8,128)(2,1)S(1)} %get-tuple-element.14.skill), kind=kOutput, calls=%fused_computation.12 | convolution fusion | flops 134217728 | bytes 786432 | tf_op jit(solution)/shard_map/dot_general | solution.py:279
  7.5 1.2 %collective-permute-done.1 = f32[24,256]{1,0:T(8,128)S(1)} collective-permute-done((f32[24,256]{1,0:T(8,128)S(1)}, f32[24,256]{1,0:T(8,128)S(1)}, u32[]{:S(2)}, u32[]{:S(2)}) %collective-permute-start.1) | collective-permute-done | bytes 24608 | tf_op jit(solution)/shard_map/ppermute | solution.py:27
  8.7 1.7 %collective-permute-start.2 = (f32[32,256]{1,0:T(8,128)S(1)}, f32[32,256]{1,0:T(8,128)S(1)}, u32[]{:S(2)}, u32[]{:S(2)}) collective-permute-start(f32[32,256]{1,0:T(8,128)S(1)} %pad_maximum_fusion.3), channel_id=1, source_target_pairs={{0,5},{1,2},{2,1},{3,6},{4,7},{5,0},{6,3},{7,4},{8,13},{9,10},{10,... | collective-permute-start | bytes 98312 | tf_op jit(solution)/shard_map/ppermute | solution.py:27
  10.4 1.7 %collective-permute-done.2 = f32[32,256]{1,0:T(8,128)S(1)} collective-permute-done((f32[32,256]{1,0:T(8,128)S(1)}, f32[32,256]{1,0:T(8,128)S(1)}, u32[]{:S(2)}, u32[]{:S(2)}) %collective-permute-start.2) | collective-permute-done | bytes 32800 | tf_op jit(solution)/shard_map/ppermute | solution.py:27
  12.1 1.6 %collective-permute-start.3 = (f32[48,256]{1,0:T(8,128)S(1)}, f32[48,256]{1,0:T(8,128)S(1)}, u32[]{:S(2)}, u32[]{:S(2)}) collective-permute-start(f32[48,256]{1,0:T(8,128)S(1)} %pad_maximum_fusion.1), channel_id=1, source_target_pairs={{0,3},{1,4},{2,7},{3,0},{4,1},{5,6},{6,5},{7,2},{8,11},{9,12},{10,... | collective-permute-start | bytes 147464 | tf_op jit(solution)/shard_map/ppermute | solution.py:27
  13.7 2.0 %collective-permute-done.3 = f32[48,256]{1,0:T(8,128)S(1)} collective-permute-done((f32[48,256]{1,0:T(8,128)S(1)}, f32[48,256]{1,0:T(8,128)S(1)}, u32[]{:S(2)}, u32[]{:S(2)}) %collective-permute-start.3) | collective-permute-done | bytes 49184 | tf_op jit(solution)/shard_map/ppermute | solution.py:27
  15.7 1.6 %collective-permute-start.4 = (f32[32,256]{1,0:T(8,128)S(1)}, f32[32,256]{1,0:T(8,128)S(1)}, u32[]{:S(2)}, u32[]{:S(2)}) collective-permute-start(f32[32,256]{1,0:T(8,128)S(1)} %pad_maximum_fusion.4), channel_id=1, source_target_pairs={{0,17},{1,16},{2,19},{3,18},{4,21},{5,20},{6,23},{7,22},{8,25},{9,... | collective-permute-start | bytes 98312 | tf_op jit(solution)/shard_map/ppermute | solution.py:27
  17.4 0.4 %collective-permute-start.6 = (f32[64,256]{1,0:T(8,128)S(1)}, f32[64,256]{1,0:T(8,128)S(1)}, u32[]{:S(2)}, u32[]{:S(2)}) collective-permute-start(f32[64,256]{1,0:T(8,128)S(1)} %pad_maximum_fusion.mine_ref), channel_id=1, source_target_pairs={{0,1},{1,0},{2,3},{3,2},{4,5},{5,4},{6,7},{7,6},{8,9},{9,8},{10,11... | collective-permute-start | bytes 196616 | tf_op jit(solution)/shard_map/ppermute | solution.py:27
  17.8 1.3 %collective-permute-done.4 = f32[32,256]{1,0:T(8,128)S(1)} collective-permute-done((f32[32,256]{1,0:T(8,128)S(1)}, f32[32,256]{1,0:T(8,128)S(1)}, u32[]{:S(2)}, u32[]{:S(2)}) %collective-permute-start.4) | collective-permute-done | bytes 32800 | tf_op jit(solution)/shard_map/ppermute | solution.py:27
  19.1 0.3 %collective-permute-start.5 = (f32[48,256]{1,0:T(8,128)S(1)}, f32[48,256]{1,0:T(8,128)S(1)}, u32[]{:S(2)}, u32[]{:S(2)}) collective-permute-start(f32[48,256]{1,0:T(8,128)S(1)} %pad_maximum_fusion.2.mine_ref), channel_id=1, source_target_pairs={{0,1},{1,0},{2,3},{3,2},{4,5},{5,4},{6,7},{7,6},{8,9},{9,8},{10,11... | collective-permute-start | bytes 147464 | tf_op jit(solution)/shard_map/ppermute | solution.py:27
  19.5 0.0 collective-permute-done.6.other_ref
  19.5 0.2 shard_map.70.gram_ref
  19.7 0.7 %collective-permute-done.5.other_ref = f32[48,256]{1,0:T(8,128)S(1)} collective-permute-done((f32[48,256]{1,0:T(8,128)S(1)}, f32[48,256]{1,0:T(8,128)S(1)}, u32[]{:S(2)}, u32[]{:S(2)}) %collective-permute-start.5) | collective-permute-done | bytes 49184 | tf_op jit(solution)/shard_map/ppermute | solution.py:27
  20.4 2.0 %shard_map.71 = (f32[16,32]{1,0:T(8,128)}, f32[16,32]{1,0:T(8,128)}) custom-call(f32[1,7]{1,0:T(1,128)S(1)} %get-tuple-element.16.coef_ref, f32[32,256]{1,0:T(8,128)S(1)} %get-tuple-element.17.prev_ref, f32[48,256]{1,0:T(8,128)S(1)} %pad_maximum_fusion.2.mine_ref, f32[48,256]{1,0:T(8,128)S(1)} %collective-permute-done.5.other_ref, ...), custom_call_target="tpu_custom_call" | custom-call | flops 100663296 | bytes 393216 | tf_op jit(solution)/shard_map/pallas_call | solution.py:245
  (14 shorter events, 0.1 us)
Async XLA Ops:
  2.1 1.4 %collective-permute-start = (f32[16,256]{1,0:T(8,128)S(1)}, f32[16,256]{1,0:T(8,128)S(1)}, u32[]{:S(2)}, u32[]{:S(2)}) collective-permute-start(f32[16,256]{1,0:T(8,128)S(1)} %get-tuple-element.19), channel_id=1, source_target_pairs={{0,1},{1,0},{2,3},{3,2},{4,5},{5,4},{6,7},{7,6},{8,9},{9,8},{10,11... | collective-permute-start | bytes 49160 | tf_op jit(solution)/shard_map/ppermute | solution.py:27
  3.4 5.3 %collective-permute-start.1 = (f32[24,256]{1,0:T(8,128)S(1)}, f32[24,256]{1,0:T(8,128)S(1)}, u32[]{:S(2)}, u32[]{:S(2)}) collective-permute-start(f32[24,256]{1,0:T(8,128)S(1)} %pad_maximum_fusion.5), channel_id=1, source_target_pairs={{0,9},{1,8},{2,11},{3,10},{4,13},{5,12},{6,15},{7,14},{8,1},{9,0},... | collective-permute-start | bytes 73736 | tf_op jit(solution)/shard_map/ppermute | solution.py:27
  8.7 3.4 %collective-permute-start.2 = (f32[32,256]{1,0:T(8,128)S(1)}, f32[32,256]{1,0:T(8,128)S(1)}, u32[]{:S(2)}, u32[]{:S(2)}) collective-permute-start(f32[32,256]{1,0:T(8,128)S(1)} %pad_maximum_fusion.3), channel_id=1, source_target_pairs={{0,5},{1,2},{2,1},{3,6},{4,7},{5,0},{6,3},{7,4},{8,13},{9,10},{10,... | collective-permute-start | bytes 98312 | tf_op jit(solution)/shard_map/ppermute | solution.py:27
  12.1 3.6 %collective-permute-start.3 = (f32[48,256]{1,0:T(8,128)S(1)}, f32[48,256]{1,0:T(8,128)S(1)}, u32[]{:S(2)}, u32[]{:S(2)}) collective-permute-start(f32[48,256]{1,0:T(8,128)S(1)} %pad_maximum_fusion.1), channel_id=1, source_target_pairs={{0,3},{1,4},{2,7},{3,0},{4,1},{5,6},{6,5},{7,2},{8,11},{9,12},{10,... | collective-permute-start | bytes 147464 | tf_op jit(solution)/shard_map/ppermute | solution.py:27
  15.7 3.4 %collective-permute-start.4 = (f32[32,256]{1,0:T(8,128)S(1)}, f32[32,256]{1,0:T(8,128)S(1)}, u32[]{:S(2)}, u32[]{:S(2)}) collective-permute-start(f32[32,256]{1,0:T(8,128)S(1)} %pad_maximum_fusion.4), channel_id=1, source_target_pairs={{0,17},{1,16},{2,19},{3,18},{4,21},{5,20},{6,23},{7,22},{8,25},{9,... | collective-permute-start | bytes 98312 | tf_op jit(solution)/shard_map/ppermute | solution.py:27
  17.4 2.1 %collective-permute-start.6 = (f32[64,256]{1,0:T(8,128)S(1)}, f32[64,256]{1,0:T(8,128)S(1)}, u32[]{:S(2)}, u32[]{:S(2)}) collective-permute-start(f32[64,256]{1,0:T(8,128)S(1)} %pad_maximum_fusion.mine_ref), channel_id=1, source_target_pairs={{0,1},{1,0},{2,3},{3,2},{4,5},{5,4},{6,7},{7,6},{8,9},{9,8},{10,11... | collective-permute-start | bytes 196616 | tf_op jit(solution)/shard_map/ppermute | solution.py:27
  19.1 1.2 %collective-permute-start.5 = (f32[48,256]{1,0:T(8,128)S(1)}, f32[48,256]{1,0:T(8,128)S(1)}, u32[]{:S(2)}, u32[]{:S(2)}) collective-permute-start(f32[48,256]{1,0:T(8,128)S(1)} %pad_maximum_fusion.2.mine_ref), channel_id=1, source_target_pairs={{0,1},{1,0},{2,3},{3,2},{4,5},{5,4},{6,7},{7,6},{8,9},{9,8},{10,11... | collective-permute-start | bytes 147464 | tf_op jit(solution)/shard_map/ppermute | solution.py:27

commit v7 on v6

--- a/solution.py
+++ b/solution.py
@@ -165,7 +165,7 @@
 
 def cg_kernel(
     columns, coef_ref, prev_ref, mine_ref, other_ref, gram_ref, factor_hbm, residual_hbm,
-    mttkrp, values, low, high, block, results, sems,
+    mttkrp, values, block, results, sems,
 ):
     days, width = prev_ref.shape
     total = mttkrp.shape[0]
@@ -180,23 +180,26 @@
                 row = (blocks + b - 1) * half
                 values[place, :] = source[row : row + half, :]
     gram_high, gram_wide = gram_ref[:, :width], gram_ref[...]
-    low[:PAD, :] = jnp.zeros((PAD, width), jnp.float32)
-    high[pl.ds(total, PAD), :] = jnp.zeros((PAD, width), jnp.float32)
+    blank = jnp.zeros((PAD, LANES), jnp.float32)
     coef = [coef_ref[:, l : l + 1] for l in range(LAGS)]
 
     def operate(v):
         v_high, v_low = split(v)
         both = product(jnp.concatenate([v_high, v_low], 0), gram_wide)
         mixed = both[:total, :width] + (both[total:, :width] + both[:total, width:])
-        low[pl.ds(PAD, total), :] = v
+        back = jnp.concatenate([smooth(v[:, t : t + LANES]) for t in range(0, width, LANES)], 1)
+        return mixed + smoothing * back
+
+    def smooth(v):
+        padded = jnp.concatenate([blank, v], 0)
         ahead = v
         for lag in range(1, LAGS + 1):
-            ahead = ahead - coef[lag - 1] * low[pl.ds(PAD - lag, total), :]
-        high[:total, :] = ahead
+            ahead = ahead - coef[lag - 1] * pltpu.roll(padded, lag, axis=0)[PAD:]
+        padded = jnp.concatenate([ahead, blank], 0)
         back = ahead
         for lag in range(1, LAGS + 1):
-            back = back - coef[lag - 1] * high[pl.ds(lag, total), :]
-        return mixed + smoothing * back
+            back = back - coef[lag - 1] * pltpu.roll(padded, total + PAD - lag, axis=0)[:total]
+        return back
 
     def inner(a, b):
         terms = a * b
@@ -251,8 +254,6 @@
         scratch_shapes=[
             pltpu.VMEM((total, width), jnp.float32),
             pltpu.VMEM((total, width), jnp.float32),
-            pltpu.VMEM((total + PAD, width), jnp.float32),
-            pltpu.VMEM((total + PAD, width), jnp.float32),
             pltpu.VMEM((4, total, width), jnp.float32),
             pltpu.VMEM((2, columns, days), jnp.float32),
             pltpu.SemaphoreType.DMA((2,)),

time: 22.6 us -> 22.4 us (level)
  no operation moved by 1% of the time
where the time goes in v7:
time: 22.4 us; the launch traced here: 22.2 us
  starting transfers between devices  9.94 us (44%)
  waiting for transfers between devices  6.92 us (31%)
  Pallas kernels  4.22 us (19%)
  between operations  0.68 us (3%)
  matrix products  0.34 us (2%)
    ppermute x7, starting transfers between devices, exchange(): return lax.ppermute(block, ('day', 'stu'), route)  9.94 us
    ppermute x7, waiting for transfers between devices, exchange(): return lax.ppermute(block, ('day', 'stu'), route)  6.92 us
    pallas_call x1, Pallas kernels, conjugate(): pl.pallas_call(functools.partial(cg_kernel, columns), compiler_params=plt...  1.8 us
    pallas_call x1, Pallas kernels, send_part(): pl.pallas_call(send_kernel, compiler_params=pltpu.CompilerParams(vmem_lim...  1.42 us
    pallas_call x1, Pallas kernels, keep_part(): pl.pallas_call(keep_kernel, compiler_params=pltpu.CompilerParams(vmem_lim...  0.78 us
  transfers between devices with their start and end apart: 7, of which 5 were waited for; matrix products, arithmetic and copies ran while one was open for 2% of the time, Pallas kernels for 5%

profile of v7, /device:TPU:0, one launch (start us, length us, event | category | flops | bytes accessed | tf_op | source)
XLA Modules:
  0.0 22.2 jit_solution(3911999074519229354)
XLA Ops:
  0.6 1.4 %shard_map.68 = (f32[16,256]{1,0:T(8,128)S(1)}, bf16[1024,256]{1,0:T(8,128)(2,1)S(1)}, bf16[128,1024]{1,0:T(8,128)(2,1)S(1)}, bf16[8,256]{1,0:T(8,128)(2,1)S(1)}) custom-call(bf16[256,1024]{1,0:T(8,128)(2,1)} %bitcast.6, bf16[1024,256]{1,0:T(8,128)(2,1)} %skill_hbm.1, bf16[8,256]{1,0:T(8,128)(2,1)} %student_hbm.1), custom_call_target="tpu_custom_call" | custom-call | flops 67108864 | bytes 1048576 | tf_op jit(solution)/shard_map/pallas_call | solution.py:82
  2.1 0.5 %collective-permute-start = (f32[16,256]{1,0:T(8,128)S(1)}, f32[16,256]{1,0:T(8,128)S(1)}, u32[]{:S(2)}, u32[]{:S(2)}) collective-permute-start(f32[16,256]{1,0:T(8,128)S(1)} %get-tuple-element.19), channel_id=1, source_target_pairs={{0,1},{1,0},{2,3},{3,2},{4,5},{5,4},{6,7},{7,6},{8,9},{9,8},{10,11... | collective-permute-start | bytes 49160 | tf_op jit(solution)/shard_map/ppermute | solution.py:27
  2.6 0.8 %shard_map.69 = (f32[24,256]{1,0:T(8,128)S(1)}, f32[32,256]{1,0:T(8,128)S(1)}, f32[1,7]{1,0:T(1,128)S(1)}) custom-call(bf16[128,1024]{1,0:T(8,128)(2,1)S(1)} %get-tuple-element.13.perf, bf16[1024,256]{1,0:T(8,128)(2,1)S(1)} %get-tuple-element.14.skill, bf16[8,256]{1,0:T(8,128)(2,1)S(1)} %get-tuple-element.15.student, f32[32,256]{1,0:T(8,128)} %prev_hbm.1, ...), custom_call_target="tpu_custom_call" | custom-call | flops 67108864 | bytes 786432 | tf_op jit(solution)/shard_map/pallas_call | solution.py:122
  3.4 0.0 collective-permute-done
  3.4 3.8 %collective-permute-start.1 = (f32[24,256]{1,0:T(8,128)S(1)}, f32[24,256]{1,0:T(8,128)S(1)}, u32[]{:S(2)}, u32[]{:S(2)}) collective-permute-start(f32[24,256]{1,0:T(8,128)S(1)} %pad_maximum_fusion.5), channel_id=1, source_target_pairs={{0,9},{1,8},{2,11},{3,10},{4,13},{5,12},{6,15},{7,14},{8,1},{9,0},... | collective-permute-start | bytes 73736 | tf_op jit(solution)/shard_map/ppermute | solution.py:27
  7.2 0.3 %fusion.1.skill_gram_ref = f32[256,256]{1,0:T(8,128)S(1)} fusion(bf16[1024,256]{1,0:T(8,128)(2,1)S(1)} %get-tuple-element.14.skill), kind=kOutput, calls=%fused_computation.12 | convolution fusion | flops 134217728 | bytes 786432 | tf_op jit(solution)/shard_map/dot_general | solution.py:280
  7.5 1.2 %collective-permute-done.1 = f32[24,256]{1,0:T(8,128)S(1)} collective-permute-done((f32[24,256]{1,0:T(8,128)S(1)}, f32[24,256]{1,0:T(8,128)S(1)}, u32[]{:S(2)}, u32[]{:S(2)}) %collective-permute-start.1) | collective-permute-done | bytes 24608 | tf_op jit(solution)/shard_map/ppermute | solution.py:27
  8.7 1.7 %collective-permute-start.2 = (f32[32,256]{1,0:T(8,128)S(1)}, f32[32,256]{1,0:T(8,128)S(1)}, u32[]{:S(2)}, u32[]{:S(2)}) collective-permute-start(f32[32,256]{1,0:T(8,128)S(1)} %pad_maximum_fusion.3), channel_id=1, source_target_pairs={{0,5},{1,2},{2,1},{3,6},{4,7},{5,0},{6,3},{7,4},{8,13},{9,10},{10,... | collective-permute-start | bytes 98312 | tf_op jit(solution)/shard_map/ppermute | solution.py:27
  10.4 1.7 %collective-permute-done.2 = f32[32,256]{1,0:T(8,128)S(1)} collective-permute-done((f32[32,256]{1,0:T(8,128)S(1)}, f32[32,256]{1,0:T(8,128)S(1)}, u32[]{:S(2)}, u32[]{:S(2)}) %collective-permute-start.2) | collective-permute-done | bytes 32800 | tf_op jit(solution)/shard_map/ppermute | solution.py:27
  12.1 1.6 %collective-permute-start.3 = (f32[48,256]{1,0:T(8,128)S(1)}, f32[48,256]{1,0:T(8,128)S(1)}, u32[]{:S(2)}, u32[]{:S(2)}) collective-permute-start(f32[48,256]{1,0:T(8,128)S(1)} %pad_maximum_fusion.1), channel_id=1, source_target_pairs={{0,3},{1,4},{2,7},{3,0},{4,1},{5,6},{6,5},{7,2},{8,11},{9,12},{10,... | collective-permute-start | bytes 147464 | tf_op jit(solution)/shard_map/ppermute | solution.py:27
  13.7 2.0 %collective-permute-done.3 = f32[48,256]{1,0:T(8,128)S(1)} collective-permute-done((f32[48,256]{1,0:T(8,128)S(1)}, f32[48,256]{1,0:T(8,128)S(1)}, u32[]{:S(2)}, u32[]{:S(2)}) %collective-permute-start.3) | collective-permute-done | bytes 49184 | tf_op jit(solution)/shard_map/ppermute | solution.py:27
  15.7 1.6 %collective-permute-start.4 = (f32[32,256]{1,0:T(8,128)S(1)}, f32[32,256]{1,0:T(8,128)S(1)}, u32[]{:S(2)}, u32[]{:S(2)}) collective-permute-start(f32[32,256]{1,0:T(8,128)S(1)} %pad_maximum_fusion.4), channel_id=1, source_target_pairs={{0,17},{1,16},{2,19},{3,18},{4,21},{5,20},{6,23},{7,22},{8,25},{9,... | collective-permute-start | bytes 98312 | tf_op jit(solution)/shard_map/ppermute | solution.py:27
  17.4 0.4 %collective-permute-start.6 = (f32[64,256]{1,0:T(8,128)S(1)}, f32[64,256]{1,0:T(8,128)S(1)}, u32[]{:S(2)}, u32[]{:S(2)}) collective-permute-start(f32[64,256]{1,0:T(8,128)S(1)} %pad_maximum_fusion.mine_ref), channel_id=1, source_target_pairs={{0,1},{1,0},{2,3},{3,2},{4,5},{5,4},{6,7},{7,6},{8,9},{9,8},{10,11... | collective-permute-start | bytes 196616 | tf_op jit(solution)/shard_map/ppermute | solution.py:27
  17.8 1.3 %collective-permute-done.4 = f32[32,256]{1,0:T(8,128)S(1)} collective-permute-done((f32[32,256]{1,0:T(8,128)S(1)}, f32[32,256]{1,0:T(8,128)S(1)}, u32[]{:S(2)}, u32[]{:S(2)}) %collective-permute-start.4) | collective-permute-done | bytes 32800 | tf_op jit(solution)/shard_map/ppermute | solution.py:27
  19.1 0.3 %collective-permute-start.5 = (f32[48,256]{1,0:T(8,128)S(1)}, f32[48,256]{1,0:T(8,128)S(1)}, u32[]{:S(2)}, u32[]{:S(2)}) collective-permute-start(f32[48,256]{1,0:T(8,128)S(1)} %pad_maximum_fusion.2.mine_ref), channel_id=1, source_target_pairs={{0,1},{1,0},{2,3},{3,2},{4,5},{5,4},{6,7},{7,6},{8,9},{9,8},{10,11... | collective-permute-start | bytes 147464 | tf_op jit(solution)/shard_map/ppermute | solution.py:27
  19.5 0.0 collective-permute-done.6.other_ref
  19.5 0.2 shard_map.70.gram_ref
  19.7 0.7 %collective-permute-done.5.other_ref = f32[48,256]{1,0:T(8,128)S(1)} collective-permute-done((f32[48,256]{1,0:T(8,128)S(1)}, f32[48,256]{1,0:T(8,128)S(1)}, u32[]{:S(2)}, u32[]{:S(2)}) %collective-permute-start.5) | collective-permute-done | bytes 49184 | tf_op jit(solution)/shard_map/ppermute | solution.py:27
  20.4 1.8 %shard_map.71 = (f32[16,32]{1,0:T(8,128)}, f32[16,32]{1,0:T(8,128)}) custom-call(f32[1,7]{1,0:T(1,128)S(1)} %get-tuple-element.16.coef_ref, f32[32,256]{1,0:T(8,128)S(1)} %get-tuple-element.17.prev_ref, f32[48,256]{1,0:T(8,128)S(1)} %pad_maximum_fusion.2.mine_ref, f32[48,256]{1,0:T(8,128)S(1)} %collective-permute-done.5.other_ref, ...), custom_call_target="tpu_custom_call" | custom-call | flops 100663296 | bytes 393216 | tf_op jit(solution)/shard_map/pallas_call | solution.py:248
  (14 shorter events, 0.1 us)
Async XLA Ops:
  2.1 1.4 %collective-permute-start = (f32[16,256]{1,0:T(8,128)S(1)}, f32[16,256]{1,0:T(8,128)S(1)}, u32[]{:S(2)}, u32[]{:S(2)}) collective-permute-start(f32[16,256]{1,0:T(8,128)S(1)} %get-tuple-element.19), channel_id=1, source_target_pairs={{0,1},{1,0},{2,3},{3,2},{4,5},{5,4},{6,7},{7,6},{8,9},{9,8},{10,11... | collective-permute-start | bytes 49160 | tf_op jit(solution)/shard_map/ppermute | solution.py:27
  3.4 5.3 %collective-permute-start.1 = (f32[24,256]{1,0:T(8,128)S(1)}, f32[24,256]{1,0:T(8,128)S(1)}, u32[]{:S(2)}, u32[]{:S(2)}) collective-permute-start(f32[24,256]{1,0:T(8,128)S(1)} %pad_maximum_fusion.5), channel_id=1, source_target_pairs={{0,9},{1,8},{2,11},{3,10},{4,13},{5,12},{6,15},{7,14},{8,1},{9,0},... | collective-permute-start | bytes 73736 | tf_op jit(solution)/shard_map/ppermute | solution.py:27
  8.7 3.4 %collective-permute-start.2 = (f32[32,256]{1,0:T(8,128)S(1)}, f32[32,256]{1,0:T(8,128)S(1)}, u32[]{:S(2)}, u32[]{:S(2)}) collective-permute-start(f32[32,256]{1,0:T(8,128)S(1)} %pad_maximum_fusion.3), channel_id=1, source_target_pairs={{0,5},{1,2},{2,1},{3,6},{4,7},{5,0},{6,3},{7,4},{8,13},{9,10},{10,... | collective-permute-start | bytes 98312 | tf_op jit(solution)/shard_map/ppermute | solution.py:27
  12.1 3.6 %collective-permute-start.3 = (f32[48,256]{1,0:T(8,128)S(1)}, f32[48,256]{1,0:T(8,128)S(1)}, u32[]{:S(2)}, u32[]{:S(2)}) collective-permute-start(f32[48,256]{1,0:T(8,128)S(1)} %pad_maximum_fusion.1), channel_id=1, source_target_pairs={{0,3},{1,4},{2,7},{3,0},{4,1},{5,6},{6,5},{7,2},{8,11},{9,12},{10,... | collective-permute-start | bytes 147464 | tf_op jit(solution)/shard_map/ppermute | solution.py:27
  15.7 3.4 %collective-permute-start.4 = (f32[32,256]{1,0:T(8,128)S(1)}, f32[32,256]{1,0:T(8,128)S(1)}, u32[]{:S(2)}, u32[]{:S(2)}) collective-permute-start(f32[32,256]{1,0:T(8,128)S(1)} %pad_maximum_fusion.4), channel_id=1, source_target_pairs={{0,17},{1,16},{2,19},{3,18},{4,21},{5,20},{6,23},{7,22},{8,25},{9,... | collective-permute-start | bytes 98312 | tf_op jit(solution)/shard_map/ppermute | solution.py:27
  17.4 2.1 %collective-permute-start.6 = (f32[64,256]{1,0:T(8,128)S(1)}, f32[64,256]{1,0:T(8,128)S(1)}, u32[]{:S(2)}, u32[]{:S(2)}) collective-permute-start(f32[64,256]{1,0:T(8,128)S(1)} %pad_maximum_fusion.mine_ref), channel_id=1, source_target_pairs={{0,1},{1,0},{2,3},{3,2},{4,5},{5,4},{6,7},{7,6},{8,9},{9,8},{10,11... | collective-permute-start | bytes 196616 | tf_op jit(solution)/shard_map/ppermute | solution.py:27
  19.1 1.2 %collective-permute-start.5 = (f32[48,256]{1,0:T(8,128)S(1)}, f32[48,256]{1,0:T(8,128)S(1)}, u32[]{:S(2)}, u32[]{:S(2)}) collective-permute-start(f32[48,256]{1,0:T(8,128)S(1)} %pad_maximum_fusion.2.mine_ref), channel_id=1, source_target_pairs={{0,1},{1,0},{2,3},{3,2},{4,5},{5,4},{6,7},{7,6},{8,9},{9,8},{10,11... | collective-permute-start | bytes 147464 | tf_op jit(solution)/shard_map/ppermute | solution.py:27

commit v8 on v7

--- a/solution.py
+++ b/solution.py
@@ -49,7 +49,7 @@
     days = total.shape[0] // students
     for t in range(proj.shape[0]):
         lanes = slice(t * LANES, (t + 1) * LANES)
-        proj[t] = total[:, lanes]
+        proj[t, : total.shape[0], :] = total[:, lanes]
         terms = None
         for s in range(students):
             row = proj[t, pl.ds(s, days, stride=students), :] * wide[s : s + 1, lanes]
@@ -92,7 +92,7 @@
         out_specs=(VMEM,) * 4,
         scratch_shapes=[
             pltpu.VMEM((rows, skills), jnp.bfloat16),
-            pltpu.VMEM((rank // LANES, rows, LANES), jnp.float32),
+            pltpu.VMEM((rank // LANES, rows + students, LANES), jnp.float32),
             pltpu.SemaphoreType.DMA((4,)),
         ],
         cost_estimate=pl.CostEstimate(
@@ -129,7 +129,7 @@
         in_specs=[VMEM] * 3 + [HBM] * 2,
         out_specs=(VMEM,) * 3,
         scratch_shapes=[
-            pltpu.VMEM((rank // LANES, rows, LANES), jnp.float32),
+            pltpu.VMEM((rank // LANES, rows + students, LANES), jnp.float32),
             pltpu.SemaphoreType.DMA((2,)),
         ],
         cost_estimate=pl.CostEstimate(

time: 22.4 us -> 22.4 us (level)
  no operation moved by 1% of the time
where the time goes in v8:
time: 22.4 us; the launch traced here: 22.2 us
  starting transfers between devices  9.94 us (44%)
  waiting for transfers between devices  6.92 us (31%)
  Pallas kernels  4.23 us (19%)
  between operations  0.68 us (3%)
  matrix products  0.34 us (2%)
    ppermute x7, starting transfers between devices, exchange(): return lax.ppermute(block, ('day', 'stu'), route)  9.94 us
    ppermute x7, waiting for transfers between devices, exchange(): return lax.ppermute(block, ('day', 'stu'), route)  6.92 us
    pallas_call x1, Pallas kernels, conjugate(): pl.pallas_call(functools.partial(cg_kernel, columns), compiler_params=plt...  1.8 us
    pallas_call x1, Pallas kernels, send_part(): pl.pallas_call(send_kernel, compiler_params=pltpu.CompilerParams(vmem_lim...  1.42 us
    pallas_call x1, Pallas kernels, keep_part(): pl.pallas_call(keep_kernel, compiler_params=pltpu.CompilerParams(vmem_lim...  0.78 us
  transfers between devices with their start and end apart: 7, of which 5 were waited for; matrix products, arithmetic and copies ran while one was open for 2% of the time, Pallas kernels for 5%

profile of v8, /device:TPU:0, one launch (start us, length us, event | category | flops | bytes accessed | tf_op | source)
XLA Modules:
  0.0 22.2 jit_solution(15546798994348130490)
XLA Ops:
  0.6 1.4 %shard_map.68 = (f32[16,256]{1,0:T(8,128)S(1)}, bf16[1024,256]{1,0:T(8,128)(2,1)S(1)}, bf16[128,1024]{1,0:T(8,128)(2,1)S(1)}, bf16[8,256]{1,0:T(8,128)(2,1)S(1)}) custom-call(bf16[256,1024]{1,0:T(8,128)(2,1)} %bitcast.6, bf16[1024,256]{1,0:T(8,128)(2,1)} %skill_hbm.1, bf16[8,256]{1,0:T(8,128)(2,1)} %student_hbm.1), custom_call_target="tpu_custom_call" | custom-call | flops 67108864 | bytes 1048576 | tf_op jit(solution)/shard_map/pallas_call | solution.py:82
  2.1 0.5 %collective-permute-start = (f32[16,256]{1,0:T(8,128)S(1)}, f32[16,256]{1,0:T(8,128)S(1)}, u32[]{:S(2)}, u32[]{:S(2)}) collective-permute-start(f32[16,256]{1,0:T(8,128)S(1)} %get-tuple-element.19), channel_id=1, source_target_pairs={{0,1},{1,0},{2,3},{3,2},{4,5},{5,4},{6,7},{7,6},{8,9},{9,8},{10,11... | collective-permute-start | bytes 49160 | tf_op jit(solution)/shard_map/ppermute | solution.py:27
  2.6 0.8 %shard_map.69 = (f32[24,256]{1,0:T(8,128)S(1)}, f32[32,256]{1,0:T(8,128)S(1)}, f32[1,7]{1,0:T(1,128)S(1)}) custom-call(bf16[128,1024]{1,0:T(8,128)(2,1)S(1)} %get-tuple-element.13.perf, bf16[1024,256]{1,0:T(8,128)(2,1)S(1)} %get-tuple-element.14.skill, bf16[8,256]{1,0:T(8,128)(2,1)S(1)} %get-tuple-element.15.student, f32[32,256]{1,0:T(8,128)} %prev_hbm.1, ...), custom_call_target="tpu_custom_call" | custom-call | flops 67108864 | bytes 786432 | tf_op jit(solution)/shard_map/pallas_call | solution.py:122
  3.4 0.0 collective-permute-done
  3.4 3.8 %collective-permute-start.1 = (f32[24,256]{1,0:T(8,128)S(1)}, f32[24,256]{1,0:T(8,128)S(1)}, u32[]{:S(2)}, u32[]{:S(2)}) collective-permute-start(f32[24,256]{1,0:T(8,128)S(1)} %pad_maximum_fusion.5), channel_id=1, source_target_pairs={{0,9},{1,8},{2,11},{3,10},{4,13},{5,12},{6,15},{7,14},{8,1},{9,0},... | collective-permute-start | bytes 73736 | tf_op jit(solution)/shard_map/ppermute | solution.py:27
  7.2 0.3 %fusion.1.skill_gram_ref = f32[256,256]{1,0:T(8,128)S(1)} fusion(bf16[1024,256]{1,0:T(8,128)(2,1)S(1)} %get-tuple-element.14.skill), kind=kOutput, calls=%fused_computation.12 | convolution fusion | flops 134217728 | bytes 786432 | tf_op jit(solution)/shard_map/dot_general | solution.py:280
  7.5 1.2 %collective-permute-done.1 = f32[24,256]{1,0:T(8,128)S(1)} collective-permute-done((f32[24,256]{1,0:T(8,128)S(1)}, f32[24,256]{1,0:T(8,128)S(1)}, u32[]{:S(2)}, u32[]{:S(2)}) %collective-permute-start.1) | collective-permute-done | bytes 24608 | tf_op jit(solution)/shard_map/ppermute | solution.py:27
  8.7 1.7 %collective-permute-start.2 = (f32[32,256]{1,0:T(8,128)S(1)}, f32[32,256]{1,0:T(8,128)S(1)}, u32[]{:S(2)}, u32[]{:S(2)}) collective-permute-start(f32[32,256]{1,0:T(8,128)S(1)} %pad_maximum_fusion.3), channel_id=1, source_target_pairs={{0,5},{1,2},{2,1},{3,6},{4,7},{5,0},{6,3},{7,4},{8,13},{9,10},{10,... | collective-permute-start | bytes 98312 | tf_op jit(solution)/shard_map/ppermute | solution.py:27
  10.4 1.7 %collective-permute-done.2 = f32[32,256]{1,0:T(8,128)S(1)} collective-permute-done((f32[32,256]{1,0:T(8,128)S(1)}, f32[32,256]{1,0:T(8,128)S(1)}, u32[]{:S(2)}, u32[]{:S(2)}) %collective-permute-start.2) | collective-permute-done | bytes 32800 | tf_op jit(solution)/shard_map/ppermute | solution.py:27
  12.1 1.6 %collective-permute-start.3 = (f32[48,256]{1,0:T(8,128)S(1)}, f32[48,256]{1,0:T(8,128)S(1)}, u32[]{:S(2)}, u32[]{:S(2)}) collective-permute-start(f32[48,256]{1,0:T(8,128)S(1)} %pad_maximum_fusion.1), channel_id=1, source_target_pairs={{0,3},{1,4},{2,7},{3,0},{4,1},{5,6},{6,5},{7,2},{8,11},{9,12},{10,... | collective-permute-start | bytes 147464 | tf_op jit(solution)/shard_map/ppermute | solution.py:27
  13.7 2.0 %collective-permute-done.3 = f32[48,256]{1,0:T(8,128)S(1)} collective-permute-done((f32[48,256]{1,0:T(8,128)S(1)}, f32[48,256]{1,0:T(8,128)S(1)}, u32[]{:S(2)}, u32[]{:S(2)}) %collective-permute-start.3) | collective-permute-done | bytes 49184 | tf_op jit(solution)/shard_map/ppermute | solution.py:27
  15.7 1.6 %collective-permute-start.4 = (f32[32,256]{1,0:T(8,128)S(1)}, f32[32,256]{1,0:T(8,128)S(1)}, u32[]{:S(2)}, u32[]{:S(2)}) collective-permute-start(f32[32,256]{1,0:T(8,128)S(1)} %pad_maximum_fusion.4), channel_id=1, source_target_pairs={{0,17},{1,16},{2,19},{3,18},{4,21},{5,20},{6,23},{7,22},{8,25},{9,... | collective-permute-start | bytes 98312 | tf_op jit(solution)/shard_map/ppermute | solution.py:27
  17.4 0.4 %collective-permute-start.6 = (f32[64,256]{1,0:T(8,128)S(1)}, f32[64,256]{1,0:T(8,128)S(1)}, u32[]{:S(2)}, u32[]{:S(2)}) collective-permute-start(f32[64,256]{1,0:T(8,128)S(1)} %pad_maximum_fusion.mine_ref), channel_id=1, source_target_pairs={{0,1},{1,0},{2,3},{3,2},{4,5},{5,4},{6,7},{7,6},{8,9},{9,8},{10,11... | collective-permute-start | bytes 196616 | tf_op jit(solution)/shard_map/ppermute | solution.py:27
  17.8 1.3 %collective-permute-done.4 = f32[32,256]{1,0:T(8,128)S(1)} collective-permute-done((f32[32,256]{1,0:T(8,128)S(1)}, f32[32,256]{1,0:T(8,128)S(1)}, u32[]{:S(2)}, u32[]{:S(2)}) %collective-permute-start.4) | collective-permute-done | bytes 32800 | tf_op jit(solution)/shard_map/ppermute | solution.py:27
  19.1 0.3 %collective-permute-start.5 = (f32[48,256]{1,0:T(8,128)S(1)}, f32[48,256]{1,0:T(8,128)S(1)}, u32[]{:S(2)}, u32[]{:S(2)}) collective-permute-start(f32[48,256]{1,0:T(8,128)S(1)} %pad_maximum_fusion.2.mine_ref), channel_id=1, source_target_pairs={{0,1},{1,0},{2,3},{3,2},{4,5},{5,4},{6,7},{7,6},{8,9},{9,8},{10,11... | collective-permute-start | bytes 147464 | tf_op jit(solution)/shard_map/ppermute | solution.py:27
  19.5 0.0 collective-permute-done.6.other_ref
  19.5 0.2 shard_map.70.gram_ref
  19.7 0.7 %collective-permute-done.5.other_ref = f32[48,256]{1,0:T(8,128)S(1)} collective-permute-done((f32[48,256]{1,0:T(8,128)S(1)}, f32[48,256]{1,0:T(8,128)S(1)}, u32[]{:S(2)}, u32[]{:S(2)}) %collective-permute-start.5) | collective-permute-done | bytes 49184 | tf_op jit(solution)/shard_map/ppermute | solution.py:27
  20.4 1.8 %shard_map.71 = (f32[16,32]{1,0:T(8,128)}, f32[16,32]{1,0:T(8,128)}) custom-call(f32[1,7]{1,0:T(1,128)S(1)} %get-tuple-element.16.coef_ref, f32[32,256]{1,0:T(8,128)S(1)} %get-tuple-element.17.prev_ref, f32[48,256]{1,0:T(8,128)S(1)} %pad_maximum_fusion.2.mine_ref, f32[48,256]{1,0:T(8,128)S(1)} %collective-permute-done.5.other_ref, ...), custom_call_target="tpu_custom_call" | custom-call | flops 100663296 | bytes 393216 | tf_op jit(solution)/shard_map/pallas_call | solution.py:248
  (14 shorter events, 0.1 us)
Async XLA Ops:
  2.1 1.4 %collective-permute-start = (f32[16,256]{1,0:T(8,128)S(1)}, f32[16,256]{1,0:T(8,128)S(1)}, u32[]{:S(2)}, u32[]{:S(2)}) collective-permute-start(f32[16,256]{1,0:T(8,128)S(1)} %get-tuple-element.19), channel_id=1, source_target_pairs={{0,1},{1,0},{2,3},{3,2},{4,5},{5,4},{6,7},{7,6},{8,9},{9,8},{10,11... | collective-permute-start | bytes 49160 | tf_op jit(solution)/shard_map/ppermute | solution.py:27
  3.4 5.3 %collective-permute-start.1 = (f32[24,256]{1,0:T(8,128)S(1)}, f32[24,256]{1,0:T(8,128)S(1)}, u32[]{:S(2)}, u32[]{:S(2)}) collective-permute-start(f32[24,256]{1,0:T(8,128)S(1)} %pad_maximum_fusion.5), channel_id=1, source_target_pairs={{0,9},{1,8},{2,11},{3,10},{4,13},{5,12},{6,15},{7,14},{8,1},{9,0},... | collective-permute-start | bytes 73736 | tf_op jit(solution)/shard_map/ppermute | solution.py:27
  8.7 3.4 %collective-permute-start.2 = (f32[32,256]{1,0:T(8,128)S(1)}, f32[32,256]{1,0:T(8,128)S(1)}, u32[]{:S(2)}, u32[]{:S(2)}) collective-permute-start(f32[32,256]{1,0:T(8,128)S(1)} %pad_maximum_fusion.3), channel_id=1, source_target_pairs={{0,5},{1,2},{2,1},{3,6},{4,7},{5,0},{6,3},{7,4},{8,13},{9,10},{10,... | collective-permute-start | bytes 98312 | tf_op jit(solution)/shard_map/ppermute | solution.py:27
  12.1 3.6 %collective-permute-start.3 = (f32[48,256]{1,0:T(8,128)S(1)}, f32[48,256]{1,0:T(8,128)S(1)}, u32[]{:S(2)}, u32[]{:S(2)}) collective-permute-start(f32[48,256]{1,0:T(8,128)S(1)} %pad_maximum_fusion.1), channel_id=1, source_target_pairs={{0,3},{1,4},{2,7},{3,0},{4,1},{5,6},{6,5},{7,2},{8,11},{9,12},{10,... | collective-permute-start | bytes 147464 | tf_op jit(solution)/shard_map/ppermute | solution.py:27
  15.7 3.4 %collective-permute-start.4 = (f32[32,256]{1,0:T(8,128)S(1)}, f32[32,256]{1,0:T(8,128)S(1)}, u32[]{:S(2)}, u32[]{:S(2)}) collective-permute-start(f32[32,256]{1,0:T(8,128)S(1)} %pad_maximum_fusion.4), channel_id=1, source_target_pairs={{0,17},{1,16},{2,19},{3,18},{4,21},{5,20},{6,23},{7,22},{8,25},{9,... | collective-permute-start | bytes 98312 | tf_op jit(solution)/shard_map/ppermute | solution.py:27
  17.4 2.1 %collective-permute-start.6 = (f32[64,256]{1,0:T(8,128)S(1)}, f32[64,256]{1,0:T(8,128)S(1)}, u32[]{:S(2)}, u32[]{:S(2)}) collective-permute-start(f32[64,256]{1,0:T(8,128)S(1)} %pad_maximum_fusion.mine_ref), channel_id=1, source_target_pairs={{0,1},{1,0},{2,3},{3,2},{4,5},{5,4},{6,7},{7,6},{8,9},{9,8},{10,11... | collective-permute-start | bytes 196616 | tf_op jit(solution)/shard_map/ppermute | solution.py:27
  19.1 1.2 %collective-permute-start.5 = (f32[48,256]{1,0:T(8,128)S(1)}, f32[48,256]{1,0:T(8,128)S(1)}, u32[]{:S(2)}, u32[]{:S(2)}) collective-permute-start(f32[48,256]{1,0:T(8,128)S(1)} %pad_maximum_fusion.2.mine_ref), channel_id=1, source_target_pairs={{0,1},{1,0},{2,3},{3,2},{4,5},{5,4},{6,7},{7,6},{8,9},{9,8},{10,11... | collective-permute-start | bytes 147464 | tf_op jit(solution)/shard_map/ppermute | solution.py:27

commit v9 on v8

--- a/solution.py
+++ b/solution.py
@@ -138,8 +138,8 @@
     )(perf, skill, student, *(pltpu.with_memory_space_constraint(x, pltpu.HBM) for x in small))
 
 
-def gram_kernel(mine_ref, other_ref, skill_gram_ref, out_ref):
-    students = jnp.concatenate([mine_ref[...], other_ref[...]], 0).astype(jnp.bfloat16)
+def gram_kernel(first, mine_ref, early_ref, late_ref, skill_gram_ref, out_ref):
+    students = jnp.concatenate([mine_ref[...], early_ref[...], late_ref[first:, :]], 0).astype(jnp.bfloat16)
     student_gram = lax.dot_general(
         students, students, (((0,), (0,)), ((), ())), preferred_element_type=jnp.float32
     )
@@ -149,36 +149,36 @@
     out_ref[:, rank:] = low
 
 
-def gram_stack(mine, other, skill_gram):
+def gram_stack(first, mine, early, late, skill_gram):
     count, rank = mine.shape
     return pl.pallas_call(
-        gram_kernel,
+        functools.partial(gram_kernel, first),
         compiler_params=pltpu.CompilerParams(vmem_limit_bytes=VMEM_BYTES),
         out_shape=jax.ShapeDtypeStruct((rank, 2 * rank), jnp.bfloat16),
-        in_specs=[VMEM] * 3,
+        in_specs=[VMEM] * 4,
         out_specs=VMEM,
         cost_estimate=pl.CostEstimate(
             flops=4 * count * rank * rank, bytes_accessed=8 * rank * rank, transcendentals=0
         ),
-    )(mine, other, skill_gram)
+    )(mine, early, late, skill_gram)
 
 
 def cg_kernel(
-    columns, coef_ref, prev_ref, mine_ref, other_ref, gram_ref, factor_hbm, residual_hbm,
+    columns, coef_ref, prev_ref, mine_ref, core_ref, far_ref, cross_ref, gram_ref, factor_hbm, residual_hbm,
     mttkrp, values, block, results, sems,
 ):
     days, width = prev_ref.shape
     total = mttkrp.shape[0]
-    blocks, half = total // days, days // 2
+    near, half = total // days // 2, days // 2
     day, stu, part = lax.axis_index("day"), lax.axis_index("stu"), own_part()
     values[pl.ds(pl.multiple_of(day * days, days), days), :] = prev_ref[...]
-    for source, at in ((mine_ref, part), (other_ref, 1 - part)):
-        for b in range(blocks):
+    for at, near_ref, away_ref in ((part, mine_ref, far_ref), (1 - part, core_ref, cross_ref)):
+        for b in range(2 * near):
+            source, row, step = (near_ref, b, near - 1) if b < near else (away_ref, b - near, near)
             place = pl.ds(pl.multiple_of((day ^ b) * days + at * half, half), half)
-            mttkrp[place, :] = source[b * half : (b + 1) * half, :]
+            mttkrp[place, :] = source[row * half : (row + 1) * half, :]
             if b > 0:
-                row = (blocks + b - 1) * half
-                values[place, :] = source[row : row + half, :]
+                values[place, :] = source[(row + step) * half : (row + step + 1) * half, :]
     gram_high, gram_wide = gram_ref[:, :width], gram_ref[...]
     blank = jnp.zeros((PAD, LANES), jnp.float32)
     coef = [coef_ref[:, l : l + 1] for l in range(LAGS)]
@@ -241,15 +241,15 @@
         copy.wait()
 
 
-def conjugate(coef, prev, mine, other, gram, blocks, columns):
+def conjugate(coef, prev, mine, core, far, cross, gram, columns):
     days, width = prev.shape
-    total = days * blocks
+    total = 2 * far.shape[0]
     shape = jax.ShapeDtypeStruct((columns, days), jnp.float32)
     return pl.pallas_call(
         functools.partial(cg_kernel, columns),
         compiler_params=pltpu.CompilerParams(vmem_limit_bytes=VMEM_BYTES),
         out_shape=(shape, shape),
-        in_specs=[VMEM] * 5,
+        in_specs=[VMEM] * 7,
         out_specs=(HBM, HBM),
         scratch_shapes=[
             pltpu.VMEM((total, width), jnp.float32),
@@ -261,7 +261,7 @@
         cost_estimate=pl.CostEstimate(
             flops=24 * total * width * width, bytes_accessed=4 * width * (width + 2 * total), transcendentals=0
         ),
-    )(coef, prev, mine, other, gram)
+    )(coef, prev, mine, core, far, cross, gram)
 
 
 def bits_of(count):
@@ -282,20 +282,25 @@
     masks = [bit | 1 for bit in bits_of(stu_size)[:0:-1]]
     for mask, other in zip(masks, masks[:-2] + masks[:-3:-1], strict=True):
         got = exchange(payload, mask, other)
+        if mask == masks[-1]:
+            early = exchange(payload[half:], 1)
         if mask == masks[0]:
             got, skill_gram = lax.optimization_barrier((got, skill_gram))
         payload = jnp.concatenate([payload[:half] + got[:half], payload[half:], got[half:]], 0)
-    mttkrp, students = payload[:half], payload[half:]
+    mttkrp, students, late = payload[:half], payload[half:], got[half:]
     factor = lax.dynamic_slice_in_dim(day_prev, own_part() * half, half, 0)
-    for bit in bits_of(day_size):
+    *bits, last = bits_of(day_size)
+    for bit in bits:
         got = exchange(jnp.concatenate([mttkrp, factor], 0), bit * stu_size + 1)
         rows = bit * half
         mttkrp = jnp.concatenate([mttkrp, got[:rows]], 0)
         factor = jnp.concatenate([factor, got[rows:]], 0)
-    stack = gram_stack(students, exchange(students, 1), skill_gram)
-    mine = jnp.concatenate([mttkrp, factor[half:]], 0)
-    other = exchange(mine, 1)
-    factor, residual = conjugate(coef, day_prev, mine, other, stack, day_size, rank // stu_size)
+    mine = jnp.concatenate([mttkrp, factor[half:], late], 0)
+    far = exchange(jnp.concatenate([mttkrp, factor], 0), last * stu_size + 1)
+    core = exchange(mine, 1)
+    stack = gram_stack(mine.shape[0] - late.shape[0], students, early, core, skill_gram)
+    cross = exchange(far, 1)
+    factor, residual = conjugate(coef, day_prev, mine, core, far, cross, stack, rank // stu_size)
     return factor.T, residual.T
 
 

time: 22.4 us -> 22.3 us (level)
  waiting for transfers between devices: 6.92 us -> 6.42 us
  starting transfers between devices: 9.94 us -> 10.4 us
    ppermute x7 -> x8, waiting for transfers between devices: 6.92 us -> 6.42 us  [exchange(): return lax.ppermute(block, ('day', 'stu'), route)]
    ppermute x7 -> x8, starting transfers between devices: 9.94 us -> 10.4 us  [exchange(): return lax.ppermute(block, ('day', 'stu'), route)]
  transfers between devices with their start and end apart: 7 -> 8, of which waited for: 5 -> 5; matrix products, arithmetic and copies ran while one was open for 2% -> 2% of each run, Pallas kernels for 5% -> 5%
where the time goes in v9:
time: 22.3 us; the launch traced here: 22.1 us
  starting transfers between devices  10.4 us (47%)
  waiting for transfers between devices  6.42 us (29%)
  Pallas kernels  4.23 us (19%)
  between operations  0.71 us (3%)
  matrix products  0.34 us (2%)
    ppermute x8, starting transfers between devices, exchange(): return lax.ppermute(block, ('day', 'stu'), route)  10.4 us
    ppermute x8, waiting for transfers between devices, exchange(): return lax.ppermute(block, ('day', 'stu'), route)  6.42 us
    pallas_call x1, Pallas kernels, conjugate(): pl.pallas_call(functools.partial(cg_kernel, columns), compiler_params=plt...  1.8 us
    pallas_call x1, Pallas kernels, send_part(): pl.pallas_call(send_kernel, compiler_params=pltpu.CompilerParams(vmem_lim...  1.42 us
    pallas_call x1, Pallas kernels, keep_part(): pl.pallas_call(keep_kernel, compiler_params=pltpu.CompilerParams(vmem_lim...  0.78 us
  transfers between devices with their start and end apart: 8, of which 5 were waited for; matrix products, arithmetic and copies ran while one was open for 2% of the time, Pallas kernels for 5%

profile of v9, /device:TPU:0, one launch (start us, length us, event | category | flops | bytes accessed | tf_op | source)
XLA Modules:
  0.0 22.1 jit_solution(1369399326644805510)
XLA Ops:
  0.6 1.4 %shard_map.68 = (f32[16,256]{1,0:T(8,128)S(1)}, bf16[1024,256]{1,0:T(8,128)(2,1)S(1)}, bf16[128,1024]{1,0:T(8,128)(2,1)S(1)}, bf16[8,256]{1,0:T(8,128)(2,1)S(1)}) custom-call(bf16[256,1024]{1,0:T(8,128)(2,1)} %bitcast.6, bf16[1024,256]{1,0:T(8,128)(2,1)} %skill_hbm.1, bf16[8,256]{1,0:T(8,128)(2,1)} %student_hbm.1), custom_call_target="tpu_custom_call" | custom-call | flops 67108864 | bytes 1048576 | tf_op jit(solution)/shard_map/pallas_call | solution.py:82
  2.1 0.5 %collective-permute-start = (f32[16,256]{1,0:T(8,128)S(1)}, f32[16,256]{1,0:T(8,128)S(1)}, u32[]{:S(2)}, u32[]{:S(2)}) collective-permute-start(f32[16,256]{1,0:T(8,128)S(1)} %get-tuple-element.19), channel_id=1, source_target_pairs={{0,1},{1,0},{2,3},{3,2},{4,5},{5,4},{6,7},{7,6},{8,9},{9,8},{10,11... | collective-permute-start | bytes 49160 | tf_op jit(solution)/shard_map/ppermute | solution.py:27
  2.6 0.8 %shard_map.69 = (f32[24,256]{1,0:T(8,128)S(1)}, f32[32,256]{1,0:T(8,128)S(1)}, f32[1,7]{1,0:T(1,128)S(1)}) custom-call(bf16[128,1024]{1,0:T(8,128)(2,1)S(1)} %get-tuple-element.13.perf, bf16[1024,256]{1,0:T(8,128)(2,1)S(1)} %get-tuple-element.14.skill, bf16[8,256]{1,0:T(8,128)(2,1)S(1)} %get-tuple-element.15.student, f32[32,256]{1,0:T(8,128)} %prev_hbm.1, ...), custom_call_target="tpu_custom_call" | custom-call | flops 67108864 | bytes 786432 | tf_op jit(solution)/shard_map/pallas_call | solution.py:122
  3.4 0.0 collective-permute-done
  3.4 3.8 %collective-permute-start.1 = (f32[24,256]{1,0:T(8,128)S(1)}, f32[24,256]{1,0:T(8,128)S(1)}, u32[]{:S(2)}, u32[]{:S(2)}) collective-permute-start(f32[24,256]{1,0:T(8,128)S(1)} %pad_maximum_fusion.6), channel_id=1, source_target_pairs={{0,9},{1,8},{2,11},{3,10},{4,13},{5,12},{6,15},{7,14},{8,1},{9,0},... | collective-permute-start | bytes 73736 | tf_op jit(solution)/shard_map/ppermute | solution.py:27
  7.2 0.3 %fusion.skill_gram_ref = f32[256,256]{1,0:T(8,128)S(1)} fusion(bf16[1024,256]{1,0:T(8,128)(2,1)S(1)} %get-tuple-element.14.skill), kind=kOutput, calls=%fused_computation.12 | convolution fusion | flops 134217728 | bytes 786432 | tf_op jit(solution)/shard_map/dot_general | solution.py:280
  7.5 1.2 %collective-permute-done.1 = f32[24,256]{1,0:T(8,128)S(1)} collective-permute-done((f32[24,256]{1,0:T(8,128)S(1)}, f32[24,256]{1,0:T(8,128)S(1)}, u32[]{:S(2)}, u32[]{:S(2)}) %collective-permute-start.1) | collective-permute-done | bytes 24608 | tf_op jit(solution)/shard_map/ppermute | solution.py:27
  8.7 1.7 %collective-permute-start.2 = (f32[32,256]{1,0:T(8,128)S(1)}, f32[32,256]{1,0:T(8,128)S(1)}, u32[]{:S(2)}, u32[]{:S(2)}) collective-permute-start(f32[32,256]{1,0:T(8,128)S(1)} %pad_maximum_fusion.3), channel_id=1, source_target_pairs={{0,5},{1,2},{2,1},{3,6},{4,7},{5,0},{6,3},{7,4},{8,13},{9,10},{10,... | collective-permute-start | bytes 98312 | tf_op jit(solution)/shard_map/ppermute | solution.py:27
  10.4 1.7 %collective-permute-done.2 = f32[32,256]{1,0:T(8,128)S(1)} collective-permute-done((f32[32,256]{1,0:T(8,128)S(1)}, f32[32,256]{1,0:T(8,128)S(1)}, u32[]{:S(2)}, u32[]{:S(2)}) %collective-permute-start.2) | collective-permute-done | bytes 32800 | tf_op jit(solution)/shard_map/ppermute | solution.py:27
  12.1 1.6 %collective-permute-start.3 = (f32[48,256]{1,0:T(8,128)S(1)}, f32[48,256]{1,0:T(8,128)S(1)}, u32[]{:S(2)}, u32[]{:S(2)}) collective-permute-start(f32[48,256]{1,0:T(8,128)S(1)} %pad_maximum_fusion.1), channel_id=1, source_target_pairs={{0,3},{1,4},{2,7},{3,0},{4,1},{5,6},{6,5},{7,2},{8,11},{9,12},{10,... | collective-permute-start | bytes 147464 | tf_op jit(solution)/shard_map/ppermute | solution.py:27
  13.7 0.4 %collective-permute-start.7 = (f32[32,256]{1,0:T(8,128)S(1)}, f32[32,256]{1,0:T(8,128)S(1)}, u32[]{:S(2)}, u32[]{:S(2)}) collective-permute-start(f32[32,256]{1,0:T(8,128)S(1)} %pad_maximum_fusion.5), channel_id=1, source_target_pairs={{0,1},{1,0},{2,3},{3,2},{4,5},{5,4},{6,7},{7,6},{8,9},{9,8},{10,11... | collective-permute-start | bytes 98312 | tf_op jit(solution)/shard_map/ppermute | solution.py:27
  14.2 1.5 %collective-permute-done.3 = f32[48,256]{1,0:T(8,128)S(1)} collective-permute-done((f32[48,256]{1,0:T(8,128)S(1)}, f32[48,256]{1,0:T(8,128)S(1)}, u32[]{:S(2)}, u32[]{:S(2)}) %collective-permute-start.3) | collective-permute-done | bytes 49184 | tf_op jit(solution)/shard_map/ppermute | solution.py:27
  15.7 1.6 %collective-permute-start.5 = (f32[32,256]{1,0:T(8,128)S(1)}, f32[32,256]{1,0:T(8,128)S(1)}, u32[]{:S(2)}, u32[]{:S(2)}) collective-permute-start(f32[32,256]{1,0:T(8,128)S(1)} %pad_maximum_fusion.4), channel_id=1, source_target_pairs={{0,17},{1,16},{2,19},{3,18},{4,21},{5,20},{6,23},{7,22},{8,25},{9,... | collective-permute-start | bytes 98312 | tf_op jit(solution)/shard_map/ppermute | solution.py:27
  17.4 0.4 %collective-permute-start.4 = (f32[48,256]{1,0:T(8,128)S(1)}, f32[48,256]{1,0:T(8,128)S(1)}, u32[]{:S(2)}, u32[]{:S(2)}) collective-permute-start(f32[48,256]{1,0:T(8,128)S(1)} %pad_maximum_fusion.2.mine_ref), channel_id=1, source_target_pairs={{0,1},{1,0},{2,3},{3,2},{4,5},{5,4},{6,7},{7,6},{8,9},{9,8},{10,11... | collective-permute-start | bytes 147464 | tf_op jit(solution)/shard_map/ppermute | solution.py:27
  17.8 1.3 %collective-permute-done.5.far_ref = f32[32,256]{1,0:T(8,128)S(1)} collective-permute-done((f32[32,256]{1,0:T(8,128)S(1)}, f32[32,256]{1,0:T(8,128)S(1)}, u32[]{:S(2)}, u32[]{:S(2)}) %collective-permute-start.5) | collective-permute-done | bytes 32800 | tf_op jit(solution)/shard_map/ppermute | solution.py:27
  19.1 0.3 %collective-permute-start.6 = (f32[32,256]{1,0:T(8,128)S(1)}, f32[32,256]{1,0:T(8,128)S(1)}, u32[]{:S(2)}, u32[]{:S(2)}) collective-permute-start(f32[32,256]{1,0:T(8,128)S(1)} %collective-permute-done.5.far_ref), channel_id=1, source_target_pairs={{0,1},{1,0},{2,3},{3,2},{4,5},{5,4},{6,7},{7,6},{8,9},{9,8},{10,11... | collective-permute-start | bytes 98312 | tf_op jit(solution)/shard_map/ppermute | solution.py:27
  19.5 0.0 collective-permute-done.7.early_ref
  19.5 0.0 collective-permute-done.4.late_ref.core_ref
  19.5 0.2 %shard_map.70.gram_ref = bf16[256,512]{1,0:T(8,128)(2,1)S(1)} custom-call(f32[64,256]{1,0:T(8,128)S(1)} %pad_maximum_fusion.mine_ref, f32[32,256]{1,0:T(8,128)S(1)} %collective-permute-done.7.early_ref, f32[48,256]{1,0:T(8,128)S(1)} %collective-permute-done.4.late_ref.core_ref, f32[256,256]{1,0:T(8,128)S(1)} %fusion.skill_gram_ref), custom_call_target="tpu_custom_call" | custom-call | flops 16777216 | bytes 524288 | tf_op jit(solution)/shard_map/pallas_call | solution.py:154
  19.7 0.6 %collective-permute-done.6.cross_ref = f32[32,256]{1,0:T(8,128)S(1)} collective-permute-done((f32[32,256]{1,0:T(8,128)S(1)}, f32[32,256]{1,0:T(8,128)S(1)}, u32[]{:S(2)}, u32[]{:S(2)}) %collective-permute-start.6) | collective-permute-done | bytes 32800 | tf_op jit(solution)/shard_map/ppermute | solution.py:27
  20.3 1.8 %shard_map.71 = (f32[16,32]{1,0:T(8,128)}, f32[16,32]{1,0:T(8,128)}) custom-call(f32[1,7]{1,0:T(1,128)S(1)} %get-tuple-element.16.coef_ref, f32[32,256]{1,0:T(8,128)S(1)} %get-tuple-element.17.prev_ref, f32[48,256]{1,0:T(8,128)S(1)} %pad_maximum_fusion.2.mine_ref, f32[48,256]{1,0:T(8,128)S(1)} %collective-permute-done.4.late_ref.core_ref, ...), custom_call_target="tpu_custom_call" | custom-call | flops 100663296 | bytes 393216 | tf_op jit(solution)/shard_map/pallas_call | solution.py:248
  (15 shorter events, 0.1 us)
Async XLA Ops:
  2.1 1.4 %collective-permute-start = (f32[16,256]{1,0:T(8,128)S(1)}, f32[16,256]{1,0:T(8,128)S(1)}, u32[]{:S(2)}, u32[]{:S(2)}) collective-permute-start(f32[16,256]{1,0:T(8,128)S(1)} %get-tuple-element.19), channel_id=1, source_target_pairs={{0,1},{1,0},{2,3},{3,2},{4,5},{5,4},{6,7},{7,6},{8,9},{9,8},{10,11... | collective-permute-start | bytes 49160 | tf_op jit(solution)/shard_map/ppermute | solution.py:27
  3.4 5.3 %collective-permute-start.1 = (f32[24,256]{1,0:T(8,128)S(1)}, f32[24,256]{1,0:T(8,128)S(1)}, u32[]{:S(2)}, u32[]{:S(2)}) collective-permute-start(f32[24,256]{1,0:T(8,128)S(1)} %pad_maximum_fusion.6), channel_id=1, source_target_pairs={{0,9},{1,8},{2,11},{3,10},{4,13},{5,12},{6,15},{7,14},{8,1},{9,0},... | collective-permute-start | bytes 73736 | tf_op jit(solution)/shard_map/ppermute | solution.py:27
  8.7 3.4 %collective-permute-start.2 = (f32[32,256]{1,0:T(8,128)S(1)}, f32[32,256]{1,0:T(8,128)S(1)}, u32[]{:S(2)}, u32[]{:S(2)}) collective-permute-start(f32[32,256]{1,0:T(8,128)S(1)} %pad_maximum_fusion.3), channel_id=1, source_target_pairs={{0,5},{1,2},{2,1},{3,6},{4,7},{5,0},{6,3},{7,4},{8,13},{9,10},{10,... | collective-permute-start | bytes 98312 | tf_op jit(solution)/shard_map/ppermute | solution.py:27
  12.1 3.6 %collective-permute-start.3 = (f32[48,256]{1,0:T(8,128)S(1)}, f32[48,256]{1,0:T(8,128)S(1)}, u32[]{:S(2)}, u32[]{:S(2)}) collective-permute-start(f32[48,256]{1,0:T(8,128)S(1)} %pad_maximum_fusion.1), channel_id=1, source_target_pairs={{0,3},{1,4},{2,7},{3,0},{4,1},{5,6},{6,5},{7,2},{8,11},{9,12},{10,... | collective-permute-start | bytes 147464 | tf_op jit(solution)/shard_map/ppermute | solution.py:27
  13.7 5.8 %collective-permute-start.7 = (f32[32,256]{1,0:T(8,128)S(1)}, f32[32,256]{1,0:T(8,128)S(1)}, u32[]{:S(2)}, u32[]{:S(2)}) collective-permute-start(f32[32,256]{1,0:T(8,128)S(1)} %pad_maximum_fusion.5), channel_id=1, source_target_pairs={{0,1},{1,0},{2,3},{3,2},{4,5},{5,4},{6,7},{7,6},{8,9},{9,8},{10,11... | collective-permute-start | bytes 98312 | tf_op jit(solution)/shard_map/ppermute | solution.py:27
  15.7 3.4 %collective-permute-start.5 = (f32[32,256]{1,0:T(8,128)S(1)}, f32[32,256]{1,0:T(8,128)S(1)}, u32[]{:S(2)}, u32[]{:S(2)}) collective-permute-start(f32[32,256]{1,0:T(8,128)S(1)} %pad_maximum_fusion.4), channel_id=1, source_target_pairs={{0,17},{1,16},{2,19},{3,18},{4,21},{5,20},{6,23},{7,22},{8,25},{9,... | collective-permute-start | bytes 98312 | tf_op jit(solution)/shard_map/ppermute | solution.py:27
  17.4 2.1 %collective-permute-start.4 = (f32[48,256]{1,0:T(8,128)S(1)}, f32[48,256]{1,0:T(8,128)S(1)}, u32[]{:S(2)}, u32[]{:S(2)}) collective-permute-start(f32[48,256]{1,0:T(8,128)S(1)} %pad_maximum_fusion.2.mine_ref), channel_id=1, source_target_pairs={{0,1},{1,0},{2,3},{3,2},{4,5},{5,4},{6,7},{7,6},{8,9},{9,8},{10,11... | collective-permute-start | bytes 147464 | tf_op jit(solution)/shard_map/ppermute | solution.py:27
  19.1 1.2 %collective-permute-start.6 = (f32[32,256]{1,0:T(8,128)S(1)}, f32[32,256]{1,0:T(8,128)S(1)}, u32[]{:S(2)}, u32[]{:S(2)}) collective-permute-start(f32[32,256]{1,0:T(8,128)S(1)} %collective-permute-done.5.far_ref), channel_id=1, source_target_pairs={{0,1},{1,0},{2,3},{3,2},{4,5},{5,4},{6,7},{7,6},{8,9},{9,8},{10,11... | collective-permute-start | bytes 98312 | tf_op jit(solution)/shard_map/ppermute | solution.py:27

commit v10 on v9

--- a/solution.py
+++ b/solution.py
@@ -165,20 +165,27 @@
 
 def cg_kernel(
     columns, coef_ref, prev_ref, mine_ref, core_ref, far_ref, cross_ref, gram_ref, factor_hbm, residual_hbm,
-    mttkrp, values, block, results, sems,
+    block, results, sems,
 ):
     days, width = prev_ref.shape
-    total = mttkrp.shape[0]
+    total = 2 * far_ref.shape[0]
     near, half = total // days // 2, days // 2
     day, stu, part = lax.axis_index("day"), lax.axis_index("stu"), own_part()
-    values[pl.ds(pl.multiple_of(day * days, days), days), :] = prev_ref[...]
-    for at, near_ref, away_ref in ((part, mine_ref, far_ref), (1 - part, core_ref, cross_ref)):
-        for b in range(2 * near):
-            source, row, step = (near_ref, b, near - 1) if b < near else (away_ref, b - near, near)
-            place = pl.ds(pl.multiple_of((day ^ b) * days + at * half, half), half)
-            mttkrp[place, :] = source[row * half : (row + 1) * half, :]
-            if b > 0:
-                values[place, :] = source[(row + step) * half : (row + step + 1) * half, :]
+    sums, starts = [], [prev_ref[...]]
+    for b in range(2 * near):
+        row, step = (b, near - 1) if b < near else (b - near, near)
+        pair = (mine_ref, core_ref) if b < near else (far_ref, cross_ref)
+        for into, at in ((sums, row), (starts, row + step)):
+            if into is sums or b > 0:
+                own, away = (source[at * half : (at + 1) * half, :] for source in pair)
+                flip = part == 1
+                into.append(jnp.concatenate([jnp.where(flip, away, own), jnp.where(flip, own, away)], 0))
+    for k in range((2 * near).bit_length() - 1):
+        flip = (day >> k) & 1 == 1
+        sums, starts = (
+            [jnp.where(flip, rows[d ^ (1 << k)], rows[d]) for d in range(2 * near)] for rows in (sums, starts)
+        )
+    mttkrp, values = jnp.concatenate(sums, 0), jnp.concatenate(starts, 0)
     gram_high, gram_wide = gram_ref[:, :width], gram_ref[...]
     blank = jnp.zeros((PAD, LANES), jnp.float32)
     coef = [coef_ref[:, l : l + 1] for l in range(LAGS)]
@@ -210,8 +217,8 @@
             tiles = [x + y for x, y in zip(tiles[::2], tiles[1::2], strict=True)]
         return jnp.sum(jnp.sum(tiles[0], axis=1, keepdims=True), axis=0, keepdims=True)
 
-    factor = values[...]
-    residual = mttkrp[...] - operate(factor)
+    factor = values
+    residual = mttkrp - operate(factor)
     start = pl.multiple_of(day * days, days)
     turn = jnp.where(stu == 0, 0, width - stu * columns)
 
@@ -252,8 +259,6 @@
         in_specs=[VMEM] * 7,
         out_specs=(HBM, HBM),
         scratch_shapes=[
-            pltpu.VMEM((total, width), jnp.float32),
-            pltpu.VMEM((total, width), jnp.float32),
             pltpu.VMEM((4, total, width), jnp.float32),
             pltpu.VMEM((2, columns, days), jnp.float32),
             pltpu.SemaphoreType.DMA((2,)),

time: 22.3 us -> 22.3 us (level)
  no operation moved by 1% of the time
where the time goes in v10:
time: 22.3 us; the launch traced here: 22.1 us
  starting transfers between devices  10.4 us (47%)
  waiting for transfers between devices  6.42 us (29%)
  Pallas kernels  4.23 us (19%)
  between operations  0.71 us (3%)
  matrix products  0.34 us (2%)
    ppermute x8, starting transfers between devices, exchange(): return lax.ppermute(block, ('day', 'stu'), route)  10.4 us
    ppermute x8, waiting for transfers between devices, exchange(): return lax.ppermute(block, ('day', 'stu'), route)  6.42 us
    pallas_call x1, Pallas kernels, conjugate(): pl.pallas_call(functools.partial(cg_kernel, columns), compiler_params=plt...  1.8 us
    pallas_call x1, Pallas kernels, send_part(): pl.pallas_call(send_kernel, compiler_params=pltpu.CompilerParams(vmem_lim...  1.42 us
    pallas_call x1, Pallas kernels, keep_part(): pl.pallas_call(keep_kernel, compiler_params=pltpu.CompilerParams(vmem_lim...  0.78 us
  transfers between devices with their start and end apart: 8, of which 5 were waited for; matrix products, arithmetic and copies ran while one was open for 2% of the time, Pallas kernels for 5%

profile of v10, /device:TPU:0, one launch (start us, length us, event | category | flops | bytes accessed | tf_op | source)
XLA Modules:
  0.0 22.1 jit_solution(2784386806660986545)
XLA Ops:
  0.6 1.4 %shard_map.68 = (f32[16,256]{1,0:T(8,128)S(1)}, bf16[1024,256]{1,0:T(8,128)(2,1)S(1)}, bf16[128,1024]{1,0:T(8,128)(2,1)S(1)}, bf16[8,256]{1,0:T(8,128)(2,1)S(1)}) custom-call(bf16[256,1024]{1,0:T(8,128)(2,1)} %bitcast.6, bf16[1024,256]{1,0:T(8,128)(2,1)} %skill_hbm.1, bf16[8,256]{1,0:T(8,128)(2,1)} %student_hbm.1), custom_call_target="tpu_custom_call" | custom-call | flops 67108864 | bytes 1048576 | tf_op jit(solution)/shard_map/pallas_call | solution.py:82
  2.1 0.5 %collective-permute-start = (f32[16,256]{1,0:T(8,128)S(1)}, f32[16,256]{1,0:T(8,128)S(1)}, u32[]{:S(2)}, u32[]{:S(2)}) collective-permute-start(f32[16,256]{1,0:T(8,128)S(1)} %get-tuple-element.19), channel_id=1, source_target_pairs={{0,1},{1,0},{2,3},{3,2},{4,5},{5,4},{6,7},{7,6},{8,9},{9,8},{10,11... | collective-permute-start | bytes 49160 | tf_op jit(solution)/shard_map/ppermute | solution.py:27
  2.6 0.8 %shard_map.69 = (f32[24,256]{1,0:T(8,128)S(1)}, f32[32,256]{1,0:T(8,128)S(1)}, f32[1,7]{1,0:T(1,128)S(1)}) custom-call(bf16[128,1024]{1,0:T(8,128)(2,1)S(1)} %get-tuple-element.13.perf, bf16[1024,256]{1,0:T(8,128)(2,1)S(1)} %get-tuple-element.14.skill, bf16[8,256]{1,0:T(8,128)(2,1)S(1)} %get-tuple-element.15.student, f32[32,256]{1,0:T(8,128)} %prev_hbm.1, ...), custom_call_target="tpu_custom_call" | custom-call | flops 67108864 | bytes 786432 | tf_op jit(solution)/shard_map/pallas_call | solution.py:122
  3.4 0.0 collective-permute-done
  3.4 3.8 %collective-permute-start.1 = (f32[24,256]{1,0:T(8,128)S(1)}, f32[24,256]{1,0:T(8,128)S(1)}, u32[]{:S(2)}, u32[]{:S(2)}) collective-permute-start(f32[24,256]{1,0:T(8,128)S(1)} %pad_maximum_fusion.6), channel_id=1, source_target_pairs={{0,9},{1,8},{2,11},{3,10},{4,13},{5,12},{6,15},{7,14},{8,1},{9,0},... | collective-permute-start | bytes 73736 | tf_op jit(solution)/shard_map/ppermute | solution.py:27
  7.2 0.3 %fusion.skill_gram_ref = f32[256,256]{1,0:T(8,128)S(1)} fusion(bf16[1024,256]{1,0:T(8,128)(2,1)S(1)} %get-tuple-element.14.skill), kind=kOutput, calls=%fused_computation.12 | convolution fusion | flops 134217728 | bytes 786432 | tf_op jit(solution)/shard_map/dot_general | solution.py:285
  7.5 1.2 %collective-permute-done.1 = f32[24,256]{1,0:T(8,128)S(1)} collective-permute-done((f32[24,256]{1,0:T(8,128)S(1)}, f32[24,256]{1,0:T(8,128)S(1)}, u32[]{:S(2)}, u32[]{:S(2)}) %collective-permute-start.1) | collective-permute-done | bytes 24608 | tf_op jit(solution)/shard_map/ppermute | solution.py:27
  8.7 1.7 %collective-permute-start.2 = (f32[32,256]{1,0:T(8,128)S(1)}, f32[32,256]{1,0:T(8,128)S(1)}, u32[]{:S(2)}, u32[]{:S(2)}) collective-permute-start(f32[32,256]{1,0:T(8,128)S(1)} %pad_maximum_fusion.3), channel_id=1, source_target_pairs={{0,5},{1,2},{2,1},{3,6},{4,7},{5,0},{6,3},{7,4},{8,13},{9,10},{10,... | collective-permute-start | bytes 98312 | tf_op jit(solution)/shard_map/ppermute | solution.py:27
  10.4 1.7 %collective-permute-done.2 = f32[32,256]{1,0:T(8,128)S(1)} collective-permute-done((f32[32,256]{1,0:T(8,128)S(1)}, f32[32,256]{1,0:T(8,128)S(1)}, u32[]{:S(2)}, u32[]{:S(2)}) %collective-permute-start.2) | collective-permute-done | bytes 32800 | tf_op jit(solution)/shard_map/ppermute | solution.py:27
  12.1 1.6 %collective-permute-start.3 = (f32[48,256]{1,0:T(8,128)S(1)}, f32[48,256]{1,0:T(8,128)S(1)}, u32[]{:S(2)}, u32[]{:S(2)}) collective-permute-start(f32[48,256]{1,0:T(8,128)S(1)} %pad_maximum_fusion.1), channel_id=1, source_target_pairs={{0,3},{1,4},{2,7},{3,0},{4,1},{5,6},{6,5},{7,2},{8,11},{9,12},{10,... | collective-permute-start | bytes 147464 | tf_op jit(solution)/shard_map/ppermute | solution.py:27
  13.7 0.4 %collective-permute-start.7 = (f32[32,256]{1,0:T(8,128)S(1)}, f32[32,256]{1,0:T(8,128)S(1)}, u32[]{:S(2)}, u32[]{:S(2)}) collective-permute-start(f32[32,256]{1,0:T(8,128)S(1)} %pad_maximum_fusion.5), channel_id=1, source_target_pairs={{0,1},{1,0},{2,3},{3,2},{4,5},{5,4},{6,7},{7,6},{8,9},{9,8},{10,11... | collective-permute-start | bytes 98312 | tf_op jit(solution)/shard_map/ppermute | solution.py:27
  14.2 1.5 %collective-permute-done.3 = f32[48,256]{1,0:T(8,128)S(1)} collective-permute-done((f32[48,256]{1,0:T(8,128)S(1)}, f32[48,256]{1,0:T(8,128)S(1)}, u32[]{:S(2)}, u32[]{:S(2)}) %collective-permute-start.3) | collective-permute-done | bytes 49184 | tf_op jit(solution)/shard_map/ppermute | solution.py:27
  15.7 1.6 %collective-permute-start.5 = (f32[32,256]{1,0:T(8,128)S(1)}, f32[32,256]{1,0:T(8,128)S(1)}, u32[]{:S(2)}, u32[]{:S(2)}) collective-permute-start(f32[32,256]{1,0:T(8,128)S(1)} %pad_maximum_fusion.4), channel_id=1, source_target_pairs={{0,17},{1,16},{2,19},{3,18},{4,21},{5,20},{6,23},{7,22},{8,25},{9,... | collective-permute-start | bytes 98312 | tf_op jit(solution)/shard_map/ppermute | solution.py:27
  17.4 0.4 %collective-permute-start.4 = (f32[48,256]{1,0:T(8,128)S(1)}, f32[48,256]{1,0:T(8,128)S(1)}, u32[]{:S(2)}, u32[]{:S(2)}) collective-permute-start(f32[48,256]{1,0:T(8,128)S(1)} %pad_maximum_fusion.2.mine_ref), channel_id=1, source_target_pairs={{0,1},{1,0},{2,3},{3,2},{4,5},{5,4},{6,7},{7,6},{8,9},{9,8},{10,11... | collective-permute-start | bytes 147464 | tf_op jit(solution)/shard_map/ppermute | solution.py:27
  17.8 1.3 %collective-permute-done.5.far_ref = f32[32,256]{1,0:T(8,128)S(1)} collective-permute-done((f32[32,256]{1,0:T(8,128)S(1)}, f32[32,256]{1,0:T(8,128)S(1)}, u32[]{:S(2)}, u32[]{:S(2)}) %collective-permute-start.5) | collective-permute-done | bytes 32800 | tf_op jit(solution)/shard_map/ppermute | solution.py:27
  19.1 0.3 %collective-permute-start.6 = (f32[32,256]{1,0:T(8,128)S(1)}, f32[32,256]{1,0:T(8,128)S(1)}, u32[]{:S(2)}, u32[]{:S(2)}) collective-permute-start(f32[32,256]{1,0:T(8,128)S(1)} %collective-permute-done.5.far_ref), channel_id=1, source_target_pairs={{0,1},{1,0},{2,3},{3,2},{4,5},{5,4},{6,7},{7,6},{8,9},{9,8},{10,11... | collective-permute-start | bytes 98312 | tf_op jit(solution)/shard_map/ppermute | solution.py:27
  19.5 0.0 collective-permute-done.7.early_ref
  19.5 0.0 collective-permute-done.4.late_ref.core_ref
  19.5 0.2 %shard_map.70.gram_ref = bf16[256,512]{1,0:T(8,128)(2,1)S(1)} custom-call(f32[64,256]{1,0:T(8,128)S(1)} %pad_maximum_fusion.mine_ref, f32[32,256]{1,0:T(8,128)S(1)} %collective-permute-done.7.early_ref, f32[48,256]{1,0:T(8,128)S(1)} %collective-permute-done.4.late_ref.core_ref, f32[256,256]{1,0:T(8,128)S(1)} %fusion.skill_gram_ref), custom_call_target="tpu_custom_call" | custom-call | flops 16777216 | bytes 524288 | tf_op jit(solution)/shard_map/pallas_call | solution.py:154
  19.7 0.6 %collective-permute-done.6.cross_ref = f32[32,256]{1,0:T(8,128)S(1)} collective-permute-done((f32[32,256]{1,0:T(8,128)S(1)}, f32[32,256]{1,0:T(8,128)S(1)}, u32[]{:S(2)}, u32[]{:S(2)}) %collective-permute-start.6) | collective-permute-done | bytes 32800 | tf_op jit(solution)/shard_map/ppermute | solution.py:27
  20.3 1.8 %shard_map.71 = (f32[16,32]{1,0:T(8,128)}, f32[16,32]{1,0:T(8,128)}) custom-call(f32[1,7]{1,0:T(1,128)S(1)} %get-tuple-element.16.coef_ref, f32[32,256]{1,0:T(8,128)S(1)} %get-tuple-element.17.prev_ref, f32[48,256]{1,0:T(8,128)S(1)} %pad_maximum_fusion.2.mine_ref, f32[48,256]{1,0:T(8,128)S(1)} %collective-permute-done.4.late_ref.core_ref, ...), custom_call_target="tpu_custom_call" | custom-call | flops 100663296 | bytes 393216 | tf_op jit(solution)/shard_map/pallas_call | solution.py:255
  (15 shorter events, 0.1 us)
Async XLA Ops:
  2.1 1.4 %collective-permute-start = (f32[16,256]{1,0:T(8,128)S(1)}, f32[16,256]{1,0:T(8,128)S(1)}, u32[]{:S(2)}, u32[]{:S(2)}) collective-permute-start(f32[16,256]{1,0:T(8,128)S(1)} %get-tuple-element.19), channel_id=1, source_target_pairs={{0,1},{1,0},{2,3},{3,2},{4,5},{5,4},{6,7},{7,6},{8,9},{9,8},{10,11... | collective-permute-start | bytes 49160 | tf_op jit(solution)/shard_map/ppermute | solution.py:27
  3.4 5.3 %collective-permute-start.1 = (f32[24,256]{1,0:T(8,128)S(1)}, f32[24,256]{1,0:T(8,128)S(1)}, u32[]{:S(2)}, u32[]{:S(2)}) collective-permute-start(f32[24,256]{1,0:T(8,128)S(1)} %pad_maximum_fusion.6), channel_id=1, source_target_pairs={{0,9},{1,8},{2,11},{3,10},{4,13},{5,12},{6,15},{7,14},{8,1},{9,0},... | collective-permute-start | bytes 73736 | tf_op jit(solution)/shard_map/ppermute | solution.py:27
  8.7 3.4 %collective-permute-start.2 = (f32[32,256]{1,0:T(8,128)S(1)}, f32[32,256]{1,0:T(8,128)S(1)}, u32[]{:S(2)}, u32[]{:S(2)}) collective-permute-start(f32[32,256]{1,0:T(8,128)S(1)} %pad_maximum_fusion.3), channel_id=1, source_target_pairs={{0,5},{1,2},{2,1},{3,6},{4,7},{5,0},{6,3},{7,4},{8,13},{9,10},{10,... | collective-permute-start | bytes 98312 | tf_op jit(solution)/shard_map/ppermute | solution.py:27
  12.1 3.6 %collective-permute-start.3 = (f32[48,256]{1,0:T(8,128)S(1)}, f32[48,256]{1,0:T(8,128)S(1)}, u32[]{:S(2)}, u32[]{:S(2)}) collective-permute-start(f32[48,256]{1,0:T(8,128)S(1)} %pad_maximum_fusion.1), channel_id=1, source_target_pairs={{0,3},{1,4},{2,7},{3,0},{4,1},{5,6},{6,5},{7,2},{8,11},{9,12},{10,... | collective-permute-start | bytes 147464 | tf_op jit(solution)/shard_map/ppermute | solution.py:27
  13.7 5.8 %collective-permute-start.7 = (f32[32,256]{1,0:T(8,128)S(1)}, f32[32,256]{1,0:T(8,128)S(1)}, u32[]{:S(2)}, u32[]{:S(2)}) collective-permute-start(f32[32,256]{1,0:T(8,128)S(1)} %pad_maximum_fusion.5), channel_id=1, source_target_pairs={{0,1},{1,0},{2,3},{3,2},{4,5},{5,4},{6,7},{7,6},{8,9},{9,8},{10,11... | collective-permute-start | bytes 98312 | tf_op jit(solution)/shard_map/ppermute | solution.py:27
  15.7 3.4 %collective-permute-start.5 = (f32[32,256]{1,0:T(8,128)S(1)}, f32[32,256]{1,0:T(8,128)S(1)}, u32[]{:S(2)}, u32[]{:S(2)}) collective-permute-start(f32[32,256]{1,0:T(8,128)S(1)} %pad_maximum_fusion.4), channel_id=1, source_target_pairs={{0,17},{1,16},{2,19},{3,18},{4,21},{5,20},{6,23},{7,22},{8,25},{9,... | collective-permute-start | bytes 98312 | tf_op jit(solution)/shard_map/ppermute | solution.py:27
  17.4 2.1 %collective-permute-start.4 = (f32[48,256]{1,0:T(8,128)S(1)}, f32[48,256]{1,0:T(8,128)S(1)}, u32[]{:S(2)}, u32[]{:S(2)}) collective-permute-start(f32[48,256]{1,0:T(8,128)S(1)} %pad_maximum_fusion.2.mine_ref), channel_id=1, source_target_pairs={{0,1},{1,0},{2,3},{3,2},{4,5},{5,4},{6,7},{7,6},{8,9},{9,8},{10,11... | collective-permute-start | bytes 147464 | tf_op jit(solution)/shard_map/ppermute | solution.py:27
  19.1 1.2 %collective-permute-start.6 = (f32[32,256]{1,0:T(8,128)S(1)}, f32[32,256]{1,0:T(8,128)S(1)}, u32[]{:S(2)}, u32[]{:S(2)}) collective-permute-start(f32[32,256]{1,0:T(8,128)S(1)} %collective-permute-done.5.far_ref), channel_id=1, source_target_pairs={{0,1},{1,0},{2,3},{3,2},{4,5},{5,4},{6,7},{7,6},{8,9},{9,8},{10,11... | collective-permute-start | bytes 98312 | tf_op jit(solution)/shard_map/ppermute | solution.py:27

commit v11 on v9

--- a/solution.py
+++ b/solution.py
@@ -299,6 +299,7 @@
     far = exchange(jnp.concatenate([mttkrp, factor], 0), last * stu_size + 1)
     core = exchange(mine, 1)
     stack = gram_stack(mine.shape[0] - late.shape[0], students, early, core, skill_gram)
+    far, stack = lax.optimization_barrier((far, stack))
     cross = exchange(far, 1)
     factor, residual = conjugate(coef, day_prev, mine, core, far, cross, stack, rank // stu_size)
     return factor.T, residual.T

time: 22.3 us -> 22.4 us (level)
  transfers between devices with their start and end apart: 8 -> 8, of which waited for: 5 -> 6; matrix products, arithmetic and copies ran while one was open for 2% -> 2% of each run, Pallas kernels for 5% -> 5%
where the time goes in v11:
time: 22.4 us; the launch traced here: 22.2 us
  starting transfers between devices  10.3 us (46%)
  waiting for transfers between devices  6.51 us (29%)
  Pallas kernels  4.23 us (19%)
  between operations  0.71 us (3%)
  matrix products  0.34 us (2%)
    ppermute x8, starting transfers between devices, exchange(): return lax.ppermute(block, ('day', 'stu'), route)  10.3 us
    ppermute x8, waiting for transfers between devices, exchange(): return lax.ppermute(block, ('day', 'stu'), route)  6.51 us
    pallas_call x1, Pallas kernels, conjugate(): pl.pallas_call(functools.partial(cg_kernel, columns), compiler_params=plt...  1.8 us
    pallas_call x1, Pallas kernels, send_part(): pl.pallas_call(send_kernel, compiler_params=pltpu.CompilerParams(vmem_lim...  1.42 us
    pallas_call x1, Pallas kernels, keep_part(): pl.pallas_call(keep_kernel, compiler_params=pltpu.CompilerParams(vmem_lim...  0.78 us
  transfers between devices with their start and end apart: 8, of which 6 were waited for; matrix products, arithmetic and copies ran while one was open for 2% of the time, Pallas kernels for 5%

profile of v11, /device:TPU:0, one launch (start us, length us, event | category | flops | bytes accessed | tf_op | source)
XLA Modules:
  0.0 22.2 jit_solution(17843495887763820300)
XLA Ops:
  0.6 1.4 %shard_map.68 = (f32[16,256]{1,0:T(8,128)S(1)}, bf16[1024,256]{1,0:T(8,128)(2,1)S(1)}, bf16[128,1024]{1,0:T(8,128)(2,1)S(1)}, bf16[8,256]{1,0:T(8,128)(2,1)S(1)}) custom-call(bf16[256,1024]{1,0:T(8,128)(2,1)} %bitcast.6, bf16[1024,256]{1,0:T(8,128)(2,1)} %skill_hbm.1, bf16[8,256]{1,0:T(8,128)(2,1)} %student_hbm.1), custom_call_target="tpu_custom_call" | custom-call | flops 67108864 | bytes 1048576 | tf_op jit(solution)/shard_map/pallas_call | solution.py:82
  2.1 0.5 %collective-permute-start = (f32[16,256]{1,0:T(8,128)S(1)}, f32[16,256]{1,0:T(8,128)S(1)}, u32[]{:S(2)}, u32[]{:S(2)}) collective-permute-start(f32[16,256]{1,0:T(8,128)S(1)} %get-tuple-element.21), channel_id=1, source_target_pairs={{0,1},{1,0},{2,3},{3,2},{4,5},{5,4},{6,7},{7,6},{8,9},{9,8},{10,11... | collective-permute-start | bytes 49160 | tf_op jit(solution)/shard_map/ppermute | solution.py:27
  2.6 0.8 %shard_map.69 = (f32[24,256]{1,0:T(8,128)S(1)}, f32[32,256]{1,0:T(8,128)S(1)}, f32[1,7]{1,0:T(1,128)S(1)}) custom-call(bf16[128,1024]{1,0:T(8,128)(2,1)S(1)} %get-tuple-element.15.perf, bf16[1024,256]{1,0:T(8,128)(2,1)S(1)} %get-tuple-element.16.skill, bf16[8,256]{1,0:T(8,128)(2,1)S(1)} %get-tuple-element.17.student, f32[32,256]{1,0:T(8,128)} %prev_hbm.1, ...), custom_call_target="tpu_custom_call" | custom-call | flops 67108864 | bytes 786432 | tf_op jit(solution)/shard_map/pallas_call | solution.py:122
  3.4 0.0 collective-permute-done
  3.4 3.8 %collective-permute-start.1 = (f32[24,256]{1,0:T(8,128)S(1)}, f32[24,256]{1,0:T(8,128)S(1)}, u32[]{:S(2)}, u32[]{:S(2)}) collective-permute-start(f32[24,256]{1,0:T(8,128)S(1)} %pad_maximum_fusion.6), channel_id=1, source_target_pairs={{0,9},{1,8},{2,11},{3,10},{4,13},{5,12},{6,15},{7,14},{8,1},{9,0},... | collective-permute-start | bytes 73736 | tf_op jit(solution)/shard_map/ppermute | solution.py:27
  7.2 0.3 %fusion.skill_gram_ref = f32[256,256]{1,0:T(8,128)S(1)} fusion(bf16[1024,256]{1,0:T(8,128)(2,1)S(1)} %get-tuple-element.16.skill), kind=kOutput, calls=%fused_computation.12 | convolution fusion | flops 134217728 | bytes 786432 | tf_op jit(solution)/shard_map/dot_general | solution.py:280
  7.5 1.2 %collective-permute-done.1 = f32[24,256]{1,0:T(8,128)S(1)} collective-permute-done((f32[24,256]{1,0:T(8,128)S(1)}, f32[24,256]{1,0:T(8,128)S(1)}, u32[]{:S(2)}, u32[]{:S(2)}) %collective-permute-start.1) | collective-permute-done | bytes 24608 | tf_op jit(solution)/shard_map/ppermute | solution.py:27
  8.7 1.7 %collective-permute-start.2 = (f32[32,256]{1,0:T(8,128)S(1)}, f32[32,256]{1,0:T(8,128)S(1)}, u32[]{:S(2)}, u32[]{:S(2)}) collective-permute-start(f32[32,256]{1,0:T(8,128)S(1)} %pad_maximum_fusion.3), channel_id=1, source_target_pairs={{0,5},{1,2},{2,1},{3,6},{4,7},{5,0},{6,3},{7,4},{8,13},{9,10},{10,... | collective-permute-start | bytes 98312 | tf_op jit(solution)/shard_map/ppermute | solution.py:27
  10.4 1.7 %collective-permute-done.2 = f32[32,256]{1,0:T(8,128)S(1)} collective-permute-done((f32[32,256]{1,0:T(8,128)S(1)}, f32[32,256]{1,0:T(8,128)S(1)}, u32[]{:S(2)}, u32[]{:S(2)}) %collective-permute-start.2) | collective-permute-done | bytes 32800 | tf_op jit(solution)/shard_map/ppermute | solution.py:27
  12.1 1.6 %collective-permute-start.3 = (f32[48,256]{1,0:T(8,128)S(1)}, f32[48,256]{1,0:T(8,128)S(1)}, u32[]{:S(2)}, u32[]{:S(2)}) collective-permute-start(f32[48,256]{1,0:T(8,128)S(1)} %pad_maximum_fusion.1), channel_id=1, source_target_pairs={{0,3},{1,4},{2,7},{3,0},{4,1},{5,6},{6,5},{7,2},{8,11},{9,12},{10,... | collective-permute-start | bytes 147464 | tf_op jit(solution)/shard_map/ppermute | solution.py:27
  13.7 0.4 %collective-permute-start.6 = (f32[32,256]{1,0:T(8,128)S(1)}, f32[32,256]{1,0:T(8,128)S(1)}, u32[]{:S(2)}, u32[]{:S(2)}) collective-permute-start(f32[32,256]{1,0:T(8,128)S(1)} %pad_maximum_fusion.5), channel_id=1, source_target_pairs={{0,1},{1,0},{2,3},{3,2},{4,5},{5,4},{6,7},{7,6},{8,9},{9,8},{10,11... | collective-permute-start | bytes 98312 | tf_op jit(solution)/shard_map/ppermute | solution.py:27
  14.2 1.5 %collective-permute-done.3 = f32[48,256]{1,0:T(8,128)S(1)} collective-permute-done((f32[48,256]{1,0:T(8,128)S(1)}, f32[48,256]{1,0:T(8,128)S(1)}, u32[]{:S(2)}, u32[]{:S(2)}) %collective-permute-start.3) | collective-permute-done | bytes 49184 | tf_op jit(solution)/shard_map/ppermute | solution.py:27
  15.8 1.6 %collective-permute-start.5 = (f32[32,256]{1,0:T(8,128)S(1)}, f32[32,256]{1,0:T(8,128)S(1)}, u32[]{:S(2)}, u32[]{:S(2)}) collective-permute-start(f32[32,256]{1,0:T(8,128)S(1)} %pad_maximum_fusion.4), channel_id=1, source_target_pairs={{0,17},{1,16},{2,19},{3,18},{4,21},{5,20},{6,23},{7,22},{8,25},{9,... | collective-permute-start | bytes 98312 | tf_op jit(solution)/shard_map/ppermute | solution.py:27
  17.4 0.4 %collective-permute-start.4 = (f32[48,256]{1,0:T(8,128)S(1)}, f32[48,256]{1,0:T(8,128)S(1)}, u32[]{:S(2)}, u32[]{:S(2)}) collective-permute-start(f32[48,256]{1,0:T(8,128)S(1)} %pad_maximum_fusion.2.mine_ref), channel_id=1, source_target_pairs={{0,1},{1,0},{2,3},{3,2},{4,5},{5,4},{6,7},{7,6},{8,9},{9,8},{10,11... | collective-permute-start | bytes 147464 | tf_op jit(solution)/shard_map/ppermute | solution.py:27
  17.7 0.0 collective-permute-done.6.early_ref
  17.7 0.9 %collective-permute-done.4.late_ref.core_ref = f32[48,256]{1,0:T(8,128)S(1)} collective-permute-done((f32[48,256]{1,0:T(8,128)S(1)}, f32[48,256]{1,0:T(8,128)S(1)}, u32[]{:S(2)}, u32[]{:S(2)}) %collective-permute-start.4) | collective-permute-done | bytes 49184 | tf_op jit(solution)/shard_map/ppermute | solution.py:27
  18.6 0.2 shard_map.70.gram_ref
  18.8 0.3 %collective-permute-done.5.far_ref = f32[32,256]{1,0:T(8,128)S(1)} collective-permute-done((f32[32,256]{1,0:T(8,128)S(1)}, f32[32,256]{1,0:T(8,128)S(1)}, u32[]{:S(2)}, u32[]{:S(2)}) %collective-permute-start.5) | collective-permute-done | bytes 32800 | tf_op jit(solution)/shard_map/ppermute | solution.py:27
  19.2 0.3 %collective-permute-start.7 = (f32[32,256]{1,0:T(8,128)S(1)}, f32[32,256]{1,0:T(8,128)S(1)}, u32[]{:S(2)}, u32[]{:S(2)}) collective-permute-start(f32[32,256]{1,0:T(8,128)S(1)} %collective-permute-done.5.far_ref), channel_id=1, source_target_pairs={{0,1},{1,0},{2,3},{3,2},{4,5},{5,4},{6,7},{7,6},{8,9},{9,8},{10,11... | collective-permute-start | bytes 98312 | tf_op jit(solution)/shard_map/ppermute | solution.py:27
  19.5 0.9 %collective-permute-done.7.cross_ref = f32[32,256]{1,0:T(8,128)S(1)} collective-permute-done((f32[32,256]{1,0:T(8,128)S(1)}, f32[32,256]{1,0:T(8,128)S(1)}, u32[]{:S(2)}, u32[]{:S(2)}) %collective-permute-start.7) | collective-permute-done | bytes 32800 | tf_op jit(solution)/shard_map/ppermute | solution.py:27
  20.4 1.8 %shard_map.71 = (f32[16,32]{1,0:T(8,128)}, f32[16,32]{1,0:T(8,128)}) custom-call(f32[1,7]{1,0:T(1,128)S(1)} %get-tuple-element.18.coef_ref, f32[32,256]{1,0:T(8,128)S(1)} %get-tuple-element.19.prev_ref, f32[48,256]{1,0:T(8,128)S(1)} %pad_maximum_fusion.2.mine_ref, f32[48,256]{1,0:T(8,128)S(1)} %collective-permute-done.4.late_ref.core_ref, ...), custom_call_target="tpu_custom_call" | custom-call | flops 100663296 | bytes 393216 | tf_op jit(solution)/shard_map/pallas_call | solution.py:248
  (15 shorter events, 0.1 us)
Async XLA Ops:
  2.1 1.4 %collective-permute-start = (f32[16,256]{1,0:T(8,128)S(1)}, f32[16,256]{1,0:T(8,128)S(1)}, u32[]{:S(2)}, u32[]{:S(2)}) collective-permute-start(f32[16,256]{1,0:T(8,128)S(1)} %get-tuple-element.21), channel_id=1, source_target_pairs={{0,1},{1,0},{2,3},{3,2},{4,5},{5,4},{6,7},{7,6},{8,9},{9,8},{10,11... | collective-permute-start | bytes 49160 | tf_op jit(solution)/shard_map/ppermute | solution.py:27
  3.4 5.3 %collective-permute-start.1 = (f32[24,256]{1,0:T(8,128)S(1)}, f32[24,256]{1,0:T(8,128)S(1)}, u32[]{:S(2)}, u32[]{:S(2)}) collective-permute-start(f32[24,256]{1,0:T(8,128)S(1)} %pad_maximum_fusion.6), channel_id=1, source_target_pairs={{0,9},{1,8},{2,11},{3,10},{4,13},{5,12},{6,15},{7,14},{8,1},{9,0},... | collective-permute-start | bytes 73736 | tf_op jit(solution)/shard_map/ppermute | solution.py:27
  8.7 3.4 %collective-permute-start.2 = (f32[32,256]{1,0:T(8,128)S(1)}, f32[32,256]{1,0:T(8,128)S(1)}, u32[]{:S(2)}, u32[]{:S(2)}) collective-permute-start(f32[32,256]{1,0:T(8,128)S(1)} %pad_maximum_fusion.3), channel_id=1, source_target_pairs={{0,5},{1,2},{2,1},{3,6},{4,7},{5,0},{6,3},{7,4},{8,13},{9,10},{10,... | collective-permute-start | bytes 98312 | tf_op jit(solution)/shard_map/ppermute | solution.py:27
  12.1 3.6 %collective-permute-start.3 = (f32[48,256]{1,0:T(8,128)S(1)}, f32[48,256]{1,0:T(8,128)S(1)}, u32[]{:S(2)}, u32[]{:S(2)}) collective-permute-start(f32[48,256]{1,0:T(8,128)S(1)} %pad_maximum_fusion.1), channel_id=1, source_target_pairs={{0,3},{1,4},{2,7},{3,0},{4,1},{5,6},{6,5},{7,2},{8,11},{9,12},{10,... | collective-permute-start | bytes 147464 | tf_op jit(solution)/shard_map/ppermute | solution.py:27
  13.7 4.0 %collective-permute-start.6 = (f32[32,256]{1,0:T(8,128)S(1)}, f32[32,256]{1,0:T(8,128)S(1)}, u32[]{:S(2)}, u32[]{:S(2)}) collective-permute-start(f32[32,256]{1,0:T(8,128)S(1)} %pad_maximum_fusion.5), channel_id=1, source_target_pairs={{0,1},{1,0},{2,3},{3,2},{4,5},{5,4},{6,7},{7,6},{8,9},{9,8},{10,11... | collective-permute-start | bytes 98312 | tf_op jit(solution)/shard_map/ppermute | solution.py:27
  15.8 3.4 %collective-permute-start.5 = (f32[32,256]{1,0:T(8,128)S(1)}, f32[32,256]{1,0:T(8,128)S(1)}, u32[]{:S(2)}, u32[]{:S(2)}) collective-permute-start(f32[32,256]{1,0:T(8,128)S(1)} %pad_maximum_fusion.4), channel_id=1, source_target_pairs={{0,17},{1,16},{2,19},{3,18},{4,21},{5,20},{6,23},{7,22},{8,25},{9,... | collective-permute-start | bytes 98312 | tf_op jit(solution)/shard_map/ppermute | solution.py:27
  17.4 1.2 %collective-permute-start.4 = (f32[48,256]{1,0:T(8,128)S(1)}, f32[48,256]{1,0:T(8,128)S(1)}, u32[]{:S(2)}, u32[]{:S(2)}) collective-permute-start(f32[48,256]{1,0:T(8,128)S(1)} %pad_maximum_fusion.2.mine_ref), channel_id=1, source_target_pairs={{0,1},{1,0},{2,3},{3,2},{4,5},{5,4},{6,7},{7,6},{8,9},{9,8},{10,11... | collective-permute-start | bytes 147464 | tf_op jit(solution)/shard_map/ppermute | solution.py:27
  19.2 1.2 %collective-permute-start.7 = (f32[32,256]{1,0:T(8,128)S(1)}, f32[32,256]{1,0:T(8,128)S(1)}, u32[]{:S(2)}, u32[]{:S(2)}) collective-permute-start(f32[32,256]{1,0:T(8,128)S(1)} %collective-permute-done.5.far_ref), channel_id=1, source_target_pairs={{0,1},{1,0},{2,3},{3,2},{4,5},{5,4},{6,7},{7,6},{8,9},{9,8},{10,11... | collective-permute-start | bytes 98312 | tf_op jit(solution)/shard_map/ppermute | solution.py:27

commit v12 on v9

--- a/solution.py
+++ b/solution.py
@@ -45,7 +45,8 @@
 
 def student_sums(perf, skill, wide, proj, out_ref):
     students = wide.shape[0]
-    total = product(perf[...], skill[...])
+    depth = perf.shape[1] // 2
+    total = product(perf[:, :depth], skill[:depth, :]) + product(perf[:, depth:], skill[depth:, :])
     days = total.shape[0] // students
     for t in range(proj.shape[0]):
         lanes = slice(t * LANES, (t + 1) * LANES)

time: 22.3 us -> 22.4 us (level)
  no operation moved by 1% of the time
where the time goes in v12:
time: 22.4 us; the launch traced here: 22.1 us
  starting transfers between devices  10.4 us (46%)
  waiting for transfers between devices  6.42 us (29%)
  Pallas kernels  4.23 us (19%)
  between operations  0.71 us (3%)
  matrix products  0.34 us (2%)
    ppermute x8, starting transfers between devices, exchange(): return lax.ppermute(block, ('day', 'stu'), route)  10.4 us
    ppermute x8, waiting for transfers between devices, exchange(): return lax.ppermute(block, ('day', 'stu'), route)  6.42 us
    pallas_call x1, Pallas kernels, conjugate(): pl.pallas_call(functools.partial(cg_kernel, columns), compiler_params=plt...  1.8 us
    pallas_call x1, Pallas kernels, send_part(): pl.pallas_call(send_kernel, compiler_params=pltpu.CompilerParams(vmem_lim...  1.42 us
    pallas_call x1, Pallas kernels, keep_part(): pl.pallas_call(keep_kernel, compiler_params=pltpu.CompilerParams(vmem_lim...  0.78 us
  transfers between devices with their start and end apart: 8, of which 5 were waited for; matrix products, arithmetic and copies ran while one was open for 2% of the time, Pallas kernels for 5%

profile of v12, /device:TPU:0, one launch (start us, length us, event | category | flops | bytes accessed | tf_op | source)
XLA Modules:
  0.0 22.1 jit_solution(16663386613352337136)
XLA Ops:
  0.6 1.4 %shard_map.68 = (f32[16,256]{1,0:T(8,128)S(1)}, bf16[1024,256]{1,0:T(8,128)(2,1)S(1)}, bf16[128,1024]{1,0:T(8,128)(2,1)S(1)}, bf16[8,256]{1,0:T(8,128)(2,1)S(1)}) custom-call(bf16[256,1024]{1,0:T(8,128)(2,1)} %bitcast.6, bf16[1024,256]{1,0:T(8,128)(2,1)} %skill_hbm.1, bf16[8,256]{1,0:T(8,128)(2,1)} %student_hbm.1), custom_call_target="tpu_custom_call" | custom-call | flops 67108864 | bytes 1048576 | tf_op jit(solution)/shard_map/pallas_call | solution.py:83
  2.1 0.5 %collective-permute-start = (f32[16,256]{1,0:T(8,128)S(1)}, f32[16,256]{1,0:T(8,128)S(1)}, u32[]{:S(2)}, u32[]{:S(2)}) collective-permute-start(f32[16,256]{1,0:T(8,128)S(1)} %get-tuple-element.19), channel_id=1, source_target_pairs={{0,1},{1,0},{2,3},{3,2},{4,5},{5,4},{6,7},{7,6},{8,9},{9,8},{10,11... | collective-permute-start | bytes 49160 | tf_op jit(solution)/shard_map/ppermute | solution.py:27
  2.6 0.8 %shard_map.69 = (f32[24,256]{1,0:T(8,128)S(1)}, f32[32,256]{1,0:T(8,128)S(1)}, f32[1,7]{1,0:T(1,128)S(1)}) custom-call(bf16[128,1024]{1,0:T(8,128)(2,1)S(1)} %get-tuple-element.13.perf, bf16[1024,256]{1,0:T(8,128)(2,1)S(1)} %get-tuple-element.14.skill, bf16[8,256]{1,0:T(8,128)(2,1)S(1)} %get-tuple-element.15.student, f32[32,256]{1,0:T(8,128)} %prev_hbm.1, ...), custom_call_target="tpu_custom_call" | custom-call | flops 67108864 | bytes 786432 | tf_op jit(solution)/shard_map/pallas_call | solution.py:123
  3.4 0.0 collective-permute-done
  3.4 3.8 %collective-permute-start.1 = (f32[24,256]{1,0:T(8,128)S(1)}, f32[24,256]{1,0:T(8,128)S(1)}, u32[]{:S(2)}, u32[]{:S(2)}) collective-permute-start(f32[24,256]{1,0:T(8,128)S(1)} %pad_maximum_fusion.6), channel_id=1, source_target_pairs={{0,9},{1,8},{2,11},{3,10},{4,13},{5,12},{6,15},{7,14},{8,1},{9,0},... | collective-permute-start | bytes 73736 | tf_op jit(solution)/shard_map/ppermute | solution.py:27
  7.2 0.3 %fusion.skill_gram_ref = f32[256,256]{1,0:T(8,128)S(1)} fusion(bf16[1024,256]{1,0:T(8,128)(2,1)S(1)} %get-tuple-element.14.skill), kind=kOutput, calls=%fused_computation.12 | convolution fusion | flops 134217728 | bytes 786432 | tf_op jit(solution)/shard_map/dot_general | solution.py:281
  7.5 1.2 %collective-permute-done.1 = f32[24,256]{1,0:T(8,128)S(1)} collective-permute-done((f32[24,256]{1,0:T(8,128)S(1)}, f32[24,256]{1,0:T(8,128)S(1)}, u32[]{:S(2)}, u32[]{:S(2)}) %collective-permute-start.1) | collective-permute-done | bytes 24608 | tf_op jit(solution)/shard_map/ppermute | solution.py:27
  8.7 1.7 %collective-permute-start.2 = (f32[32,256]{1,0:T(8,128)S(1)}, f32[32,256]{1,0:T(8,128)S(1)}, u32[]{:S(2)}, u32[]{:S(2)}) collective-permute-start(f32[32,256]{1,0:T(8,128)S(1)} %pad_maximum_fusion.3), channel_id=1, source_target_pairs={{0,5},{1,2},{2,1},{3,6},{4,7},{5,0},{6,3},{7,4},{8,13},{9,10},{10,... | collective-permute-start | bytes 98312 | tf_op jit(solution)/shard_map/ppermute | solution.py:27
  10.4 1.7 %collective-permute-done.2 = f32[32,256]{1,0:T(8,128)S(1)} collective-permute-done((f32[32,256]{1,0:T(8,128)S(1)}, f32[32,256]{1,0:T(8,128)S(1)}, u32[]{:S(2)}, u32[]{:S(2)}) %collective-permute-start.2) | collective-permute-done | bytes 32800 | tf_op jit(solution)/shard_map/ppermute | solution.py:27
  12.1 1.6 %collective-permute-start.3 = (f32[48,256]{1,0:T(8,128)S(1)}, f32[48,256]{1,0:T(8,128)S(1)}, u32[]{:S(2)}, u32[]{:S(2)}) collective-permute-start(f32[48,256]{1,0:T(8,128)S(1)} %pad_maximum_fusion.1), channel_id=1, source_target_pairs={{0,3},{1,4},{2,7},{3,0},{4,1},{5,6},{6,5},{7,2},{8,11},{9,12},{10,... | collective-permute-start | bytes 147464 | tf_op jit(solution)/shard_map/ppermute | solution.py:27
  13.7 0.4 %collective-permute-start.7 = (f32[32,256]{1,0:T(8,128)S(1)}, f32[32,256]{1,0:T(8,128)S(1)}, u32[]{:S(2)}, u32[]{:S(2)}) collective-permute-start(f32[32,256]{1,0:T(8,128)S(1)} %pad_maximum_fusion.5), channel_id=1, source_target_pairs={{0,1},{1,0},{2,3},{3,2},{4,5},{5,4},{6,7},{7,6},{8,9},{9,8},{10,11... | collective-permute-start | bytes 98312 | tf_op jit(solution)/shard_map/ppermute | solution.py:27
  14.2 1.5 %collective-permute-done.3 = f32[48,256]{1,0:T(8,128)S(1)} collective-permute-done((f32[48,256]{1,0:T(8,128)S(1)}, f32[48,256]{1,0:T(8,128)S(1)}, u32[]{:S(2)}, u32[]{:S(2)}) %collective-permute-start.3) | collective-permute-done | bytes 49184 | tf_op jit(solution)/shard_map/ppermute | solution.py:27
  15.7 1.6 %collective-permute-start.5 = (f32[32,256]{1,0:T(8,128)S(1)}, f32[32,256]{1,0:T(8,128)S(1)}, u32[]{:S(2)}, u32[]{:S(2)}) collective-permute-start(f32[32,256]{1,0:T(8,128)S(1)} %pad_maximum_fusion.4), channel_id=1, source_target_pairs={{0,17},{1,16},{2,19},{3,18},{4,21},{5,20},{6,23},{7,22},{8,25},{9,... | collective-permute-start | bytes 98312 | tf_op jit(solution)/shard_map/ppermute | solution.py:27
  17.4 0.4 %collective-permute-start.4 = (f32[48,256]{1,0:T(8,128)S(1)}, f32[48,256]{1,0:T(8,128)S(1)}, u32[]{:S(2)}, u32[]{:S(2)}) collective-permute-start(f32[48,256]{1,0:T(8,128)S(1)} %pad_maximum_fusion.2.mine_ref), channel_id=1, source_target_pairs={{0,1},{1,0},{2,3},{3,2},{4,5},{5,4},{6,7},{7,6},{8,9},{9,8},{10,11... | collective-permute-start | bytes 147464 | tf_op jit(solution)/shard_map/ppermute | solution.py:27
  17.8 1.3 %collective-permute-done.5.far_ref = f32[32,256]{1,0:T(8,128)S(1)} collective-permute-done((f32[32,256]{1,0:T(8,128)S(1)}, f32[32,256]{1,0:T(8,128)S(1)}, u32[]{:S(2)}, u32[]{:S(2)}) %collective-permute-start.5) | collective-permute-done | bytes 32800 | tf_op jit(solution)/shard_map/ppermute | solution.py:27
  19.1 0.3 %collective-permute-start.6 = (f32[32,256]{1,0:T(8,128)S(1)}, f32[32,256]{1,0:T(8,128)S(1)}, u32[]{:S(2)}, u32[]{:S(2)}) collective-permute-start(f32[32,256]{1,0:T(8,128)S(1)} %collective-permute-done.5.far_ref), channel_id=1, source_target_pairs={{0,1},{1,0},{2,3},{3,2},{4,5},{5,4},{6,7},{7,6},{8,9},{9,8},{10,11... | collective-permute-start | bytes 98312 | tf_op jit(solution)/shard_map/ppermute | solution.py:27
  19.5 0.0 collective-permute-done.7.early_ref
  19.5 0.0 collective-permute-done.4.late_ref.core_ref
  19.5 0.2 %shard_map.70.gram_ref = bf16[256,512]{1,0:T(8,128)(2,1)S(1)} custom-call(f32[64,256]{1,0:T(8,128)S(1)} %pad_maximum_fusion.mine_ref, f32[32,256]{1,0:T(8,128)S(1)} %collective-permute-done.7.early_ref, f32[48,256]{1,0:T(8,128)S(1)} %collective-permute-done.4.late_ref.core_ref, f32[256,256]{1,0:T(8,128)S(1)} %fusion.skill_gram_ref), custom_call_target="tpu_custom_call" | custom-call | flops 16777216 | bytes 524288 | tf_op jit(solution)/shard_map/pallas_call | solution.py:155
  19.7 0.6 %collective-permute-done.6.cross_ref = f32[32,256]{1,0:T(8,128)S(1)} collective-permute-done((f32[32,256]{1,0:T(8,128)S(1)}, f32[32,256]{1,0:T(8,128)S(1)}, u32[]{:S(2)}, u32[]{:S(2)}) %collective-permute-start.6) | collective-permute-done | bytes 32800 | tf_op jit(solution)/shard_map/ppermute | solution.py:27
  20.3 1.8 %shard_map.71 = (f32[16,32]{1,0:T(8,128)}, f32[16,32]{1,0:T(8,128)}) custom-call(f32[1,7]{1,0:T(1,128)S(1)} %get-tuple-element.16.coef_ref, f32[32,256]{1,0:T(8,128)S(1)} %get-tuple-element.17.prev_ref, f32[48,256]{1,0:T(8,128)S(1)} %pad_maximum_fusion.2.mine_ref, f32[48,256]{1,0:T(8,128)S(1)} %collective-permute-done.4.late_ref.core_ref, ...), custom_call_target="tpu_custom_call" | custom-call | flops 100663296 | bytes 393216 | tf_op jit(solution)/shard_map/pallas_call | solution.py:249
  (15 shorter events, 0.1 us)
Async XLA Ops:
  2.1 1.4 %collective-permute-start = (f32[16,256]{1,0:T(8,128)S(1)}, f32[16,256]{1,0:T(8,128)S(1)}, u32[]{:S(2)}, u32[]{:S(2)}) collective-permute-start(f32[16,256]{1,0:T(8,128)S(1)} %get-tuple-element.19), channel_id=1, source_target_pairs={{0,1},{1,0},{2,3},{3,2},{4,5},{5,4},{6,7},{7,6},{8,9},{9,8},{10,11... | collective-permute-start | bytes 49160 | tf_op jit(solution)/shard_map/ppermute | solution.py:27
  3.4 5.3 %collective-permute-start.1 = (f32[24,256]{1,0:T(8,128)S(1)}, f32[24,256]{1,0:T(8,128)S(1)}, u32[]{:S(2)}, u32[]{:S(2)}) collective-permute-start(f32[24,256]{1,0:T(8,128)S(1)} %pad_maximum_fusion.6), channel_id=1, source_target_pairs={{0,9},{1,8},{2,11},{3,10},{4,13},{5,12},{6,15},{7,14},{8,1},{9,0},... | collective-permute-start | bytes 73736 | tf_op jit(solution)/shard_map/ppermute | solution.py:27
  8.7 3.4 %collective-permute-start.2 = (f32[32,256]{1,0:T(8,128)S(1)}, f32[32,256]{1,0:T(8,128)S(1)}, u32[]{:S(2)}, u32[]{:S(2)}) collective-permute-start(f32[32,256]{1,0:T(8,128)S(1)} %pad_maximum_fusion.3), channel_id=1, source_target_pairs={{0,5},{1,2},{2,1},{3,6},{4,7},{5,0},{6,3},{7,4},{8,13},{9,10},{10,... | collective-permute-start | bytes 98312 | tf_op jit(solution)/shard_map/ppermute | solution.py:27
  12.1 3.6 %collective-permute-start.3 = (f32[48,256]{1,0:T(8,128)S(1)}, f32[48,256]{1,0:T(8,128)S(1)}, u32[]{:S(2)}, u32[]{:S(2)}) collective-permute-start(f32[48,256]{1,0:T(8,128)S(1)} %pad_maximum_fusion.1), channel_id=1, source_target_pairs={{0,3},{1,4},{2,7},{3,0},{4,1},{5,6},{6,5},{7,2},{8,11},{9,12},{10,... | collective-permute-start | bytes 147464 | tf_op jit(solution)/shard_map/ppermute | solution.py:27
  13.7 5.8 %collective-permute-start.7 = (f32[32,256]{1,0:T(8,128)S(1)}, f32[32,256]{1,0:T(8,128)S(1)}, u32[]{:S(2)}, u32[]{:S(2)}) collective-permute-start(f32[32,256]{1,0:T(8,128)S(1)} %pad_maximum_fusion.5), channel_id=1, source_target_pairs={{0,1},{1,0},{2,3},{3,2},{4,5},{5,4},{6,7},{7,6},{8,9},{9,8},{10,11... | collective-permute-start | bytes 98312 | tf_op jit(solution)/shard_map/ppermute | solution.py:27
  15.7 3.4 %collective-permute-start.5 = (f32[32,256]{1,0:T(8,128)S(1)}, f32[32,256]{1,0:T(8,128)S(1)}, u32[]{:S(2)}, u32[]{:S(2)}) collective-permute-start(f32[32,256]{1,0:T(8,128)S(1)} %pad_maximum_fusion.4), channel_id=1, source_target_pairs={{0,17},{1,16},{2,19},{3,18},{4,21},{5,20},{6,23},{7,22},{8,25},{9,... | collective-permute-start | bytes 98312 | tf_op jit(solution)/shard_map/ppermute | solution.py:27
  17.4 2.1 %collective-permute-start.4 = (f32[48,256]{1,0:T(8,128)S(1)}, f32[48,256]{1,0:T(8,128)S(1)}, u32[]{:S(2)}, u32[]{:S(2)}) collective-permute-start(f32[48,256]{1,0:T(8,128)S(1)} %pad_maximum_fusion.2.mine_ref), channel_id=1, source_target_pairs={{0,1},{1,0},{2,3},{3,2},{4,5},{5,4},{6,7},{7,6},{8,9},{9,8},{10,11... | collective-permute-start | bytes 147464 | tf_op jit(solution)/shard_map/ppermute | solution.py:27
  19.1 1.2 %collective-permute-start.6 = (f32[32,256]{1,0:T(8,128)S(1)}, f32[32,256]{1,0:T(8,128)S(1)}, u32[]{:S(2)}, u32[]{:S(2)}) collective-permute-start(f32[32,256]{1,0:T(8,128)S(1)} %collective-permute-done.5.far_ref), channel_id=1, source_target_pairs={{0,1},{1,0},{2,3},{3,2},{4,5},{5,4},{6,7},{7,6},{8,9},{9,8},{10,11... | collective-permute-start | bytes 98312 | tf_op jit(solution)/shard_map/ppermute | solution.py:27
